TPU v7x, 128 devices: a whole 4x4x4 slice. The times are simulated.
128 devices in a mesh: lon: 16 (over x, z_lo, core), lat: 8 (over y, z_hi).
Axes of the slice: x: 4, y: 4, z: 4 (z_hi: 2, z_lo: 2; z = z_hi * 2 + z_lo), core: 2. Of those that a mesh axis runs over, the one named last changes fastest.
Arguments:
- tracers: float32 [12, 512, 8192], P(None, 'lat', 'lon'), may hold values from -6 to 6
- lon_shift: int32 [2, 12, 512], P(None, None, 'lat'), may hold values from -255 to 255, as said below
- lon_frac: float32 [2, 12, 512], P(None, None, 'lat'), may hold values from 0 to 1
- lat_shift: int32 [2, 12, 512], P(None, None, 'lat'), may hold values from -1 to 1
- lat_frac: float32 [2, 12, 512], P(None, None, 'lat'), may hold values from 0 to 1
- remap_frac: float32 [2, 12, 512], P(None, None, 'lat'), may hold values from 0 to 1
- diffusivity: float32 [12, 512], P(None, 'lat'), may hold values from 0.1 to 3
Outputs:
- advected: float32 [12, 512, 8192], P(None, 'lat', 'lon')
Inputs may be any that keep to these rules, and one draw needn't show every extreme that they name: In latitude row j, with e = |2 * j - 511|, |lon_shift| is at most min(255, 64 * 512 // (513 - e)).
All inputs are finite; a program needn't handle non-finite values.
Results may differ from a plain program's by a relative error of at most 0.00002.
Values sent between devices are 32-bit elements; how exact they have to be, the bound alone decides.
A program may use at most 64 MiB of HBM per device.

v0:
```python
import functools

import jax
import jax.numpy as jnp
from jax import lax
from jax.experimental import pallas as pl
from jax.experimental.pallas import tpu as pltpu
from jax.sharding import PartitionSpec as P

NTR = 8
STEPS = 2


def from_behind(x, axis, by):
    peers = lax.axis_size(axis)
    return lax.ppermute(x, axis, [(i, (i + by) % peers) for i in range(peers)])


def with_halo(block, sides, width, periodic):
    for axis, dim in sides:
        count = lax.axis_size(axis)
        forward = [(i, i + 1) for i in range(count - 1)]
        if periodic:
            forward.append((count - 1, 0))
        backward = [(target, source) for source, target in forward]
        low = lax.ppermute(
            lax.slice_in_dim(block, block.shape[dim] - width, None, axis=dim), axis, forward
        )
        high = lax.ppermute(lax.slice_in_dim(block, 0, width, axis=dim), axis, backward)
        block = jnp.concatenate([low, block, high], axis=dim)
    return block


def cubic_weights(fraction):
    w_zero = -fraction * (fraction - 1.0) * (fraction - 2.0) / 6.0
    w_one = (fraction + 1.0) * (fraction - 1.0) * (fraction - 2.0) / 2.0
    w_two = -(fraction + 1.0) * fraction * (fraction - 2.0) / 2.0
    w_three = (fraction + 1.0) * fraction * (fraction - 1.0) / 6.0
    return (w_zero, w_one, w_two, w_three)


def lat_step(padded, offset, fraction, row_count):
    weights = cubic_weights(fraction)
    summed = None
    for place_index in range(6):
        row_delta = place_index - 2
        coeff = jnp.zeros_like(fraction)
        for tap_index in range(4):
            coeff = coeff + jnp.where(offset == tap_index - 1 - row_delta, weights[tap_index], 0.0)
        addend = coeff[:, :, None] * padded[:, 1 + place_index : 1 + place_index + row_count, :]
        summed = addend if summed is None else summed + addend
    return summed


def lon_step(wrapped, fraction, tracer_count):
    weights = cubic_weights(fraction)
    width_cols = wrapped.shape[2] - 4 * tracer_count
    summed = None
    for tap_index in range(4):
        offset_cols = (1 + tap_index) * tracer_count
        addend = (
            weights[tap_index][:, :, None] * wrapped[:, :, offset_cols : offset_cols + width_cols]
        )
        summed = addend if summed is None else summed + addend
    return summed


def remap(tracer_field, fraction):
    level_above = jnp.concatenate([tracer_field[1:], tracer_field[-1:]], axis=0)
    return (1.0 - fraction)[:, :, None] * tracer_field + fraction[:, :, None] * level_above


def diffuse(tracer_field, kappa):
    levels = tracer_field.shape[0]
    face_kappa = 0.5 * (kappa[:-1] + kappa[1:])
    zero_face = jnp.zeros_like(kappa[:1])
    face_below = jnp.concatenate([zero_face, face_kappa], axis=0)
    face_above = jnp.concatenate([face_kappa, zero_face], axis=0)
    ratio_prev = jnp.zeros_like(kappa[0])
    solved_prev = jnp.zeros_like(tracer_field[0])
    ratios = []
    solveds = []
    for level_index in range(levels):
        below = face_below[level_index]
        above = face_above[level_index]
        pivot_value = 1.0 + below + above + below * ratio_prev
        ratio_now = -above / pivot_value
        solved_now = (tracer_field[level_index] + below[:, None] * solved_prev) / pivot_value[
            :, None
        ]
        ratios.append(ratio_now)
        solveds.append(solved_now)
        ratio_prev = ratio_now
        solved_prev = solved_now
    results = [None] * levels
    results[levels - 1] = solveds[levels - 1]
    for level_index in range(levels - 2, -1, -1):
        results[level_index] = (
            solveds[level_index] - ratios[level_index][:, None] * results[level_index + 1]
        )
    return jnp.stack(results, axis=0)


def bit_mask(amount, position):
    return (amount // 2**position % 2 == 1)[:, :, None]


PAIR = 2


def pair_order(cells):
    cols = jnp.arange(cells * NTR)
    cell, tracer = cols // NTR, cols % NTR
    target = (tracer // PAIR) * cells * PAIR + cell * PAIR + tracer % PAIR
    return target


def exact_permute(block, target, inverse):
    width = block.shape[-1]
    flat = block.reshape(-1, width)
    cols = jnp.arange(width)
    if inverse:
        matrix = cols[:, None] == target[None, :]
    else:
        matrix = cols[None, :] == target[:, None]
    matrix = matrix.astype(jnp.bfloat16)
    rest = flat
    total = None
    for _ in range(3):
        part = lax.reduce_precision(rest, exponent_bits=8, mantissa_bits=7)
        rest = rest - part
        piece = jnp.dot(part.astype(jnp.bfloat16), matrix, preferred_element_type=jnp.float32)
        total = piece if total is None else total + piece
    return total.reshape(block.shape)


def exchange_kernel(src_ref, dst_ref, send_sem, recv_sem, local_sem, *, src_at, dst_at):
    count = lax.axis_size("lon")
    me = lax.axis_index("lon")
    lat = lax.axis_index("lat")
    barrier = pltpu.get_barrier_semaphore()
    for offset in range(1, count):
        peer = lax.rem(me + offset, count)
        pl.semaphore_signal(barrier, 1, device_id=(peer, lat), device_id_type=pl.DeviceIdType.MESH)
    pl.semaphore_wait(barrier, count - 1)
    copies = []
    for offset in range(1, count):
        peer = lax.rem(me + offset, count)
        copy = pltpu.make_async_remote_copy(
            src_ref=src_at(src_ref, peer),
            dst_ref=dst_at(dst_ref, me),
            send_sem=send_sem.at[offset],
            recv_sem=recv_sem.at[offset],
            device_id=(peer, lat),
            device_id_type=pl.DeviceIdType.MESH,
        )
        copy.start()
        copies.append(copy)
    local = pltpu.make_async_copy(src_at(src_ref, me), dst_at(dst_ref, me), local_sem)
    local.start()
    for copy in copies:
        copy.wait_send()
    for copy in copies:
        copy.wait_recv()
    local.wait()


def exchange(block, out_shape, src_at, dst_at, ident):
    count = lax.axis_size("lon")
    return pl.pallas_call(
        functools.partial(exchange_kernel, src_at=src_at, dst_at=dst_at),
        out_shape=jax.ShapeDtypeStruct(out_shape, block.dtype),
        in_specs=[pl.BlockSpec(memory_space=pl.ANY)],
        out_specs=pl.BlockSpec(memory_space=pl.ANY),
        scratch_shapes=[
            pltpu.SemaphoreType.DMA((count,)),
            pltpu.SemaphoreType.DMA((count,)),
            pltpu.SemaphoreType.DMA,
        ],
        compiler_params=pltpu.CompilerParams(collective_id=ident, has_side_effects=True),
    )(block)


def to_columns(block):
    levels, rows, width = block.shape
    cells = width // NTR
    devices = lax.axis_size("lon")
    parts = devices // (NTR // PAIR)
    count = rows // parts
    lane = cells * PAIR
    moved = exact_permute(block, pair_order(cells), False)

    def src_at(ref, peer):
        return ref.at[:, pl.ds((peer % parts) * count, count), pl.ds((peer // parts) * lane, lane)]

    def dst_at(ref, sender):
        return ref.at[:, :, pl.ds(sender * lane, lane)]

    return exchange(moved, (levels, count, devices * lane), src_at, dst_at, 0)


def from_columns(field, rows):
    levels, count, width = field.shape
    devices = lax.axis_size("lon")
    parts = devices // (NTR // PAIR)
    lane = width // devices
    cells = lane // PAIR

    def src_at(ref, peer):
        return ref.at[:, :, pl.ds(peer * lane, lane)]

    def dst_at(ref, sender):
        return ref.at[:, pl.ds((sender % parts) * count, count), pl.ds((sender // parts) * lane, lane)]

    moved = exchange(field, (levels, rows, cells * NTR), src_at, dst_at, 1)
    return exact_permute(moved, pair_order(cells), True)


def lat_halo(field, width):
    lon_n = lax.axis_size("lon")
    lat_n = lax.axis_size("lat")
    parts = lon_n // (NTR // PAIR)
    up = []
    for b in range(lat_n):
        for l in range(lon_n):
            t, h = l // parts, l % parts
            g = b * parts + h
            if g + 1 < lat_n * parts:
                nb, nh = (g + 1) // parts, (g + 1) % parts
                up.append((l * lat_n + b, (t * parts + nh) * lat_n + nb))
    down = [(d, s) for s, d in up]
    rows = field.shape[1]
    below = lax.ppermute(field[:, rows - width :], ("lon", "lat"), up)
    above = lax.ppermute(field[:, :width], ("lon", "lat"), down)
    return jnp.concatenate([below, field, above], axis=1)


def roll_rows(field, amount):
    cells = field.shape[2] // PAIR
    current = field
    for position in range(cells.bit_length() - 1):
        moved = jnp.roll(current, PAIR * 2**position, axis=2)
        current = jnp.where(bit_mask(amount, position), moved, current)
    return current


def lon_cubic(shifted, fraction):
    weights = cubic_weights(fraction)
    taps = [jnp.roll(shifted, PAIR * (1 - p), axis=2) for p in range(4)]
    summed = None
    for p in range(4):
        addend = weights[p][:, :, None] * taps[p]
        summed = addend if summed is None else summed + addend
    return summed


def own_rows(values, count):
    parts = lax.axis_size("lon") // (NTR // PAIR)
    start = (lax.axis_index("lon") % parts) * count
    return lax.dynamic_slice_in_dim(values, start, count, axis=values.ndim - 1)


def per_device(tracers, lon_shift, lon_frac, lat_shift, lat_frac, remap_frac, diffusivity):
    rows = tracers.shape[1]
    field = to_columns(tracers)
    count = field.shape[1]
    width = field.shape[2]
    lon_shift, lon_frac, lat_shift, lat_frac, remap_frac, diffusivity = (
        own_rows(v, count) for v in (lon_shift, lon_frac, lat_shift, lat_frac, remap_frac, diffusivity)
    )
    for time_step in range(STEPS):
        padded = lat_halo(field, 3)
        field = lat_step(padded, lat_shift[time_step], lat_frac[time_step], count)
        amount = jnp.remainder(lon_shift[time_step], width // PAIR)
        field = lon_cubic(roll_rows(field, amount), lon_frac[time_step])
        field = remap(field, remap_frac[time_step])
        field = diffuse(field, diffusivity)
    return from_columns(field, rows)


def solution(mesh):
    in_specs = (
        P(None, "lat", "lon"),
        P(None, None, "lat"),
        P(None, None, "lat"),
        P(None, None, "lat"),
        P(None, None, "lat"),
        P(None, None, "lat"),
        P(None, "lat"),
    )
    out_specs = P(None, "lat", "lon")
    return jax.shard_map(
        per_device, mesh=mesh, in_specs=in_specs, out_specs=out_specs, check_vma=False
    )
```

profile of v0, /device:TPU:101, one launch (start us, length us, event | category | flops | bytes accessed | tf_op | source)
XLA Modules:
  0.0 117.3 jit_solution(5269068112218264409)
XLA Ops:
  0.0 1.8 %reduce-precision_convert_fusion.3 = (bf16[768,512]{1,0:T(8,128)(2,1)S(1)}, bf16[768,512]{1,0:T(8,128)(2,1)S(1)}, bf16[768,512]{1,0:T(8,128)(2,1)S(1)}) fusion(f32[12,64,512]{2,1,0:T(8,128)} %param.7), kind=kLoop, calls=%fused_computation.19 | loop fusion | flops 3145728 | bytes 3932160 | tf_op jit(solution)/shard_map/convert_element_type | solution.py:132
  1.8 0.7 fusion.41
  2.5 0.7 fusion.42
  3.2 0.8 fusion.38
  4.0 1.6 %copy.23 = f32[768,512]{1,0:T(8,128)} copy(f32[768,512]{0,1:T(8,128)S(1)} %fusion.38) | data formatting | bytes 3145728 | tf_op jit(solution)/shard_map/add | solution.py:133
  5.6 29.4 %shard_map.73 = f32[12,16,2048]{2,1,0:T(8,128)} custom-call(f32[12,64,512]{2,1,0:T(8,128)} %bitcast.585), custom_call_target="tpu_custom_call" | custom-call | tf_op jit(solution)/shard_map/pallas_call | solution.py:170
  35.1 1.6 %fusion.248 = (f32[12,3,2048]{2,1,0:T(4,128)S(1)}, f32[12,3,2048]{2,1,0:T(4,128)S(1)}) fusion(f32[12,16,2048]{2,1,0:T(8,128)} %shard_map.73), kind=kLoop, calls=%fused_computation.590 | loop fusion | bytes 1179648 | tf_op jit(solution)/shard_map/slice | solution.py:234
  36.7 1.9 %collective-permute-start = (f32[12,3,2048]{2,1,0:T(4,128)S(1)}, f32[12,3,2048]{2,1,0:T(4,128)S(1)}, u32[]{:S(2)}, u32[]{:S(2)}) collective-permute-start(f32[12,3,2048]{2,1,0:T(4,128)S(1)} %get-tuple-element.67), channel_id=1, source_target_pairs={{0,8},{8,16},{16,24},{24,1},{32,40},{40,48},{48,56},{56,33},{64,72... | collective-permute-start | bytes 884744 | tf_op jit(solution)/shard_map/ppermute | solution.py:233
  38.7 2.6 %collective-permute-start.1 = (f32[12,3,2048]{2,1,0:T(4,128)S(1)}, f32[12,3,2048]{2,1,0:T(4,128)S(1)}, u32[]{:S(2)}, u32[]{:S(2)}) collective-permute-start(f32[12,3,2048]{2,1,0:T(4,128)S(1)} %get-tuple-element.66), channel_id=1, source_target_pairs={{8,0},{16,8},{24,16},{1,24},{40,32},{48,40},{56,48},{33,56},{72,64... | collective-permute-start | bytes 884744 | tf_op jit(solution)/shard_map/ppermute | solution.py:234
  41.4 0.1 constant_dynamic-slice_fusion
  41.7 0.1 constant_dynamic-slice_fusion.1
  42.1 1.3 %collective-permute-done = f32[12,3,2048]{2,1,0:T(4,128)S(1)} collective-permute-done((f32[12,3,2048]{2,1,0:T(4,128)S(1)}, f32[12,3,2048]{2,1,0:T(4,128)S(1)}, u32[]{:S(2)}, u32[]{:S(2)}) %collective-permute-start) | collective-permute-done | bytes 294944 | tf_op jit(solution)/shard_map/ppermute | solution.py:233
  43.4 6.5 %collective-permute-done.1 = f32[12,3,2048]{2,1,0:T(4,128)S(1)} collective-permute-done((f32[12,3,2048]{2,1,0:T(4,128)S(1)}, f32[12,3,2048]{2,1,0:T(4,128)S(1)}, u32[]{:S(2)}, u32[]{:S(2)}) %collective-permute-start.1) | collective-permute-done | bytes 294944 | tf_op jit(solution)/shard_map/ppermute | solution.py:234
  49.9 1.7 %fusion.17 = f32[12,16,2048]{2,1,0:T(8,128)S(1)} fusion(f32[12,3,2048]{2,1,0:T(4,128)S(1)} %collective-permute-done, f32[12,16,2048]{2,1,0:T(8,128)S(1)} %copy-done, f32[12,3,2048]{2,1,0:T(4,128)S(1)} %collective-permute-done.1, f32[12,16]{1,0:T(8,128)S(1)} %get-tuple-element.92, f32[12,16]{1,0:T(8,128)S(1)} %get-tuple-element.91, ...), kind=kLoop, calls=%fused_computation.37 | loop fusion | flops 6291456 | bytes 3740160 | tf_op jit(solution)/shard_map/add | solution.py:51
  51.7 0.5 maximum_select_fusion
  52.3 0.5 maximum_select_fusion.1
  52.9 0.5 maximum_select_fusion.2
  53.5 0.5 maximum_select_fusion.3
  54.1 0.5 maximum_select_fusion.4
  54.7 0.5 maximum_select_fusion.5
  55.2 0.1 slice.556
  55.3 0.2 maximum_select_fusion.6
  55.6 0.1 slice.558
  55.7 0.2 maximum_select_fusion.7
  56.1 0.2 maximum_select_fusion.8
  56.3 0.2 fusion.247
  56.5 0.2 maximum_select_fusion.9
  56.7 0.6 fusion.245
  57.3 0.5 slice.567
  57.9 0.9 fusion.32
  58.9 0.3 fusion.33
  59.2 0.4 subtract_dynamic-update-slice_fusion.1
  60.0 0.1 constant_dynamic-update-slice_fusion.1
  60.2 0.1 fusion.244
  60.4 1.9 %collective-permute-start.2 = (f32[12,3,2048]{2,1,0:T(4,128)S(1)}, f32[12,3,2048]{2,1,0:T(4,128)S(1)}, u32[]{:S(2)}, u32[]{:S(2)}) collective-permute-start(f32[12,3,2048]{2,1,0:T(4,128)S(1)} %get-tuple-element.59), channel_id=1, source_target_pairs={{0,8},{8,16},{16,24},{24,1},{32,40},{40,48},{48,56},{56,33},{64,72... | collective-permute-start | bytes 884744 | tf_op jit(solution)/shard_map/ppermute | solution.py:233
  62.3 2.6 %collective-permute-start.3 = (f32[12,3,2048]{2,1,0:T(4,128)S(1)}, f32[12,3,2048]{2,1,0:T(4,128)S(1)}, u32[]{:S(2)}, u32[]{:S(2)}) collective-permute-start(f32[12,3,2048]{2,1,0:T(4,128)S(1)} %get-tuple-element.58), channel_id=1, source_target_pairs={{8,0},{16,8},{24,16},{1,24},{40,32},{48,40},{56,48},{33,56},{72,64... | collective-permute-start | bytes 884744 | tf_op jit(solution)/shard_map/ppermute | solution.py:234
  65.1 1.9 %collective-permute-done.2 = f32[12,3,2048]{2,1,0:T(4,128)S(1)} collective-permute-done((f32[12,3,2048]{2,1,0:T(4,128)S(1)}, f32[12,3,2048]{2,1,0:T(4,128)S(1)}, u32[]{:S(2)}, u32[]{:S(2)}) %collective-permute-start.2) | collective-permute-done | bytes 294944 | tf_op jit(solution)/shard_map/ppermute | solution.py:233
  67.0 6.5 %collective-permute-done.3 = f32[12,3,2048]{2,1,0:T(4,128)S(1)} collective-permute-done((f32[12,3,2048]{2,1,0:T(4,128)S(1)}, f32[12,3,2048]{2,1,0:T(4,128)S(1)}, u32[]{:S(2)}, u32[]{:S(2)}) %collective-permute-start.3) | collective-permute-done | bytes 294944 | tf_op jit(solution)/shard_map/ppermute | solution.py:234
  73.5 1.8 %fusion.10 = f32[12,16,2048]{2,1,0:T(8,128)S(1)} fusion(f32[12,3,2048]{2,1,0:T(4,128)S(1)} %collective-permute-done.2, f32[12,16,2048]{2,1,0:T(8,128)S(1)} %constant_dynamic-update-slice_fusion, f32[12,3,2048]{2,1,0:T(4,128)S(1)} %collective-permute-done.3, f32[12,16]{1,0:T(8,128)S(1)} %get-tuple-element.82, f32[12,16]{1,0:T(8,128)S(1)} %get-tuple-element.81, ...), kind=kLoop, calls=%fused_computation.30 | loop fusion | flops 6291456 | bytes 3740160 | tf_op jit(solution)/shard_map/add | solution.py:51
  75.4 0.5 maximum_select_fusion.10
  76.0 0.5 maximum_select_fusion.11
  76.6 0.5 maximum_select_fusion.12
  77.2 0.5 maximum_select_fusion.13
  77.8 0.5 maximum_select_fusion.14
  78.4 0.5 maximum_select_fusion.15
  78.9 0.1 slice.615
  79.0 0.2 maximum_select_fusion.16
  79.3 0.1 slice.617
  79.4 0.2 maximum_select_fusion.17
  79.8 0.2 maximum_select_fusion.18
  80.0 0.2 fusion.243
  80.2 0.2 maximum_select_fusion.19
  80.4 0.6 fusion.241
  81.0 0.5 slice.626
  81.5 0.9 fusion.36
  82.6 0.3 fusion.37
  82.9 0.4 subtract_dynamic-update-slice_fusion
  83.7 0.1 constant_dynamic-update-slice_fusion.12
  83.9 1.1 copy-done.1
  85.1 27.4 %shard_map.74 = f32[12,64,512]{2,1,0:T(8,128)} custom-call(f32[12,16,2048]{2,1,0:T(8,128)} %copy-done.1), custom_call_target="tpu_custom_call" | custom-call | tf_op jit(solution)/shard_map/pallas_call | solution.py:170
  112.5 1.8 %fusion.3 = (bf16[768,512]{1,0:T(8,128)(2,1)S(1)}, bf16[768,512]{1,0:T(8,128)(2,1)S(1)}, bf16[768,512]{1,0:T(8,128)(2,1)S(1)}) fusion(f32[12,64,512]{2,1,0:T(8,128)} %shard_map.74), kind=kLoop, calls=%fused_computation.23 | loop fusion | flops 3145728 | bytes 3932160 | tf_op jit(solution)/shard_map/convert_element_type | solution.py:132
  114.2 0.6 fusion.39
  114.9 0.6 fusion.40
  115.5 1.8 %add_add_fusion = f32[768,512]{1,0:T(8,128)} fusion(f32[768,512]{1,0:T(8,128)S(1)} %fusion.40, f32[768,512]{1,0:T(8,128)S(1)} %fusion.39, bf16[768,512]{1,0:T(8,128)(2,1)S(1)} %get-tuple-element.49, s32[512]{0:T(512)S(1)} %fusion.224), kind=kOutput, calls=%fused_computation.92 | convolution fusion | flops 403701760 | bytes 5507072 | tf_op jit(solution)/shard_map/dot_general | solution.py:132
  (76 shorter events, 3.3 us)
Async XLA Ops:
  35.0 6.3 %copy-start.3 = (f32[2,12,64]{2,0,1:T(2,128)S(1)}, f32[2,12,64]{2,0,1:T(2,128)}, u32[]{:S(2)}) copy-start(f32[2,12,64]{2,0,1:T(2,128)} %param.12) | copy-start | bytes 18436
  35.0 6.4 %copy-start.4 = (s32[2,12,64]{2,0,1:T(2,128)S(1)}, s32[2,12,64]{2,0,1:T(2,128)}, u32[]{:S(2)}) copy-start(s32[2,12,64]{2,0,1:T(2,128)} %param.8) | copy-start | bytes 18436
  35.0 6.4 %copy-start.5 = (s32[2,12,64]{2,0,1:T(2,128)S(1)}, s32[2,12,64]{2,0,1:T(2,128)}, u32[]{:S(2)}) copy-start(s32[2,12,64]{2,0,1:T(2,128)} %param.10) | copy-start | bytes 18436
  35.0 6.6 %copy-start.6 = (f32[2,12,64]{2,0,1:T(2,128)S(1)}, f32[2,12,64]{2,0,1:T(2,128)}, u32[]{:S(2)}) copy-start(f32[2,12,64]{2,0,1:T(2,128)} %param.11) | copy-start | bytes 18436
  35.1 6.6 %copy-start.7 = (f32[2,12,64]{2,0,1:T(2,128)S(1)}, f32[2,12,64]{2,0,1:T(2,128)}, u32[]{:S(2)}) copy-start(f32[2,12,64]{2,0,1:T(2,128)} %param.9) | copy-start | bytes 18436
  35.1 6.7 %copy-start.2 = (f32[12,64]{1,0:T(8,128)S(1)}, f32[12,64]{1,0:T(8,128)}, u32[]{:S(2)}) copy-start(f32[12,64]{1,0:T(8,128)} %param.13) | copy-start | bytes 9220
  35.1 14.8 %copy-start = (f32[12,16,2048]{2,1,0:T(8,128)S(1)}, f32[12,16,2048]{2,1,0:T(8,128)}, u32[]{:S(2)}) copy-start(f32[12,16,2048]{2,1,0:T(8,128)} %shard_map.73) | copy-start | bytes 4718596
  36.7 6.6 %collective-permute-start = (f32[12,3,2048]{2,1,0:T(4,128)S(1)}, f32[12,3,2048]{2,1,0:T(4,128)S(1)}, u32[]{:S(2)}, u32[]{:S(2)}) collective-permute-start(f32[12,3,2048]{2,1,0:T(4,128)S(1)} %get-tuple-element.67), channel_id=1, source_target_pairs={{0,8},{8,16},{16,24},{24,1},{32,40},{40,48},{48,56},{56,33},{64,72... | collective-permute-start | bytes 884744 | tf_op jit(solution)/shard_map/ppermute | solution.py:233
  38.7 11.2 %collective-permute-start.1 = (f32[12,3,2048]{2,1,0:T(4,128)S(1)}, f32[12,3,2048]{2,1,0:T(4,128)S(1)}, u32[]{:S(2)}, u32[]{:S(2)}) collective-permute-start(f32[12,3,2048]{2,1,0:T(4,128)S(1)} %get-tuple-element.66), channel_id=1, source_target_pairs={{8,0},{16,8},{24,16},{1,24},{40,32},{48,40},{56,48},{33,56},{72,64... | collective-permute-start | bytes 884744 | tf_op jit(solution)/shard_map/ppermute | solution.py:234
  60.4 6.6 %collective-permute-start.2 = (f32[12,3,2048]{2,1,0:T(4,128)S(1)}, f32[12,3,2048]{2,1,0:T(4,128)S(1)}, u32[]{:S(2)}, u32[]{:S(2)}) collective-permute-start(f32[12,3,2048]{2,1,0:T(4,128)S(1)} %get-tuple-element.59), channel_id=1, source_target_pairs={{0,8},{8,16},{16,24},{24,1},{32,40},{40,48},{48,56},{56,33},{64,72... | collective-permute-start | bytes 884744 | tf_op jit(solution)/shard_map/ppermute | solution.py:233
  62.3 11.2 %collective-permute-start.3 = (f32[12,3,2048]{2,1,0:T(4,128)S(1)}, f32[12,3,2048]{2,1,0:T(4,128)S(1)}, u32[]{:S(2)}, u32[]{:S(2)}) collective-permute-start(f32[12,3,2048]{2,1,0:T(4,128)S(1)} %get-tuple-element.58), channel_id=1, source_target_pairs={{8,0},{16,8},{24,16},{1,24},{40,32},{48,40},{56,48},{33,56},{72,64... | collective-permute-start | bytes 884744 | tf_op jit(solution)/shard_map/ppermute | solution.py:234
  83.9 1.1 copy-start.1
where the time goes:
time: 118 us; the launch traced here: 117 us
  Pallas kernels  56.8 us (48%)
  other arithmetic  19.4 us (16%)
  waiting for transfers between devices  16.3 us (14%)
  local copies, waits for them, and re-layouts  9.61 us (8%)
  starting transfers between devices  9.05 us (8%)
  matrix products  5.21 us (4%)
    pallas_call x2, Pallas kernels, exchange(): pl.pallas_call(functools.partial(exchange_kernel, src_at=src_at, dst_at=d...  56.8 us
    ppermute x2, waiting for transfers between devices, lat_halo(): above = lax.ppermute(field[:, :width], ('lon', 'lat'), down)  13 us
    select_n x20, other arithmetic, roll_rows(): current = jnp.where(bit_mask(amount, position), moved, current)  7.75 us
    ppermute x2, starting transfers between devices, lat_halo(): above = lax.ppermute(field[:, :width], ('lon', 'lat'), down)  5.21 us
    dot_general x6, matrix products, exact_permute(): jnp.dot(part.astype(jnp.bfloat16), matrix, preferred_element_type=jnp.flo...  5.21 us
    ppermute x2, starting transfers between devices, lat_halo(): below = lax.ppermute(field[:, rows - width:], ('lon', 'lat'), up)  3.84 us
    convert_element_type x2, other arithmetic, exact_permute(): part.astype(jnp.bfloat16)  3.55 us
    add x2, other arithmetic, lat_step(): summed = addend if summed is None else summed + addend  3.53 us
  transfers between devices with their start and end apart: 4, of which 4 were waited for; matrix products, arithmetic and copies ran while one was open for 1% of the time, Pallas kernels for 0%

commit v1 on v0

--- a/solution.py
+++ b/solution.py
@@ -235,23 +235,96 @@
     return jnp.concatenate([below, field, above], axis=1)
 
 
-def roll_rows(field, amount):
-    cells = field.shape[2] // PAIR
-    current = field
-    for position in range(cells.bit_length() - 1):
-        moved = jnp.roll(current, PAIR * 2**position, axis=2)
-        current = jnp.where(bit_mask(amount, position), moved, current)
-    return current
-
-
-def lon_cubic(shifted, fraction):
+def step_kernel(pad_ref, latc_ref, lonw_ref, bits_ref, keep_ref, take_ref, below_ref, pivot_ref, ratio_ref, out_ref, moved_ref):
+    levels, rows, width = out_ref.shape
+    stages = bits_ref.shape[0]
+
+    def move_level(k, carry):
+        summed = None
+        for place in range(latc_ref.shape[0]):
+            addend = latc_ref[place, k] * pad_ref[k, pl.ds(1 + place, rows), :]
+            summed = addend if summed is None else summed + addend
+        current = summed
+        for position in range(stages):
+            rolled = pltpu.roll(current, PAIR * 2**position, 1)
+            current = jnp.where(bits_ref[position, k] != 0, rolled, current)
+        summed = None
+        for tap in range(4):
+            shift = (PAIR * (1 - tap)) % width
+            moved = pltpu.roll(current, shift, 1) if shift else current
+            addend = lonw_ref[tap, k] * moved
+            summed = addend if summed is None else summed + addend
+        moved_ref[k] = summed
+        return carry
+
+    lax.fori_loop(0, levels, move_level, 0)
+
+    def sweep_down(k, solved_prev):
+        above = moved_ref[jnp.minimum(k + 1, levels - 1)]
+        remapped = keep_ref[k] * moved_ref[k] + take_ref[k] * above
+        solved = (remapped + below_ref[k] * solved_prev) / pivot_ref[k]
+        moved_ref[k] = solved
+        return solved
+
+    last = lax.fori_loop(0, levels, sweep_down, jnp.zeros((rows, width), jnp.float32))
+    out_ref[levels - 1] = last
+
+    def sweep_up(i, result):
+        k = levels - 2 - i
+        result = moved_ref[k] - ratio_ref[k] * result
+        out_ref[k] = result
+        return result
+
+    lax.fori_loop(0, levels - 1, sweep_up, last)
+
+
+def lat_coefficients(offset, fraction):
     weights = cubic_weights(fraction)
-    taps = [jnp.roll(shifted, PAIR * (1 - p), axis=2) for p in range(4)]
-    summed = None
-    for p in range(4):
-        addend = weights[p][:, :, None] * taps[p]
-        summed = addend if summed is None else summed + addend
-    return summed
+    coeffs = []
+    for place_index in range(6):
+        row_delta = place_index - 2
+        coeff = jnp.zeros_like(fraction)
+        for tap_index in range(4):
+            coeff = coeff + jnp.where(offset == tap_index - 1 - row_delta, weights[tap_index], 0.0)
+        coeffs.append(coeff)
+    return jnp.stack(coeffs)[..., None]
+
+
+def diffusion_coefficients(kappa):
+    levels = kappa.shape[0]
+    face_kappa = 0.5 * (kappa[:-1] + kappa[1:])
+    zero_face = jnp.zeros_like(kappa[:1])
+    face_below = jnp.concatenate([zero_face, face_kappa], axis=0)
+    face_above = jnp.concatenate([face_kappa, zero_face], axis=0)
+    ratio_prev = jnp.zeros_like(kappa[0])
+    pivots = []
+    ratios = []
+    for level_index in range(levels):
+        below = face_below[level_index]
+        above = face_above[level_index]
+        pivot_value = 1.0 + below + above + below * ratio_prev
+        ratio_now = -above / pivot_value
+        pivots.append(pivot_value)
+        ratios.append(ratio_now)
+        ratio_prev = ratio_now
+    return face_below[..., None], jnp.stack(pivots)[..., None], jnp.stack(ratios)[..., None]
+
+
+def transport_step(padded, latc, lonw, bits, keep, take, below, pivot, ratio):
+    levels = padded.shape[0]
+    rows = padded.shape[1] - 6
+    width = padded.shape[2]
+    shape = (levels, rows, width)
+    vmem = pl.BlockSpec(memory_space=pltpu.VMEM)
+    size = levels * rows * width
+    return pl.pallas_call(
+        step_kernel,
+        out_shape=jax.ShapeDtypeStruct(shape, jnp.float32),
+        in_specs=[vmem] * 9,
+        out_specs=vmem,
+        scratch_shapes=[pltpu.VMEM(shape, jnp.float32)],
+        cost_estimate=pl.CostEstimate(flops=60 * size, bytes_accessed=12 * size, transcendentals=0),
+    )(padded, latc, lonw, bits, keep, take, below, pivot, ratio)
 
 
 def own_rows(values, count):
@@ -264,17 +337,21 @@
     rows = tracers.shape[1]
     field = to_columns(tracers)
     count = field.shape[1]
-    width = field.shape[2]
+    cells = field.shape[2] // PAIR
     lon_shift, lon_frac, lat_shift, lat_frac, remap_frac, diffusivity = (
         own_rows(v, count) for v in (lon_shift, lon_frac, lat_shift, lat_frac, remap_frac, diffusivity)
     )
+    below, pivot, ratio = diffusion_coefficients(diffusivity)
+    stages = cells.bit_length() - 1
     for time_step in range(STEPS):
         padded = lat_halo(field, 3)
-        field = lat_step(padded, lat_shift[time_step], lat_frac[time_step], count)
-        amount = jnp.remainder(lon_shift[time_step], width // PAIR)
-        field = lon_cubic(roll_rows(field, amount), lon_frac[time_step])
-        field = remap(field, remap_frac[time_step])
-        field = diffuse(field, diffusivity)
+        latc = lat_coefficients(lat_shift[time_step], lat_frac[time_step])
+        lonw = jnp.stack(cubic_weights(lon_frac[time_step]))[..., None]
+        amount = jnp.remainder(lon_shift[time_step], cells)
+        bits = jnp.stack([(amount // 2**position % 2).astype(jnp.int32) for position in range(stages)])[..., None]
+        take = remap_frac[time_step][..., None]
+        keep = (1.0 - remap_frac[time_step])[..., None]
+        field = transport_step(padded, latc, lonw, bits, keep, take, below, pivot, ratio)
     return from_columns(field, rows)
 
 

time: 118 us -> 142 us (1.20)
  the two profiles are of different devices: /device:TPU:101 before, /device:TPU:61 now
where the time goes in v1:
time: 142 us
  Pallas kernels  98.2 us (69%)
  local copies, waits for them, and re-layouts  16.2 us (11%)
  starting transfers between devices  11.1 us (8%)
  other arithmetic  9.35 us (7%)
  matrix products  5.21 us (4%)
    pallas_call x2, Pallas kernels, exchange(): pl.pallas_call(functools.partial(exchange_kernel, src_at=src_at, dst_at=d...  65.5 us
    pallas_call x2, Pallas kernels, transport_step(): pl.pallas_call(step_kernel, out_shape=jax.ShapeDtypeStruct(shape, jnp.flo...  32.7 us
    ppermute x2, starting transfers between devices, lat_halo(): below = lax.ppermute(field[:, rows - width:], ('lon', 'lat'), up)  7.28 us
    dot_general x6, matrix products, exact_permute(): jnp.dot(part.astype(jnp.bfloat16), matrix, preferred_element_type=jnp.flo...  5.21 us
    ppermute x2, starting transfers between devices, lat_halo(): above = lax.ppermute(field[:, :width], ('lon', 'lat'), down)  3.84 us
    concatenate x2, other arithmetic, lat_halo(): return jnp.concatenate([below, field, above], axis=1)  3.65 us
    convert_element_type x2, other arithmetic, exact_permute(): part.astype(jnp.bfloat16)  3.55 us
    broadcast_in_dim x2, local copies, waits for them, and re-layouts, per_device(): jnp.stack([(amount // 2 ** position % 2).astype(jnp.int32) for position i...  3.47 us
  transfers between devices with their start and end apart: 4, of which 2 were waited for; matrix products, arithmetic and copies ran while one was open for 10% of the time, Pallas kernels for 0%

profile of v1, /device:TPU:61, one launch (start us, length us, event | category | flops | bytes accessed | tf_op | source)
XLA Modules:
  0.0 141.6 jit_solution(8169082985001731996)
XLA Ops:
  0.0 1.8 %reduce-precision_convert_fusion.3 = (bf16[768,512]{1,0:T(8,128)(2,1)S(1)}, bf16[768,512]{1,0:T(8,128)(2,1)S(1)}, bf16[768,512]{1,0:T(8,128)(2,1)S(1)}) fusion(f32[12,64,512]{2,1,0:T(8,128)} %param.7), kind=kLoop, calls=%fused_computation.9 | loop fusion | flops 3145728 | bytes 3932160 | tf_op jit(solution)/shard_map/convert_element_type | solution.py:132
  1.8 0.7 fusion.7
  2.5 0.7 fusion.8
  3.2 0.8 fusion.4
  4.0 1.6 %copy.163 = f32[768,512]{1,0:T(8,128)} copy(f32[768,512]{0,1:T(8,128)S(1)} %fusion.4) | data formatting | bytes 3145728 | tf_op jit(solution)/shard_map/add | solution.py:133
  5.6 29.4 %shard_map.73 = f32[12,16,2048]{2,1,0:T(8,128)} custom-call(f32[12,64,512]{2,1,0:T(8,128)} %bitcast.42), custom_call_target="tpu_custom_call" | custom-call | tf_op jit(solution)/shard_map/pallas_call | solution.py:170
  35.0 0.0 copy-start.5
  35.0 0.0 copy-start.6
  35.0 0.0 copy-start.7
  35.0 0.0 copy-start.8
  35.1 0.0 copy-start.9
  35.1 1.5 %fusion.126 = (f32[12,3,2048]{2,1,0:T(4,128)S(1)}, f32[12,3,2048]{2,1,0:T(4,128)S(1)}) fusion(f32[12,16,2048]{2,1,0:T(8,128)} %shard_map.73), kind=kLoop, calls=%fused_computation.385 | loop fusion | bytes 1179648 | tf_op jit(solution)/shard_map/slice | solution.py:233
  36.6 0.0 copy-start.4
  36.6 1.9 %collective-permute-start.1 = (f32[12,3,2048]{2,1,0:T(4,128)S(1)}, f32[12,3,2048]{2,1,0:T(4,128)S(1)}, u32[]{:S(2)}, u32[]{:S(2)}) collective-permute-start(f32[12,3,2048]{2,1,0:T(4,128)S(1)} %get-tuple-element.34), channel_id=1, source_target_pairs={{8,0},{16,8},{24,16},{1,24},{40,32},{48,40},{56,48},{33,56},{72,64... | collective-permute-start | bytes 884744 | tf_op jit(solution)/shard_map/ppermute | solution.py:234
  38.6 3.6 %collective-permute-start = (f32[12,3,2048]{2,1,0:T(4,128)S(1)}, f32[12,3,2048]{2,1,0:T(4,128)S(1)}, u32[]{:S(2)}, u32[]{:S(2)}) collective-permute-start(f32[12,3,2048]{2,1,0:T(4,128)S(1)} %get-tuple-element.33), channel_id=1, source_target_pairs={{0,8},{8,16},{16,24},{24,1},{32,40},{40,48},{48,56},{56,33},{64,72... | collective-permute-start | bytes 884744 | tf_op jit(solution)/shard_map/ppermute | solution.py:233
  42.2 0.0 copy-done.5
  42.2 0.1 constant_dynamic-slice_fusion.6
  42.3 0.0 copy-done.6
  42.3 0.0 copy-done.7
  42.4 0.1 constant_dynamic-slice_fusion.4
  42.6 1.3 copy.171.latc_ref
  43.9 0.0 copy-done.8
  43.9 0.0 copy-done.9
  43.9 0.1 dynamic-slice_bitcast_fusion
  44.1 0.0 copy-start
  44.1 1.1 copy.172.lonw_ref
  45.5 1.7 %copy.173.bits_ref = s32[10,12,16,1]{3,2,1,0:T(8,128)} copy(s32[10,12,16,1]{2,1,0,3:T(8,128)S(1)} %bitcast.43) | data formatting | bytes 15360 | tf_op jit(solution)/shard_map/broadcast_in_dim | solution.py:351
  47.2 0.1 copy.170.take_ref
  47.4 0.0 copy-done.4
  47.4 0.0 copy-start.2
  47.4 0.1 fusion.93
  47.4 0.1 broadcast_divide_fusion
  48.0 0.8 copy.175.below_ref
  48.8 0.8 copy.176.pivot_ref
  49.6 0.8 copy.177.ratio_ref
  50.4 1.3 copy.181.latc_ref
  51.7 0.6 broadcast_subtract_fusion.1.keep_ref
  52.4 0.0 collective-permute-done.1
  52.4 0.0 collective-permute-done
  52.4 0.0 copy-done
  52.4 1.8 %pad_maximum_fusion.pad_ref = f32[12,22,2048]{2,1,0:T(8,128)} fusion(f32[12,3,2048]{2,1,0:T(4,128)S(1)} %collective-permute-done.1, f32[12,16,2048]{2,1,0:T(8,128)S(1)} %copy-done, f32[12,3,2048]{2,1,0:T(4,128)S(1)} %collective-permute-done), kind=kLoop, calls=%fused_computation | loop fusion | flops 1081344 | bytes 4325376 | tf_op jit(solution)/shard_map/concatenate | solution.py:235
  54.2 0.0 copy-done.2
  54.2 16.4 %shard_map.74 = f32[12,16,2048]{2,1,0:T(8,128)} custom-call(f32[12,22,2048]{2,1,0:T(8,128)} %pad_maximum_fusion.pad_ref, f32[6,12,16,1]{3,2,1,0:T(8,128)} %copy.171.latc_ref, f32[4,12,16,1]{3,2,1,0:T(8,128)} %copy.172.lonw_ref, s32[10,12,16,1]{3,2,1,0:T(8,128)} %copy.173.bits_ref, f32[12,16,1]{2,1,0:T(8,128)} %broadcast_subtract_fusion.1.keep_ref, ...), custom_call_target="tpu_custom_call" | custom-call | flops 23592960 | bytes 4718592 | tf_op jit(solution)/shard_map/pallas_call | solution.py:320
  70.6 0.0 copy-start.1
  70.6 1.6 %fusion.125 = (f32[12,3,2048]{2,1,0:T(4,128)S(1)}, f32[12,3,2048]{2,1,0:T(4,128)S(1)}) fusion(f32[12,16,2048]{2,1,0:T(8,128)} %shard_map.74), kind=kLoop, calls=%fused_computation.384 | loop fusion | bytes 1179648 | tf_op jit(solution)/shard_map/slice | solution.py:233
  72.2 1.9 %collective-permute-start.3 = (f32[12,3,2048]{2,1,0:T(4,128)S(1)}, f32[12,3,2048]{2,1,0:T(4,128)S(1)}, u32[]{:S(2)}, u32[]{:S(2)}) collective-permute-start(f32[12,3,2048]{2,1,0:T(4,128)S(1)} %get-tuple-element.32), channel_id=1, source_target_pairs={{8,0},{16,8},{24,16},{1,24},{40,32},{48,40},{56,48},{33,56},{72,64... | collective-permute-start | bytes 884744 | tf_op jit(solution)/shard_map/ppermute | solution.py:234
  74.2 3.6 %collective-permute-start.2 = (f32[12,3,2048]{2,1,0:T(4,128)S(1)}, f32[12,3,2048]{2,1,0:T(4,128)S(1)}, u32[]{:S(2)}, u32[]{:S(2)}) collective-permute-start(f32[12,3,2048]{2,1,0:T(4,128)S(1)} %get-tuple-element.31), channel_id=1, source_target_pairs={{0,8},{8,16},{16,24},{24,1},{32,40},{40,48},{48,56},{56,33},{64,72... | collective-permute-start | bytes 884744 | tf_op jit(solution)/shard_map/ppermute | solution.py:233
  77.8 1.1 copy.182.lonw_ref
  78.9 1.7 %copy.183.bits_ref = s32[10,12,16,1]{3,2,1,0:T(8,128)} copy(s32[10,12,16,1]{2,1,0,3:T(8,128)S(1)} %bitcast.44) | data formatting | bytes 15360 | tf_op jit(solution)/shard_map/broadcast_in_dim | solution.py:351
  80.7 0.1 copy.180.take_ref
  80.8 0.0 copy-start.3
  80.8 0.7 broadcast_subtract_fusion.keep_ref
  81.5 0.1 collective-permute-done.3
  81.6 0.9 collective-permute-done.2
  82.5 0.0 copy-done.1
  82.5 1.8 %pad_maximum_fusion.1.pad_ref = f32[12,22,2048]{2,1,0:T(8,128)} fusion(f32[12,3,2048]{2,1,0:T(4,128)S(1)} %collective-permute-done.3, f32[12,16,2048]{2,1,0:T(8,128)S(1)} %copy-done.1, f32[12,3,2048]{2,1,0:T(4,128)S(1)} %collective-permute-done.2), kind=kLoop, calls=%fused_computation.1 | loop fusion | flops 1081344 | bytes 4325376 | tf_op jit(solution)/shard_map/concatenate | solution.py:235
  84.3 0.0 copy-done.3
  84.3 16.4 %shard_map.75.src_ref = f32[12,16,2048]{2,1,0:T(8,128)} custom-call(f32[12,22,2048]{2,1,0:T(8,128)} %pad_maximum_fusion.1.pad_ref, f32[6,12,16,1]{3,2,1,0:T(8,128)} %copy.181.latc_ref, f32[4,12,16,1]{3,2,1,0:T(8,128)} %copy.182.lonw_ref, s32[10,12,16,1]{3,2,1,0:T(8,128)} %copy.183.bits_ref, f32[12,16,1]{2,1,0:T(8,128)} %broadcast_subtract_fusion.keep_ref, ...), custom_call_target="tpu_custom_call" | custom-call | flops 23592960 | bytes 4718592 | tf_op jit(solution)/shard_map/pallas_call | solution.py:320
  100.7 36.1 %shard_map.76 = f32[12,64,512]{2,1,0:T(8,128)} custom-call(f32[12,16,2048]{2,1,0:T(8,128)} %shard_map.75.src_ref), custom_call_target="tpu_custom_call" | custom-call | tf_op jit(solution)/shard_map/pallas_call | solution.py:170
  136.8 1.8 %reduce-precision_convert_fusion.1 = (bf16[768,512]{1,0:T(8,128)(2,1)S(1)}, bf16[768,512]{1,0:T(8,128)(2,1)S(1)}, bf16[768,512]{1,0:T(8,128)(2,1)S(1)}) fusion(f32[12,64,512]{2,1,0:T(8,128)} %shard_map.76), kind=kLoop, calls=%fused_computation.5 | loop fusion | flops 3145728 | bytes 3932160 | tf_op jit(solution)/shard_map/convert_element_type | solution.py:132
  138.6 0.6 fusion.5
  139.2 0.6 fusion.6
  139.9 1.8 %add_add_fusion = f32[768,512]{1,0:T(8,128)} fusion(f32[768,512]{1,0:T(8,128)S(1)} %fusion.5, f32[768,512]{1,0:T(8,128)S(1)} %fusion.6, bf16[768,512]{1,0:T(8,128)(2,1)S(1)} %get-tuple-element.28, s32[512]{0:T(512)S(1)} %fusion.118), kind=kOutput, calls=%fused_computation.16 | convolution fusion | flops 403701760 | bytes 5507072 | tf_op jit(solution)/shard_map/dot_general | solution.py:132
  (40 shorter events, 0.8 us)
Async XLA Ops:
  35.0 7.2 %copy-start.5 = (f32[2,12,64]{2,0,1:T(2,128)S(1)}, f32[2,12,64]{2,0,1:T(2,128)}, u32[]{:S(2)}) copy-start(f32[2,12,64]{2,0,1:T(2,128)} %param.11) | copy-start | bytes 18436
  35.0 7.3 %copy-start.6 = (s32[2,12,64]{2,0,1:T(2,128)S(1)}, s32[2,12,64]{2,0,1:T(2,128)}, u32[]{:S(2)}) copy-start(s32[2,12,64]{2,0,1:T(2,128)} %param.8) | copy-start | bytes 18436
  35.0 7.3 %copy-start.7 = (s32[2,12,64]{2,0,1:T(2,128)S(1)}, s32[2,12,64]{2,0,1:T(2,128)}, u32[]{:S(2)}) copy-start(s32[2,12,64]{2,0,1:T(2,128)} %param.10) | copy-start | bytes 18436
  35.0 8.9 %copy-start.8 = (f32[2,12,64]{2,0,1:T(2,128)S(1)}, f32[2,12,64]{2,0,1:T(2,128)}, u32[]{:S(2)}) copy-start(f32[2,12,64]{2,0,1:T(2,128)} %param.12) | copy-start | bytes 18436
  35.1 8.9 %copy-start.9 = (f32[2,12,64]{2,0,1:T(2,128)S(1)}, f32[2,12,64]{2,0,1:T(2,128)}, u32[]{:S(2)}) copy-start(f32[2,12,64]{2,0,1:T(2,128)} %param.9) | copy-start | bytes 18436
  36.6 10.7 %copy-start.4 = (f32[12,64]{1,0:T(8,128)S(1)}, f32[12,64]{1,0:T(8,128)}, u32[]{:S(2)}) copy-start(f32[12,64]{1,0:T(8,128)} %param.13) | copy-start | bytes 9220
  36.6 15.8 %collective-permute-start.1 = (f32[12,3,2048]{2,1,0:T(4,128)S(1)}, f32[12,3,2048]{2,1,0:T(4,128)S(1)}, u32[]{:S(2)}, u32[]{:S(2)}) collective-permute-start(f32[12,3,2048]{2,1,0:T(4,128)S(1)} %get-tuple-element.34), channel_id=1, source_target_pairs={{8,0},{16,8},{24,16},{1,24},{40,32},{48,40},{56,48},{33,56},{72,64... | collective-permute-start | bytes 884744 | tf_op jit(solution)/shard_map/ppermute | solution.py:234
  38.6 13.8 %collective-permute-start = (f32[12,3,2048]{2,1,0:T(4,128)S(1)}, f32[12,3,2048]{2,1,0:T(4,128)S(1)}, u32[]{:S(2)}, u32[]{:S(2)}) collective-permute-start(f32[12,3,2048]{2,1,0:T(4,128)S(1)} %get-tuple-element.33), channel_id=1, source_target_pairs={{0,8},{8,16},{16,24},{24,1},{32,40},{40,48},{48,56},{56,33},{64,72... | collective-permute-start | bytes 884744 | tf_op jit(solution)/shard_map/ppermute | solution.py:233
  44.1 8.3 %copy-start = (f32[12,16,2048]{2,1,0:T(8,128)S(1)}, f32[12,16,2048]{2,1,0:T(8,128)}, u32[]{:S(2)}) copy-start(f32[12,16,2048]{2,1,0:T(8,128)} %shard_map.73) | copy-start | bytes 4718596
  47.4 6.9 %copy-start.2 = (f32[12,16,1]{2,1,0:T(8,128)}, f32[12,16,1]{2,1,0:T(8,128)S(1)}, u32[]{:S(2)}) copy-start(f32[12,16,1]{2,1,0:T(8,128)S(1)} %copy.170.take_ref) | copy-start | bytes 2308
  70.6 11.9 %copy-start.1 = (f32[12,16,2048]{2,1,0:T(8,128)S(1)}, f32[12,16,2048]{2,1,0:T(8,128)}, u32[]{:S(2)}) copy-start(f32[12,16,2048]{2,1,0:T(8,128)} %shard_map.74) | copy-start | bytes 4718596
  72.2 9.4 %collective-permute-start.3 = (f32[12,3,2048]{2,1,0:T(4,128)S(1)}, f32[12,3,2048]{2,1,0:T(4,128)S(1)}, u32[]{:S(2)}, u32[]{:S(2)}) collective-permute-start(f32[12,3,2048]{2,1,0:T(4,128)S(1)} %get-tuple-element.32), channel_id=1, source_target_pairs={{8,0},{16,8},{24,16},{1,24},{40,32},{48,40},{56,48},{33,56},{72,64... | collective-permute-start | bytes 884744 | tf_op jit(solution)/shard_map/ppermute | solution.py:234
  74.2 8.3 %collective-permute-start.2 = (f32[12,3,2048]{2,1,0:T(4,128)S(1)}, f32[12,3,2048]{2,1,0:T(4,128)S(1)}, u32[]{:S(2)}, u32[]{:S(2)}) collective-permute-start(f32[12,3,2048]{2,1,0:T(4,128)S(1)} %get-tuple-element.31), channel_id=1, source_target_pairs={{0,8},{8,16},{16,24},{24,1},{32,40},{40,48},{48,56},{56,33},{64,72... | collective-permute-start | bytes 884744 | tf_op jit(solution)/shard_map/ppermute | solution.py:233
  80.8 3.5 %copy-start.3 = (f32[12,16,1]{2,1,0:T(8,128)}, f32[12,16,1]{2,1,0:T(8,128)S(1)}, u32[]{:S(2)}) copy-start(f32[12,16,1]{2,1,0:T(8,128)S(1)} %copy.180.take_ref) | copy-start | bytes 2308

commit v2 on v0

--- a/solution.py
+++ b/solution.py
@@ -134,48 +134,125 @@
     return total.reshape(block.shape)
 
 
-def exchange_kernel(src_ref, dst_ref, send_sem, recv_sem, local_sem, *, src_at, dst_at):
+GROUP = 4
+
+
+def exchange_kernel(src_ref, dst_ref, relay_buf, send_sem, recv_sem, local_sem, relay_send, relay_recv, fwd_send, fwd_recv, *, src_at, dst_at):
     count = lax.axis_size("lon")
+    ring = count // GROUP
+    far = ring // 2
     me = lax.axis_index("lon")
     lat = lax.axis_index("lat")
+    x_me, lo_me = me // GROUP, me % GROUP
+    levels = relay_buf.shape[1] * 2
+    half = levels // 2
+    everything = pl.ds(0, levels)
+    low_half, high_half = pl.ds(0, half), pl.ds(half, half)
+
+    def device(peer):
+        return (peer, lat)
+
     barrier = pltpu.get_barrier_semaphore()
     for offset in range(1, count):
         peer = lax.rem(me + offset, count)
-        pl.semaphore_signal(barrier, 1, device_id=(peer, lat), device_id_type=pl.DeviceIdType.MESH)
+        pl.semaphore_signal(barrier, 1, device_id=device(peer), device_id_type=pl.DeviceIdType.MESH)
     pl.semaphore_wait(barrier, count - 1)
+
+    peers = [(x_me * GROUP + lax.rem(lo_me + j, GROUP), False, j - 1, j - 1) for j in range(1, GROUP)]
+    for dx in range(1, ring):
+        for lo in range(GROUP):
+            base = GROUP - 1 + (dx - 1) * GROUP
+            peers.append((lax.rem(x_me + dx, ring) * GROUP + lo, dx == far, base + lo, base + lo_me))
     copies = []
-    for offset in range(1, count):
-        peer = lax.rem(me + offset, count)
+    arrivals = []
+    relays = []
+    for peer, split, mine, theirs in peers:
+        part = low_half if split else everything
         copy = pltpu.make_async_remote_copy(
-            src_ref=src_at(src_ref, peer),
-            dst_ref=dst_at(dst_ref, me),
-            send_sem=send_sem.at[offset],
-            recv_sem=recv_sem.at[offset],
-            device_id=(peer, lat),
+            src_ref=src_at(src_ref, peer, part),
+            dst_ref=dst_at(dst_ref, me, part),
+            send_sem=send_sem.at[mine],
+            recv_sem=recv_sem.at[theirs],
+            device_id=device(peer),
             device_id_type=pl.DeviceIdType.MESH,
         )
         copy.start()
         copies.append(copy)
-    local = pltpu.make_async_copy(src_at(src_ref, me), dst_at(dst_ref, me), local_sem)
+        arrivals.append(
+            pltpu.make_async_remote_copy(
+                src_ref=src_at(src_ref, peer, part),
+                dst_ref=dst_at(dst_ref, me, part),
+                send_sem=send_sem.at[mine],
+                recv_sem=recv_sem.at[mine],
+                device_id=device(peer),
+                device_id_type=pl.DeviceIdType.MESH,
+            )
+        )
+        if split:
+            lo = len(relays)
+            helper = lax.rem(x_me + ring - 1, ring) * GROUP + lo
+            relay = pltpu.make_async_remote_copy(
+                src_ref=src_at(src_ref, peer, high_half),
+                dst_ref=relay_buf.at[lo_me],
+                send_sem=relay_send.at[lo],
+                recv_sem=relay_recv.at[lo_me],
+                device_id=device(helper),
+                device_id_type=pl.DeviceIdType.MESH,
+            )
+            relay.start()
+            relays.append(relay)
+    local = pltpu.make_async_copy(src_at(src_ref, me, everything), dst_at(dst_ref, me, everything), local_sem)
     local.start()
-    for copy in copies:
+
+    target = lax.rem(x_me + ring - 1, ring) * GROUP + lo_me
+    forwards = []
+    for lo in range(GROUP):
+        origin = lax.rem(x_me + 1, ring) * GROUP + lo
+        arrived = pltpu.make_async_remote_copy(
+            src_ref=relay_buf.at[lo],
+            dst_ref=relay_buf.at[lo],
+            send_sem=relay_send.at[lo],
+            recv_sem=relay_recv.at[lo],
+            device_id=device(target),
+            device_id_type=pl.DeviceIdType.MESH,
+        )
+        arrived.wait_recv()
+        forward = pltpu.make_async_remote_copy(
+            src_ref=relay_buf.at[lo],
+            dst_ref=dst_at(dst_ref, origin, high_half),
+            send_sem=fwd_send.at[lo],
+            recv_sem=fwd_recv.at[lo],
+            device_id=device(target),
+            device_id_type=pl.DeviceIdType.MESH,
+        )
+        forward.start()
+        forwards.append(forward)
+    for copy in copies + relays + forwards:
         copy.wait_send()
-    for copy in copies:
-        copy.wait_recv()
+    for arrival in arrivals:
+        arrival.wait_recv()
+    for forward in forwards:
+        forward.wait_recv()
     local.wait()
 
 
-def exchange(block, out_shape, src_at, dst_at, ident):
+def exchange(block, out_shape, piece, src_at, dst_at, ident):
     count = lax.axis_size("lon")
+    levels = block.shape[0]
     return pl.pallas_call(
         functools.partial(exchange_kernel, src_at=src_at, dst_at=dst_at),
         out_shape=jax.ShapeDtypeStruct(out_shape, block.dtype),
         in_specs=[pl.BlockSpec(memory_space=pl.ANY)],
         out_specs=pl.BlockSpec(memory_space=pl.ANY),
         scratch_shapes=[
+            pltpu.VMEM((GROUP, levels // 2) + piece, block.dtype),
             pltpu.SemaphoreType.DMA((count,)),
             pltpu.SemaphoreType.DMA((count,)),
             pltpu.SemaphoreType.DMA,
+            pltpu.SemaphoreType.DMA((GROUP,)),
+            pltpu.SemaphoreType.DMA((GROUP,)),
+            pltpu.SemaphoreType.DMA((GROUP,)),
+            pltpu.SemaphoreType.DMA((GROUP,)),
         ],
         compiler_params=pltpu.CompilerParams(collective_id=ident, has_side_effects=True),
     )(block)
@@ -190,13 +267,13 @@
     lane = cells * PAIR
     moved = exact_permute(block, pair_order(cells), False)
 
-    def src_at(ref, peer):
-        return ref.at[:, pl.ds((peer % parts) * count, count), pl.ds((peer // parts) * lane, lane)]
-
-    def dst_at(ref, sender):
-        return ref.at[:, :, pl.ds(sender * lane, lane)]
-
-    return exchange(moved, (levels, count, devices * lane), src_at, dst_at, 0)
+    def src_at(ref, peer, part):
+        return ref.at[part, pl.ds((peer % parts) * count, count), pl.ds((peer // parts) * lane, lane)]
+
+    def dst_at(ref, sender, part):
+        return ref.at[part, :, pl.ds(sender * lane, lane)]
+
+    return exchange(moved, (levels, count, devices * lane), (count, lane), src_at, dst_at, 0)
 
 
 def from_columns(field, rows):
@@ -206,13 +283,13 @@
     lane = width // devices
     cells = lane // PAIR
 
-    def src_at(ref, peer):
-        return ref.at[:, :, pl.ds(peer * lane, lane)]
-
-    def dst_at(ref, sender):
-        return ref.at[:, pl.ds((sender % parts) * count, count), pl.ds((sender // parts) * lane, lane)]
-
-    moved = exchange(field, (levels, rows, cells * NTR), src_at, dst_at, 1)
+    def src_at(ref, peer, part):
+        return ref.at[part, :, pl.ds(peer * lane, lane)]
+
+    def dst_at(ref, sender, part):
+        return ref.at[part, pl.ds((sender % parts) * count, count), pl.ds((sender // parts) * lane, lane)]
+
+    moved = exchange(field, (levels, rows, cells * NTR), (count, lane), src_at, dst_at, 1)
     return exact_permute(moved, pair_order(cells), True)
 
 

time: 118 us -> 119 us (level)
  the two profiles are of different devices: /device:TPU:101 before, /device:TPU:25 now
where the time goes in v2:
time: 119 us; the launch traced here: 118 us
  Pallas kernels  58.8 us (49%)
  other arithmetic  19.4 us (16%)
  waiting for transfers between devices  12.5 us (11%)
  starting transfers between devices  11.3 us (9%)
  local copies, waits for them, and re-layouts  9.61 us (8%)
  matrix products  5.21 us (4%)
    pallas_call x2, Pallas kernels, exchange(): pl.pallas_call(functools.partial(exchange_kernel, src_at=src_at, dst_at=d...  58.8 us
    ppermute x2, waiting for transfers between devices, lat_halo(): above = lax.ppermute(field[:, :width], ('lon', 'lat'), down)  11.3 us
    select_n x20, other arithmetic, roll_rows(): current = jnp.where(bit_mask(amount, position), moved, current)  7.75 us
    ppermute x2, starting transfers between devices, lat_halo(): above = lax.ppermute(field[:, :width], ('lon', 'lat'), down)  7.29 us
    dot_general x6, matrix products, exact_permute(): jnp.dot(part.astype(jnp.bfloat16), matrix, preferred_element_type=jnp.flo...  5.21 us
    ppermute x2, starting transfers between devices, lat_halo(): below = lax.ppermute(field[:, rows - width:], ('lon', 'lat'), up)  4 us
    convert_element_type x2, other arithmetic, exact_permute(): part.astype(jnp.bfloat16)  3.55 us
    add x2, other arithmetic, lat_step(): summed = addend if summed is None else summed + addend  3.53 us
  transfers between devices with their start and end apart: 4, of which 4 were waited for; matrix products, arithmetic and copies ran while one was open for 1% of the time, Pallas kernels for 0%

profile of v2, /device:TPU:25, one launch (start us, length us, event | category | flops | bytes accessed | tf_op | source)
XLA Modules:
  0.0 117.7 jit_solution(17033360493332565686)
XLA Ops:
  0.0 1.8 %reduce-precision_convert_fusion.3 = (bf16[768,512]{1,0:T(8,128)(2,1)S(1)}, bf16[768,512]{1,0:T(8,128)(2,1)S(1)}, bf16[768,512]{1,0:T(8,128)(2,1)S(1)}) fusion(f32[12,64,512]{2,1,0:T(8,128)} %param.7), kind=kLoop, calls=%fused_computation.19 | loop fusion | flops 3145728 | bytes 3932160 | tf_op jit(solution)/shard_map/convert_element_type | solution.py:132
  1.8 0.7 fusion.41
  2.5 0.7 fusion.42
  3.2 0.8 fusion.38
  4.0 1.6 %copy.23 = f32[768,512]{1,0:T(8,128)} copy(f32[768,512]{0,1:T(8,128)S(1)} %fusion.38) | data formatting | bytes 3145728 | tf_op jit(solution)/shard_map/add | solution.py:133
  5.6 29.4 %shard_map.73 = f32[12,16,2048]{2,1,0:T(8,128)} custom-call(f32[12,64,512]{2,1,0:T(8,128)} %bitcast.585), custom_call_target="tpu_custom_call" | custom-call | tf_op jit(solution)/shard_map/pallas_call | solution.py:242
  35.1 1.6 %fusion.248 = (f32[12,3,2048]{2,1,0:T(4,128)S(1)}, f32[12,3,2048]{2,1,0:T(4,128)S(1)}) fusion(f32[12,16,2048]{2,1,0:T(8,128)} %shard_map.73), kind=kLoop, calls=%fused_computation.590 | loop fusion | bytes 1179648 | tf_op jit(solution)/shard_map/slice | solution.py:311
  36.8 2.1 %collective-permute-start = (f32[12,3,2048]{2,1,0:T(4,128)S(1)}, f32[12,3,2048]{2,1,0:T(4,128)S(1)}, u32[]{:S(2)}, u32[]{:S(2)}) collective-permute-start(f32[12,3,2048]{2,1,0:T(4,128)S(1)} %get-tuple-element.67), channel_id=1, source_target_pairs={{0,8},{8,16},{16,24},{24,1},{32,40},{40,48},{48,56},{56,33},{64,72... | collective-permute-start | bytes 884744 | tf_op jit(solution)/shard_map/ppermute | solution.py:310
  38.9 2.8 %collective-permute-start.1 = (f32[12,3,2048]{2,1,0:T(4,128)S(1)}, f32[12,3,2048]{2,1,0:T(4,128)S(1)}, u32[]{:S(2)}, u32[]{:S(2)}) collective-permute-start(f32[12,3,2048]{2,1,0:T(4,128)S(1)} %get-tuple-element.66), channel_id=1, source_target_pairs={{8,0},{16,8},{24,16},{1,24},{40,32},{48,40},{56,48},{33,56},{72,64... | collective-permute-start | bytes 884744 | tf_op jit(solution)/shard_map/ppermute | solution.py:311
  41.9 0.1 constant_dynamic-slice_fusion
  42.1 0.1 constant_dynamic-slice_fusion.1
  42.5 1.1 collective-permute-done
  43.6 4.7 %collective-permute-done.1 = f32[12,3,2048]{2,1,0:T(4,128)S(1)} collective-permute-done((f32[12,3,2048]{2,1,0:T(4,128)S(1)}, f32[12,3,2048]{2,1,0:T(4,128)S(1)}, u32[]{:S(2)}, u32[]{:S(2)}) %collective-permute-start.1) | collective-permute-done | bytes 294944 | tf_op jit(solution)/shard_map/ppermute | solution.py:311
  48.3 1.7 %fusion.17 = f32[12,16,2048]{2,1,0:T(8,128)S(1)} fusion(f32[12,3,2048]{2,1,0:T(4,128)S(1)} %collective-permute-done, f32[12,16,2048]{2,1,0:T(8,128)S(1)} %copy-done, f32[12,3,2048]{2,1,0:T(4,128)S(1)} %collective-permute-done.1, f32[12,16]{1,0:T(8,128)S(1)} %get-tuple-element.92, f32[12,16]{1,0:T(8,128)S(1)} %get-tuple-element.91, ...), kind=kLoop, calls=%fused_computation.37 | loop fusion | flops 6291456 | bytes 3740160 | tf_op jit(solution)/shard_map/add | solution.py:51
  50.1 0.5 maximum_select_fusion
  50.7 0.5 maximum_select_fusion.1
  51.3 0.5 maximum_select_fusion.2
  51.9 0.5 maximum_select_fusion.3
  52.5 0.5 maximum_select_fusion.4
  53.1 0.5 maximum_select_fusion.5
  53.6 0.1 slice.556
  53.7 0.2 maximum_select_fusion.6
  54.0 0.1 slice.558
  54.1 0.2 maximum_select_fusion.7
  54.4 0.2 maximum_select_fusion.8
  54.7 0.2 fusion.247
  54.8 0.2 maximum_select_fusion.9
  55.1 0.6 fusion.245
  55.7 0.5 slice.567
  56.2 0.9 fusion.32
  57.2 0.1 slice.569
  57.3 0.3 fusion.33
  57.6 0.4 subtract_dynamic-update-slice_fusion.1
  58.4 0.1 constant_dynamic-update-slice_fusion.1
  58.6 0.1 fusion.244
  58.8 1.9 %collective-permute-start.2 = (f32[12,3,2048]{2,1,0:T(4,128)S(1)}, f32[12,3,2048]{2,1,0:T(4,128)S(1)}, u32[]{:S(2)}, u32[]{:S(2)}) collective-permute-start(f32[12,3,2048]{2,1,0:T(4,128)S(1)} %get-tuple-element.59), channel_id=1, source_target_pairs={{0,8},{8,16},{16,24},{24,1},{32,40},{40,48},{48,56},{56,33},{64,72... | collective-permute-start | bytes 884744 | tf_op jit(solution)/shard_map/ppermute | solution.py:310
  60.7 4.5 %collective-permute-start.3 = (f32[12,3,2048]{2,1,0:T(4,128)S(1)}, f32[12,3,2048]{2,1,0:T(4,128)S(1)}, u32[]{:S(2)}, u32[]{:S(2)}) collective-permute-start(f32[12,3,2048]{2,1,0:T(4,128)S(1)} %get-tuple-element.58), channel_id=1, source_target_pairs={{8,0},{16,8},{24,16},{1,24},{40,32},{48,40},{56,48},{33,56},{72,64... | collective-permute-start | bytes 884744 | tf_op jit(solution)/shard_map/ppermute | solution.py:311
  65.4 6.6 %collective-permute-done.3 = f32[12,3,2048]{2,1,0:T(4,128)S(1)} collective-permute-done((f32[12,3,2048]{2,1,0:T(4,128)S(1)}, f32[12,3,2048]{2,1,0:T(4,128)S(1)}, u32[]{:S(2)}, u32[]{:S(2)}) %collective-permute-start.3) | collective-permute-done | bytes 294944 | tf_op jit(solution)/shard_map/ppermute | solution.py:311
  72.0 1.8 %fusion.10 = f32[12,16,2048]{2,1,0:T(8,128)S(1)} fusion(f32[12,3,2048]{2,1,0:T(4,128)S(1)} %collective-permute-done.2, f32[12,16,2048]{2,1,0:T(8,128)S(1)} %constant_dynamic-update-slice_fusion, f32[12,3,2048]{2,1,0:T(4,128)S(1)} %collective-permute-done.3, f32[12,16]{1,0:T(8,128)S(1)} %get-tuple-element.82, f32[12,16]{1,0:T(8,128)S(1)} %get-tuple-element.81, ...), kind=kLoop, calls=%fused_computation.30 | loop fusion | flops 6291456 | bytes 3740160 | tf_op jit(solution)/shard_map/add | solution.py:51
  73.9 0.5 maximum_select_fusion.10
  74.5 0.5 maximum_select_fusion.11
  75.1 0.5 maximum_select_fusion.12
  75.7 0.5 maximum_select_fusion.13
  76.3 0.5 maximum_select_fusion.14
  76.9 0.5 maximum_select_fusion.15
  77.4 0.1 slice.615
  77.5 0.2 maximum_select_fusion.16
  77.8 0.1 slice.617
  77.9 0.2 maximum_select_fusion.17
  78.3 0.2 maximum_select_fusion.18
  78.5 0.2 fusion.243
  78.6 0.2 maximum_select_fusion.19
  78.9 0.6 fusion.241
  79.5 0.5 slice.626
  80.0 0.9 fusion.36
  81.1 0.3 fusion.37
  81.4 0.4 subtract_dynamic-update-slice_fusion
  82.2 0.1 constant_dynamic-update-slice_fusion.12
  82.4 1.1 copy-done.1
  83.5 29.4 %shard_map.74 = f32[12,64,512]{2,1,0:T(8,128)} custom-call(f32[12,16,2048]{2,1,0:T(8,128)} %copy-done.1), custom_call_target="tpu_custom_call" | custom-call | tf_op jit(solution)/shard_map/pallas_call | solution.py:242
  112.9 1.8 %fusion.3 = (bf16[768,512]{1,0:T(8,128)(2,1)S(1)}, bf16[768,512]{1,0:T(8,128)(2,1)S(1)}, bf16[768,512]{1,0:T(8,128)(2,1)S(1)}) fusion(f32[12,64,512]{2,1,0:T(8,128)} %shard_map.74), kind=kLoop, calls=%fused_computation.23 | loop fusion | flops 3145728 | bytes 3932160 | tf_op jit(solution)/shard_map/convert_element_type | solution.py:132
  114.7 0.6 fusion.39
  115.3 0.6 fusion.40
  116.0 1.8 %add_add_fusion = f32[768,512]{1,0:T(8,128)} fusion(f32[768,512]{1,0:T(8,128)S(1)} %fusion.40, f32[768,512]{1,0:T(8,128)S(1)} %fusion.39, bf16[768,512]{1,0:T(8,128)(2,1)S(1)} %get-tuple-element.49, s32[512]{0:T(512)S(1)} %fusion.224), kind=kOutput, calls=%fused_computation.92 | convolution fusion | flops 403701760 | bytes 5507072 | tf_op jit(solution)/shard_map/dot_general | solution.py:132
  (76 shorter events, 3.2 us)
Async XLA Ops:
  35.1 6.6 %copy-start.3 = (f32[2,12,64]{2,0,1:T(2,128)S(1)}, f32[2,12,64]{2,0,1:T(2,128)}, u32[]{:S(2)}) copy-start(f32[2,12,64]{2,0,1:T(2,128)} %param.12) | copy-start | bytes 18436
  35.1 6.8 %copy-start.4 = (s32[2,12,64]{2,0,1:T(2,128)S(1)}, s32[2,12,64]{2,0,1:T(2,128)}, u32[]{:S(2)}) copy-start(s32[2,12,64]{2,0,1:T(2,128)} %param.8) | copy-start | bytes 18436
  35.1 6.8 %copy-start.5 = (s32[2,12,64]{2,0,1:T(2,128)S(1)}, s32[2,12,64]{2,0,1:T(2,128)}, u32[]{:S(2)}) copy-start(s32[2,12,64]{2,0,1:T(2,128)} %param.10) | copy-start | bytes 18436
  35.1 7.0 %copy-start.6 = (f32[2,12,64]{2,0,1:T(2,128)S(1)}, f32[2,12,64]{2,0,1:T(2,128)}, u32[]{:S(2)}) copy-start(f32[2,12,64]{2,0,1:T(2,128)} %param.11) | copy-start | bytes 18436
  35.1 7.0 %copy-start.7 = (f32[2,12,64]{2,0,1:T(2,128)S(1)}, f32[2,12,64]{2,0,1:T(2,128)}, u32[]{:S(2)}) copy-start(f32[2,12,64]{2,0,1:T(2,128)} %param.9) | copy-start | bytes 18436
  35.1 7.1 %copy-start.2 = (f32[12,64]{1,0:T(8,128)S(1)}, f32[12,64]{1,0:T(8,128)}, u32[]{:S(2)}) copy-start(f32[12,64]{1,0:T(8,128)} %param.13) | copy-start | bytes 9220
  35.1 13.1 %copy-start = (f32[12,16,2048]{2,1,0:T(8,128)S(1)}, f32[12,16,2048]{2,1,0:T(8,128)}, u32[]{:S(2)}) copy-start(f32[12,16,2048]{2,1,0:T(8,128)} %shard_map.73) | copy-start | bytes 4718596
  36.8 6.8 %collective-permute-start = (f32[12,3,2048]{2,1,0:T(4,128)S(1)}, f32[12,3,2048]{2,1,0:T(4,128)S(1)}, u32[]{:S(2)}, u32[]{:S(2)}) collective-permute-start(f32[12,3,2048]{2,1,0:T(4,128)S(1)} %get-tuple-element.67), channel_id=1, source_target_pairs={{0,8},{8,16},{16,24},{24,1},{32,40},{40,48},{48,56},{56,33},{64,72... | collective-permute-start | bytes 884744 | tf_op jit(solution)/shard_map/ppermute | solution.py:310
  38.9 9.4 %collective-permute-start.1 = (f32[12,3,2048]{2,1,0:T(4,128)S(1)}, f32[12,3,2048]{2,1,0:T(4,128)S(1)}, u32[]{:S(2)}, u32[]{:S(2)}) collective-permute-start(f32[12,3,2048]{2,1,0:T(4,128)S(1)} %get-tuple-element.66), channel_id=1, source_target_pairs={{8,0},{16,8},{24,16},{1,24},{40,32},{48,40},{56,48},{33,56},{72,64... | collective-permute-start | bytes 884744 | tf_op jit(solution)/shard_map/ppermute | solution.py:311
  58.8 6.6 %collective-permute-start.2 = (f32[12,3,2048]{2,1,0:T(4,128)S(1)}, f32[12,3,2048]{2,1,0:T(4,128)S(1)}, u32[]{:S(2)}, u32[]{:S(2)}) collective-permute-start(f32[12,3,2048]{2,1,0:T(4,128)S(1)} %get-tuple-element.59), channel_id=1, source_target_pairs={{0,8},{8,16},{16,24},{24,1},{32,40},{40,48},{48,56},{56,33},{64,72... | collective-permute-start | bytes 884744 | tf_op jit(solution)/shard_map/ppermute | solution.py:310
  60.7 11.3 %collective-permute-start.3 = (f32[12,3,2048]{2,1,0:T(4,128)S(1)}, f32[12,3,2048]{2,1,0:T(4,128)S(1)}, u32[]{:S(2)}, u32[]{:S(2)}) collective-permute-start(f32[12,3,2048]{2,1,0:T(4,128)S(1)} %get-tuple-element.58), channel_id=1, source_target_pairs={{8,0},{16,8},{24,16},{1,24},{40,32},{48,40},{56,48},{33,56},{72,64... | collective-permute-start | bytes 884744 | tf_op jit(solution)/shard_map/ppermute | solution.py:311
  82.4 1.1 copy-start.1

commit v3 on v0

--- a/solution.py
+++ b/solution.py
@@ -115,70 +115,137 @@
     return target
 
 
-def exact_permute(block, target, inverse):
-    width = block.shape[-1]
-    flat = block.reshape(-1, width)
-    cols = jnp.arange(width)
+def permutation(target, inverse):
+    cols = jnp.arange(target.shape[0])
     if inverse:
         matrix = cols[:, None] == target[None, :]
     else:
         matrix = cols[None, :] == target[:, None]
-    matrix = matrix.astype(jnp.bfloat16)
-    rest = flat
-    total = None
-    for _ in range(3):
-        part = lax.reduce_precision(rest, exponent_bits=8, mantissa_bits=7)
-        rest = rest - part
-        piece = jnp.dot(part.astype(jnp.bfloat16), matrix, preferred_element_type=jnp.float32)
-        total = piece if total is None else total + piece
-    return total.reshape(block.shape)
-
-
-def exchange_kernel(src_ref, dst_ref, send_sem, recv_sem, local_sem, *, src_at, dst_at):
+    return matrix.astype(jnp.bfloat16)
+
+
+def permute_block(block, matrix):
+    high = block.astype(jnp.bfloat16)
+    rest = block - high.astype(jnp.float32)
+    middle = rest.astype(jnp.bfloat16)
+    low = (rest - middle.astype(jnp.float32)).astype(jnp.bfloat16)
+    total = jnp.dot(high, matrix, preferred_element_type=jnp.float32)
+    total = total + jnp.dot(middle, matrix, preferred_element_type=jnp.float32)
+    return total + jnp.dot(low, matrix, preferred_element_type=jnp.float32)
+
+
+CHUNKS = 2
+MESH_ID = pl.DeviceIdType.MESH
+
+
+def greet(count, me, lat):
+    barrier = pltpu.get_barrier_semaphore()
+    for offset in range(1, count):
+        peer = lax.rem(me + offset, count)
+        pl.semaphore_signal(barrier, 1, device_id=(peer, lat), device_id_type=MESH_ID)
+    return barrier
+
+
+def entry_kernel(x_ref, matrix_ref, dst_ref, moved, send_sem, recv_sem, local_sem, *, src_at, dst_at):
     count = lax.axis_size("lon")
     me = lax.axis_index("lon")
     lat = lax.axis_index("lat")
-    barrier = pltpu.get_barrier_semaphore()
-    for offset in range(1, count):
-        peer = lax.rem(me + offset, count)
-        pl.semaphore_signal(barrier, 1, device_id=(peer, lat), device_id_type=pl.DeviceIdType.MESH)
-    pl.semaphore_wait(barrier, count - 1)
+    levels = x_ref.shape[0]
+    per = levels // CHUNKS
+    barrier = greet(count, me, lat)
     copies = []
-    for offset in range(1, count):
-        peer = lax.rem(me + offset, count)
-        copy = pltpu.make_async_remote_copy(
-            src_ref=src_at(src_ref, peer),
-            dst_ref=dst_at(dst_ref, me),
-            send_sem=send_sem.at[offset],
-            recv_sem=recv_sem.at[offset],
-            device_id=(peer, lat),
-            device_id_type=pl.DeviceIdType.MESH,
-        )
-        copy.start()
-        copies.append(copy)
-    local = pltpu.make_async_copy(src_at(src_ref, me), dst_at(dst_ref, me), local_sem)
-    local.start()
+    locals_ = []
+    for chunk in range(CHUNKS):
+        def body(k, carry):
+            moved[k] = permute_block(x_ref[k], matrix_ref[...])
+            return carry
+
+        lax.fori_loop(chunk * per, (chunk + 1) * per, body, 0)
+        if chunk == 0:
+            pl.semaphore_wait(barrier, count - 1)
+        part = pl.ds(chunk * per, per)
+        for offset in range(1, count):
+            peer = lax.rem(me + offset, count)
+            copy = pltpu.make_async_remote_copy(
+                src_ref=src_at(moved, peer, part),
+                dst_ref=dst_at(dst_ref, me, part),
+                send_sem=send_sem.at[chunk, offset],
+                recv_sem=recv_sem.at[chunk, offset],
+                device_id=(peer, lat),
+                device_id_type=MESH_ID,
+            )
+            copy.start()
+            copies.append(copy)
+        local = pltpu.make_async_copy(src_at(moved, me, part), dst_at(dst_ref, me, part), local_sem.at[chunk])
+        local.start()
+        locals_.append(local)
     for copy in copies:
         copy.wait_send()
     for copy in copies:
         copy.wait_recv()
-    local.wait()
-
-
-def exchange(block, out_shape, src_at, dst_at, ident):
+    for local in locals_:
+        local.wait()
+
+
+def exit_kernel(src_ref, matrix_ref, out_ref, landed, send_sem, recv_sem, local_sem, *, src_at, dst_at):
+    count = lax.axis_size("lon")
+    me = lax.axis_index("lon")
+    lat = lax.axis_index("lat")
+    levels = out_ref.shape[0]
+    per = levels // CHUNKS
+    barrier = greet(count, me, lat)
+    pl.semaphore_wait(barrier, count - 1)
+    copies = []
+    locals_ = []
+    for chunk in range(CHUNKS):
+        part = pl.ds(chunk * per, per)
+        row = []
+        for offset in range(1, count):
+            peer = lax.rem(me + offset, count)
+            copy = pltpu.make_async_remote_copy(
+                src_ref=src_at(src_ref, peer, part),
+                dst_ref=dst_at(landed, me, part),
+                send_sem=send_sem.at[chunk, offset],
+                recv_sem=recv_sem.at[chunk, offset],
+                device_id=(peer, lat),
+                device_id_type=MESH_ID,
+            )
+            copy.start()
+            row.append(copy)
+        copies.append(row)
+        local = pltpu.make_async_copy(src_at(src_ref, me, part), dst_at(landed, me, part), local_sem.at[chunk])
+        local.start()
+        locals_.append(local)
+    for chunk in range(CHUNKS):
+        for copy in copies[chunk]:
+            copy.wait_recv()
+        locals_[chunk].wait()
+
+        def body(k, carry):
+            out_ref[k] = permute_block(landed[k], matrix_ref[...])
+            return carry
+
+        lax.fori_loop(chunk * per, (chunk + 1) * per, body, 0)
+    for row in copies:
+        for copy in row:
+            copy.wait_send()
+
+
+def run_exchange(kernel, operand, matrix, out_shape, src_spec, out_spec, scratch, src_at, dst_at, ident):
     count = lax.axis_size("lon")
     return pl.pallas_call(
-        functools.partial(exchange_kernel, src_at=src_at, dst_at=dst_at),
-        out_shape=jax.ShapeDtypeStruct(out_shape, block.dtype),
-        in_specs=[pl.BlockSpec(memory_space=pl.ANY)],
-        out_specs=pl.BlockSpec(memory_space=pl.ANY),
+        functools.partial(kernel, src_at=src_at, dst_at=dst_at),
+        out_shape=jax.ShapeDtypeStruct(out_shape, operand.dtype),
+        in_specs=[src_spec, pl.BlockSpec(memory_space=pltpu.VMEM)],
+        out_specs=out_spec,
         scratch_shapes=[
-            pltpu.SemaphoreType.DMA((count,)),
-            pltpu.SemaphoreType.DMA((count,)),
-            pltpu.SemaphoreType.DMA,
+            pltpu.VMEM(scratch, operand.dtype),
+            pltpu.SemaphoreType.DMA((CHUNKS, count)),
+            pltpu.SemaphoreType.DMA((CHUNKS, count)),
+            pltpu.SemaphoreType.DMA((CHUNKS,)),
         ],
         compiler_params=pltpu.CompilerParams(collective_id=ident, has_side_effects=True),
-    )(block)
+    )(operand, matrix)
 
 
 def to_columns(block):
@@ -188,15 +255,18 @@
     parts = devices // (NTR // PAIR)
     count = rows // parts
     lane = cells * PAIR
-    moved = exact_permute(block, pair_order(cells), False)
-
-    def src_at(ref, peer):
-        return ref.at[:, pl.ds((peer % parts) * count, count), pl.ds((peer // parts) * lane, lane)]
-
-    def dst_at(ref, sender):
-        return ref.at[:, :, pl.ds(sender * lane, lane)]
-
-    return exchange(moved, (levels, count, devices * lane), src_at, dst_at, 0)
+
+    def src_at(ref, peer, part):
+        return ref.at[part, pl.ds((peer % parts) * count, count), pl.ds((peer // parts) * lane, lane)]
+
+    def dst_at(ref, sender, part):
+        return ref.at[part, :, pl.ds(sender * lane, lane)]
+
+    return run_exchange(
+        entry_kernel, block, permutation(pair_order(cells), False), (levels, count, devices * lane),
+        pl.BlockSpec(memory_space=pltpu.VMEM), pl.BlockSpec(memory_space=pl.ANY), block.shape,
+        src_at, dst_at, 0,
+    )
 
 
 def from_columns(field, rows):
@@ -206,14 +276,18 @@
     lane = width // devices
     cells = lane // PAIR
 
-    def src_at(ref, peer):
-        return ref.at[:, :, pl.ds(peer * lane, lane)]
-
-    def dst_at(ref, sender):
-        return ref.at[:, pl.ds((sender % parts) * count, count), pl.ds((sender // parts) * lane, lane)]
-
-    moved = exchange(field, (levels, rows, cells * NTR), src_at, dst_at, 1)
-    return exact_permute(moved, pair_order(cells), True)
+    def src_at(ref, peer, part):
+        return ref.at[part, :, pl.ds(peer * lane, lane)]
+
+    def dst_at(ref, sender, part):
+        return ref.at[part, pl.ds((sender % parts) * count, count), pl.ds((sender // parts) * lane, lane)]
+
+    shape = (levels, rows, cells * NTR)
+    return run_exchange(
+        exit_kernel, field, permutation(pair_order(cells), True), shape,
+        pl.BlockSpec(memory_space=pl.ANY), pl.BlockSpec(memory_space=pltpu.VMEM), shape,
+        src_at, dst_at, 1,
+    )
 
 
 def lat_halo(field, width):

time: 118 us -> 109 us (0.924)
  the two profiles are of different devices: /device:TPU:101 before, /device:TPU:25 now
where the time goes in v3:
time: 109 us; the launch traced here: 107 us
  Pallas kernels  54.7 us (50%)
  other arithmetic  17 us (16%)
  waiting for transfers between devices  12.6 us (12%)
  starting transfers between devices  11.6 us (11%)
  local copies, waits for them, and re-layouts  10.7 us (10%)
    pallas_call x2, Pallas kernels, run_exchange(): pl.pallas_call(functools.partial(kernel, src_at=src_at, dst_at=dst_at), o...  54.7 us
    ppermute x2, waiting for transfers between devices, lat_halo(): above = lax.ppermute(field[:, :width], ('lon', 'lat'), down)  9.09 us
    select_n x20, other arithmetic, roll_rows(): current = jnp.where(bit_mask(amount, position), moved, current)  7.75 us
    ppermute x2, starting transfers between devices, lat_halo(): below = lax.ppermute(field[:, rows - width:], ('lon', 'lat'), up)  6.59 us
    ppermute x2, starting transfers between devices, lat_halo(): above = lax.ppermute(field[:, :width], ('lon', 'lat'), down)  4.98 us
    unnamed x27, local copies, waits for them, and re-layouts  3.96 us
    add x2, other arithmetic, lat_step(): summed = addend if summed is None else summed + addend  3.53 us
    ppermute x2, waiting for transfers between devices, lat_halo(): below = lax.ppermute(field[:, rows - width:], ('lon', 'lat'), up)  3.48 us
  transfers between devices with their start and end apart: 4, of which 4 were waited for; matrix products, arithmetic and copies ran while one was open for 1% of the time, Pallas kernels for 0%

profile of v3, /device:TPU:25, one launch (start us, length us, event | category | flops | bytes accessed | tf_op | source)
XLA Modules:
  0.0 107.4 jit_solution(2527203690958912857)
XLA Ops:
  0.0 1.1 %fusion.35 = (bf16[512,512]{1,0:T(8,128)(2,1)}, bf16[512,512]{1,0:T(8,128)(2,1)}) fusion(s32[512]{0:T(512)S(1)} %fusion.209), kind=kLoop, calls=%fused_computation.81 | loop fusion | flops 1048576 | bytes 1050624 | tf_op jit(solution)/shard_map/convert_element_type | solution.py:124
  1.1 25.3 %shard_map.73 = f32[12,16,2048]{2,1,0:T(8,128)} custom-call(f32[12,64,512]{2,1,0:T(8,128)} %x_ref.1, bf16[512,512]{1,0:T(8,128)(2,1)} %get-tuple-element.128.matrix_ref), custom_call_target="tpu_custom_call" | custom-call | tf_op jit(solution)/shard_map/pallas_call | solution.py:236
  26.5 1.6 %fusion.233 = (f32[12,3,2048]{2,1,0:T(4,128)S(1)}, f32[12,3,2048]{2,1,0:T(4,128)S(1)}) fusion(f32[12,16,2048]{2,1,0:T(8,128)} %shard_map.73), kind=kLoop, calls=%fused_computation.566 | loop fusion | bytes 1179648 | tf_op jit(solution)/shard_map/slice | solution.py:308
  28.1 4.7 %collective-permute-start = (f32[12,3,2048]{2,1,0:T(4,128)S(1)}, f32[12,3,2048]{2,1,0:T(4,128)S(1)}, u32[]{:S(2)}, u32[]{:S(2)}) collective-permute-start(f32[12,3,2048]{2,1,0:T(4,128)S(1)} %get-tuple-element.64), channel_id=1, source_target_pairs={{0,8},{8,16},{16,24},{24,1},{32,40},{40,48},{48,56},{56,33},{64,72... | collective-permute-start | bytes 884744 | tf_op jit(solution)/shard_map/ppermute | solution.py:307
  32.8 1.9 %collective-permute-start.1 = (f32[12,3,2048]{2,1,0:T(4,128)S(1)}, f32[12,3,2048]{2,1,0:T(4,128)S(1)}, u32[]{:S(2)}, u32[]{:S(2)}) collective-permute-start(f32[12,3,2048]{2,1,0:T(4,128)S(1)} %get-tuple-element.63), channel_id=1, source_target_pairs={{8,0},{16,8},{24,16},{1,24},{40,32},{48,40},{56,48},{33,56},{72,64... | collective-permute-start | bytes 884744 | tf_op jit(solution)/shard_map/ppermute | solution.py:308
  34.8 0.1 constant_dynamic-slice_fusion.3
  34.9 0.1 constant_dynamic-slice_fusion
  35.2 0.1 constant_dynamic-slice_fusion.1
  35.6 2.0 %collective-permute-done = f32[12,3,2048]{2,1,0:T(4,128)S(1)} collective-permute-done((f32[12,3,2048]{2,1,0:T(4,128)S(1)}, f32[12,3,2048]{2,1,0:T(4,128)S(1)}, u32[]{:S(2)}, u32[]{:S(2)}) %collective-permute-start) | collective-permute-done | bytes 294944 | tf_op jit(solution)/shard_map/ppermute | solution.py:307
  37.5 4.4 %collective-permute-done.1 = f32[12,3,2048]{2,1,0:T(4,128)S(1)} collective-permute-done((f32[12,3,2048]{2,1,0:T(4,128)S(1)}, f32[12,3,2048]{2,1,0:T(4,128)S(1)}, u32[]{:S(2)}, u32[]{:S(2)}) %collective-permute-start.1) | collective-permute-done | bytes 294944 | tf_op jit(solution)/shard_map/ppermute | solution.py:308
  41.9 1.7 %fusion.13 = f32[12,16,2048]{2,1,0:T(8,128)S(1)} fusion(f32[12,3,2048]{2,1,0:T(4,128)S(1)} %collective-permute-done, f32[12,16,2048]{2,1,0:T(8,128)S(1)} %copy-done, f32[12,3,2048]{2,1,0:T(4,128)S(1)} %collective-permute-done.1, f32[12,16]{1,0:T(8,128)S(1)} %get-tuple-element.86, f32[12,16]{1,0:T(8,128)S(1)} %get-tuple-element.85, ...), kind=kLoop, calls=%fused_computation.25 | loop fusion | flops 6291456 | bytes 3740160 | tf_op jit(solution)/shard_map/add | solution.py:51
  43.8 0.5 maximum_select_fusion
  44.4 0.5 maximum_select_fusion.1
  45.0 0.5 maximum_select_fusion.2
  45.6 0.5 maximum_select_fusion.3
  46.2 0.5 maximum_select_fusion.4
  46.8 0.5 maximum_select_fusion.5
  47.3 0.1 slice.556
  47.4 0.2 maximum_select_fusion.6
  47.6 0.1 slice.558
  47.8 0.2 maximum_select_fusion.7
  48.1 0.2 maximum_select_fusion.8
  48.3 0.2 fusion.232
  48.5 0.2 maximum_select_fusion.9
  48.7 0.6 fusion.230
  49.3 0.5 slice.567
  49.8 0.1 fusion.231
  49.9 0.9 fusion.28
  50.8 0.1 slice.569
  51.0 0.3 fusion.29
  51.2 0.4 subtract_dynamic-update-slice_fusion.1
  52.1 0.1 constant_dynamic-update-slice_fusion.1
  52.2 0.1 constant_dynamic-update-slice_fusion
  52.3 0.1 fusion.229
  52.4 1.9 %collective-permute-start.2 = (f32[12,3,2048]{2,1,0:T(4,128)S(1)}, f32[12,3,2048]{2,1,0:T(4,128)S(1)}, u32[]{:S(2)}, u32[]{:S(2)}) collective-permute-start(f32[12,3,2048]{2,1,0:T(4,128)S(1)} %get-tuple-element.56), channel_id=1, source_target_pairs={{0,8},{8,16},{16,24},{24,1},{32,40},{40,48},{48,56},{56,33},{64,72... | collective-permute-start | bytes 884744 | tf_op jit(solution)/shard_map/ppermute | solution.py:307
  54.3 3.1 %collective-permute-start.3 = (f32[12,3,2048]{2,1,0:T(4,128)S(1)}, f32[12,3,2048]{2,1,0:T(4,128)S(1)}, u32[]{:S(2)}, u32[]{:S(2)}) collective-permute-start(f32[12,3,2048]{2,1,0:T(4,128)S(1)} %get-tuple-element.55), channel_id=1, source_target_pairs={{8,0},{16,8},{24,16},{1,24},{40,32},{48,40},{56,48},{33,56},{72,64... | collective-permute-start | bytes 884744 | tf_op jit(solution)/shard_map/ppermute | solution.py:308
  57.5 1.5 %collective-permute-done.2 = f32[12,3,2048]{2,1,0:T(4,128)S(1)} collective-permute-done((f32[12,3,2048]{2,1,0:T(4,128)S(1)}, f32[12,3,2048]{2,1,0:T(4,128)S(1)}, u32[]{:S(2)}, u32[]{:S(2)}) %collective-permute-start.2) | collective-permute-done | bytes 294944 | tf_op jit(solution)/shard_map/ppermute | solution.py:307
  59.0 4.7 %collective-permute-done.3 = f32[12,3,2048]{2,1,0:T(4,128)S(1)} collective-permute-done((f32[12,3,2048]{2,1,0:T(4,128)S(1)}, f32[12,3,2048]{2,1,0:T(4,128)S(1)}, u32[]{:S(2)}, u32[]{:S(2)}) %collective-permute-start.3) | collective-permute-done | bytes 294944 | tf_op jit(solution)/shard_map/ppermute | solution.py:308
  63.7 1.8 %fusion.6 = f32[12,16,2048]{2,1,0:T(8,128)S(1)} fusion(f32[12,3,2048]{2,1,0:T(4,128)S(1)} %collective-permute-done.2, f32[12,16,2048]{2,1,0:T(8,128)S(1)} %constant_dynamic-update-slice_fusion, f32[12,3,2048]{2,1,0:T(4,128)S(1)} %collective-permute-done.3, f32[12,16]{1,0:T(8,128)S(1)} %get-tuple-element.76, f32[12,16]{1,0:T(8,128)S(1)} %get-tuple-element.75, ...), kind=kLoop, calls=%fused_computation.18 | loop fusion | flops 6291456 | bytes 3740160 | tf_op jit(solution)/shard_map/add | solution.py:51
  65.6 0.5 maximum_select_fusion.10
  66.2 0.5 maximum_select_fusion.11
  66.8 0.5 maximum_select_fusion.12
  67.4 0.5 maximum_select_fusion.13
  68.0 0.5 maximum_select_fusion.14
  68.6 0.5 maximum_select_fusion.15
  69.1 0.1 slice.615
  69.3 0.2 maximum_select_fusion.16
  69.5 0.1 slice.617
  69.6 0.2 maximum_select_fusion.17
  70.0 0.2 maximum_select_fusion.18
  70.2 0.2 fusion.228
  70.4 0.2 maximum_select_fusion.19
  70.6 0.6 fusion.226
  71.2 0.5 slice.626
  71.7 0.1 fusion.227
  71.8 0.9 fusion.32
  72.7 0.1 slice.628
  72.8 0.3 fusion.33
  73.1 0.4 subtract_dynamic-update-slice_fusion
  73.9 0.1 constant_dynamic-update-slice_fusion.12
  74.0 0.1 constant_dynamic-update-slice_fusion.11.src_ref
  74.2 1.1 %copy-done.1 = f32[12,16,2048]{2,1,0:T(8,128)} copy-done((f32[12,16,2048]{2,1,0:T(8,128)}, f32[12,16,2048]{2,1,0:T(8,128)S(1)}, u32[]{:S(2)}) %copy-start.1) | copy-done | bytes 1572888
  75.3 29.4 %shard_map.74 = f32[12,64,512]{2,1,0:T(8,128)} custom-call(f32[12,16,2048]{2,1,0:T(8,128)} %copy-done.1, bf16[512,512]{1,0:T(8,128)(2,1)} %get-tuple-element.127.matrix_ref), custom_call_target="tpu_custom_call" | custom-call | tf_op jit(solution)/shard_map/pallas_call | solution.py:236
  104.7 2.7 %copy.482 = f32[12,64,512]{2,1,0:T(8,128)} copy(f32[12,64,512]{2,1,0:T(8,128)} %shard_map.74) | data formatting | bytes 3145728
  (69 shorter events, 2.6 us)
Async XLA Ops:
  26.4 8.4 %copy-start.3 = (f32[2,12,64]{2,0,1:T(2,128)S(1)}, f32[2,12,64]{2,0,1:T(2,128)}, u32[]{:S(2)}) copy-start(f32[2,12,64]{2,0,1:T(2,128)} %param.12) | copy-start | bytes 18436
  26.4 8.5 %copy-start.4 = (s32[2,12,64]{2,0,1:T(2,128)S(1)}, s32[2,12,64]{2,0,1:T(2,128)}, u32[]{:S(2)}) copy-start(s32[2,12,64]{2,0,1:T(2,128)} %param.8) | copy-start | bytes 18436
  26.4 8.5 %copy-start.5 = (s32[2,12,64]{2,0,1:T(2,128)S(1)}, s32[2,12,64]{2,0,1:T(2,128)}, u32[]{:S(2)}) copy-start(s32[2,12,64]{2,0,1:T(2,128)} %param.10) | copy-start | bytes 18436
  26.5 8.7 %copy-start.6 = (f32[2,12,64]{2,0,1:T(2,128)S(1)}, f32[2,12,64]{2,0,1:T(2,128)}, u32[]{:S(2)}) copy-start(f32[2,12,64]{2,0,1:T(2,128)} %param.11) | copy-start | bytes 18436
  26.5 8.7 %copy-start.7 = (f32[2,12,64]{2,0,1:T(2,128)S(1)}, f32[2,12,64]{2,0,1:T(2,128)}, u32[]{:S(2)}) copy-start(f32[2,12,64]{2,0,1:T(2,128)} %param.9) | copy-start | bytes 18436
  26.5 8.8 %copy-start.2 = (f32[12,64]{1,0:T(8,128)S(1)}, f32[12,64]{1,0:T(8,128)}, u32[]{:S(2)}) copy-start(f32[12,64]{1,0:T(8,128)} %param.13) | copy-start | bytes 9220
  26.5 15.4 %copy-start = (f32[12,16,2048]{2,1,0:T(8,128)S(1)}, f32[12,16,2048]{2,1,0:T(8,128)}, u32[]{:S(2)}) copy-start(f32[12,16,2048]{2,1,0:T(8,128)} %shard_map.73) | copy-start | bytes 4718596
  28.1 9.4 %collective-permute-start = (f32[12,3,2048]{2,1,0:T(4,128)S(1)}, f32[12,3,2048]{2,1,0:T(4,128)S(1)}, u32[]{:S(2)}, u32[]{:S(2)}) collective-permute-start(f32[12,3,2048]{2,1,0:T(4,128)S(1)} %get-tuple-element.64), channel_id=1, source_target_pairs={{0,8},{8,16},{16,24},{24,1},{32,40},{40,48},{48,56},{56,33},{64,72... | collective-permute-start | bytes 884744 | tf_op jit(solution)/shard_map/ppermute | solution.py:307
  32.8 9.1 %collective-permute-start.1 = (f32[12,3,2048]{2,1,0:T(4,128)S(1)}, f32[12,3,2048]{2,1,0:T(4,128)S(1)}, u32[]{:S(2)}, u32[]{:S(2)}) collective-permute-start(f32[12,3,2048]{2,1,0:T(4,128)S(1)} %get-tuple-element.63), channel_id=1, source_target_pairs={{8,0},{16,8},{24,16},{1,24},{40,32},{48,40},{56,48},{33,56},{72,64... | collective-permute-start | bytes 884744 | tf_op jit(solution)/shard_map/ppermute | solution.py:308
  52.4 6.6 %collective-permute-start.2 = (f32[12,3,2048]{2,1,0:T(4,128)S(1)}, f32[12,3,2048]{2,1,0:T(4,128)S(1)}, u32[]{:S(2)}, u32[]{:S(2)}) collective-permute-start(f32[12,3,2048]{2,1,0:T(4,128)S(1)} %get-tuple-element.56), channel_id=1, source_target_pairs={{0,8},{8,16},{16,24},{24,1},{32,40},{40,48},{48,56},{56,33},{64,72... | collective-permute-start | bytes 884744 | tf_op jit(solution)/shard_map/ppermute | solution.py:307
  54.3 9.4 %collective-permute-start.3 = (f32[12,3,2048]{2,1,0:T(4,128)S(1)}, f32[12,3,2048]{2,1,0:T(4,128)S(1)}, u32[]{:S(2)}, u32[]{:S(2)}) collective-permute-start(f32[12,3,2048]{2,1,0:T(4,128)S(1)} %get-tuple-element.55), channel_id=1, source_target_pairs={{8,0},{16,8},{24,16},{1,24},{40,32},{48,40},{56,48},{33,56},{72,64... | collective-permute-start | bytes 884744 | tf_op jit(solution)/shard_map/ppermute | solution.py:308
  74.1 1.1 %copy-start.1 = (f32[12,16,2048]{2,1,0:T(8,128)}, f32[12,16,2048]{2,1,0:T(8,128)S(1)}, u32[]{:S(2)}) copy-start(f32[12,16,2048]{2,1,0:T(8,128)S(1)} %constant_dynamic-update-slice_fusion.11.src_ref) | copy-start | bytes 4718596

commit v4 on v3

--- a/solution.py
+++ b/solution.py
@@ -290,23 +290,77 @@
     )
 
 
-def lat_halo(field, width):
-    lon_n = lax.axis_size("lon")
-    lat_n = lax.axis_size("lat")
-    parts = lon_n // (NTR // PAIR)
-    up = []
-    for b in range(lat_n):
-        for l in range(lon_n):
-            t, h = l // parts, l % parts
-            g = b * parts + h
-            if g + 1 < lat_n * parts:
-                nb, nh = (g + 1) // parts, (g + 1) % parts
-                up.append((l * lat_n + b, (t * parts + nh) * lat_n + nb))
-    down = [(d, s) for s, d in up]
+def halo_kernel(top_ref, bottom_ref, below_ref, above_ref, send_sem, recv_sem, *, parts):
+    lon = lax.axis_index("lon")
+    lat = lax.axis_index("lat")
+    bands = lax.axis_size("lat")
+    quarter = lon % parts
+    has_up = jnp.logical_or(quarter < parts - 1, lat < bands - 1)
+    has_down = jnp.logical_or(quarter > 0, lat > 0)
+    up = (jnp.where(quarter < parts - 1, lon + 1, lon + 1 - parts), jnp.where(quarter < parts - 1, lat, lat + 1))
+    down = (jnp.where(quarter > 0, lon - 1, lon + parts - 1), jnp.where(quarter > 0, lat, lat - 1))
+    barrier = pltpu.get_barrier_semaphore()
+
+    @pl.when(has_up)
+    def _():
+        pl.semaphore_signal(barrier, 1, device_id=up, device_id_type=MESH_ID)
+
+    @pl.when(has_down)
+    def _():
+        pl.semaphore_signal(barrier, 1, device_id=down, device_id_type=MESH_ID)
+
+    pl.semaphore_wait(barrier, has_up.astype(jnp.int32) + has_down.astype(jnp.int32))
+    to_up = pltpu.make_async_remote_copy(
+        src_ref=top_ref, dst_ref=below_ref, send_sem=send_sem.at[0], recv_sem=recv_sem.at[0],
+        device_id=up, device_id_type=MESH_ID,
+    )
+    to_down = pltpu.make_async_remote_copy(
+        src_ref=bottom_ref, dst_ref=above_ref, send_sem=send_sem.at[1], recv_sem=recv_sem.at[1],
+        device_id=down, device_id_type=MESH_ID,
+    )
+
+    @pl.when(has_up)
+    def _():
+        to_up.start()
+
+    @pl.when(has_down)
+    def _():
+        to_down.start()
+
+    @pl.when(jnp.logical_not(has_down))
+    def _():
+        below_ref[...] = jnp.zeros(below_ref.shape, below_ref.dtype)
+
+    @pl.when(jnp.logical_not(has_up))
+    def _():
+        above_ref[...] = jnp.zeros(above_ref.shape, above_ref.dtype)
+
+    @pl.when(has_up)
+    def _():
+        to_up.wait_send()
+        to_down.wait_recv()
+
+    @pl.when(has_down)
+    def _():
+        to_down.wait_send()
+        to_up.wait_recv()
+
+
+def lat_halo(field, ident):
+    parts = lax.axis_size("lon") // (NTR // PAIR)
     rows = field.shape[1]
-    below = lax.ppermute(field[:, rows - width :], ("lon", "lat"), up)
-    above = lax.ppermute(field[:, :width], ("lon", "lat"), down)
-    return jnp.concatenate([below, field, above], axis=1)
+    top = field[:, rows - 2 :]
+    bottom = field[:, :3]
+    vmem = pl.BlockSpec(memory_space=pltpu.VMEM)
+    below, above = pl.pallas_call(
+        functools.partial(halo_kernel, parts=parts),
+        out_shape=(jax.ShapeDtypeStruct(top.shape, field.dtype), jax.ShapeDtypeStruct(bottom.shape, field.dtype)),
+        in_specs=[vmem, vmem],
+        out_specs=(vmem, vmem),
+        scratch_shapes=[pltpu.SemaphoreType.DMA((2,)), pltpu.SemaphoreType.DMA((2,))],
+        compiler_params=pltpu.CompilerParams(collective_id=ident, has_side_effects=True),
+    )(top, bottom)
+    return jnp.concatenate([below[:, :1], below, field, above], axis=1)
 
 
 def roll_rows(field, amount):
@@ -343,7 +397,7 @@
         own_rows(v, count) for v in (lon_shift, lon_frac, lat_shift, lat_frac, remap_frac, diffusivity)
     )
     for time_step in range(STEPS):
-        padded = lat_halo(field, 3)
+        padded = lat_halo(field, 2 + time_step)
         field = lat_step(padded, lat_shift[time_step], lat_frac[time_step], count)
         amount = jnp.remainder(lon_shift[time_step], width // PAIR)
         field = lon_cubic(roll_rows(field, amount), lon_frac[time_step])

time: 109 us -> 115 us (1.055)
  Pallas kernels: 54.7 us -> 76 us
  waiting for transfers between devices: 12.6 us -> 0 us
  starting transfers between devices: 11.6 us -> 0 us
  local copies, waits for them, and re-layouts: 10.7 us -> 17 us
  other arithmetic: 17 us -> 19.7 us
    pallas_call x0 -> x2, Pallas kernels: none -> 20.3 us  [lat_halo(): pl.pallas_call(functools.partial(halo_kernel, parts=parts), out_shape=(ja...]
    ppermute x4 -> x0, waiting for transfers between devices: 12.6 us -> none  [the longest x2 9.09 us: lat_halo(): above = lax.ppermute(field[:, :width], ('lon', 'lat'), down)]
    ppermute x4 -> x0, starting transfers between devices: 11.6 us -> none  [the longest x2 6.59 us: lat_halo(): below = lax.ppermute(field[:, rows - width:], ('lon', 'lat'), up)]
    slice x2 -> x4, local copies, waits for them, and re-layouts: 1.79 us -> 5.55 us  [the longest x2 2.85 us: lat_halo(): bottom = field[:, :3]]
    add x2, other arithmetic: 3.53 us -> 6.21 us  [lat_step(): summed = addend if summed is None else summed + addend]
    unnamed x27 -> x19, local copies, waits for them, and re-layouts: 3.96 us -> 4.93 us
  transfers between devices with their start and end apart: 4 -> 0, of which waited for: 4 -> 0; matrix products, arithmetic and copies ran while one was open for 1% -> 0% of each run, Pallas kernels for 0% -> 0%
where the time goes in v4:
time: 115 us; the launch traced here: 113 us
  Pallas kernels  76 us (66%)
  other arithmetic  19.7 us (17%)
  local copies, waits for them, and re-layouts  17 us (15%)
    pallas_call x2, Pallas kernels, run_exchange(): pl.pallas_call(functools.partial(kernel, src_at=src_at, dst_at=dst_at), o...  55.8 us
    pallas_call x2, Pallas kernels, lat_halo(): pl.pallas_call(functools.partial(halo_kernel, parts=parts), out_shape=(ja...  20.3 us
    select_n x20, other arithmetic, roll_rows(): current = jnp.where(bit_mask(amount, position), moved, current)  7.74 us
    add x2, other arithmetic, lat_step(): summed = addend if summed is None else summed + addend  6.21 us
    unnamed x19, local copies, waits for them, and re-layouts  4.93 us
    slice x2, local copies, waits for them, and re-layouts, lat_halo(): bottom = field[:, :3]  2.85 us
    slice x2, local copies, waits for them, and re-layouts, lat_halo(): top = field[:, rows - 2:]  2.7 us

profile of v4, /device:TPU:25, one launch (start us, length us, event | category | flops | bytes accessed | tf_op | source)
XLA Modules:
  0.0 113.4 jit_solution(10734215787904200377)
XLA Ops:
  0.0 0.9 constant_dynamic-slice_fusion
  0.9 0.9 constant_dynamic-slice_fusion.1
  1.9 1.1 fusion.35
  3.0 25.3 %shard_map.73 = f32[12,16,2048]{2,1,0:T(8,128)} custom-call(f32[12,64,512]{2,1,0:T(8,128)} %x_ref.1, bf16[512,512]{1,0:T(8,128)(2,1)} %get-tuple-element.132.matrix_ref), custom_call_target="tpu_custom_call" | custom-call | tf_op jit(solution)/shard_map/pallas_call | solution.py:236
  28.3 2.0 %slice.433.bottom_ref = f32[12,3,2048]{2,1,0:T(4,128)} slice(f32[12,16,2048]{2,1,0:T(8,128)} %shard_map.73), slice={[0:12], [0:3], [0:2048]} | slice | bytes 589824 | tf_op jit(solution)/shard_map/slice | solution.py:353
  30.3 1.9 %slice.432.top_ref = f32[12,2,2048]{2,1,0:T(2,128)} slice(f32[12,16,2048]{2,1,0:T(8,128)} %shard_map.73), slice={[0:12], [14:16], [0:2048]} | slice | bytes 393216 | tf_op jit(solution)/shard_map/slice | solution.py:352
  32.2 10.8 %shard_map.74 = (f32[12,2,2048]{2,1,0:T(2,128)}, f32[12,3,2048]{2,1,0:T(4,128)}) custom-call(f32[12,2,2048]{2,1,0:T(2,128)} %slice.432.top_ref, f32[12,3,2048]{2,1,0:T(4,128)} %slice.433.bottom_ref), custom_call_target="tpu_custom_call" | custom-call | tf_op jit(solution)/shard_map/pallas_call | solution.py:355
  43.1 3.1 %fusion.13 = f32[12,16,2048]{2,1,0:T(8,128)S(1)} fusion(f32[12,2,2048]{2,1,0:T(2,128)} %get-tuple-element.9, f32[12,16,2048]{2,1,0:T(8,128)S(1)} %copy-done, f32[12,3,2048]{2,1,0:T(4,128)} %get-tuple-element.10, f32[12,16]{1,0:T(8,128)S(1)} %get-tuple-element.90, f32[12,16]{1,0:T(8,128)S(1)} %get-tuple-element.89, f32[12,16]{1,0:T(8,128)S(1)} %get-tuple-element.88, ...), kind=kLoop, calls=%fused_computation.25 | loop fusion | flops 6291456 | bytes 3641856 | tf_op jit(solution)/shard_map/add | solution.py:51
  46.3 0.1 fusion.117
  46.3 0.5 maximum_select_fusion
  46.9 0.5 maximum_select_fusion.1
  47.5 0.5 maximum_select_fusion.2
  48.1 0.5 maximum_select_fusion.3
  48.7 0.5 maximum_select_fusion.4
  49.3 0.5 maximum_select_fusion.5
  49.9 0.1 slice.558
  50.0 0.2 maximum_select_fusion.6
  50.2 0.1 slice.560
  50.4 0.2 maximum_select_fusion.7
  50.7 0.2 maximum_select_fusion.8
  50.9 0.2 fusion.231
  51.1 0.2 maximum_select_fusion.9
  51.3 0.6 fusion.229
  51.9 0.5 slice.569
  52.4 0.1 fusion.230
  52.5 0.9 fusion.28
  53.5 0.1 slice.571
  53.6 0.6 copy-done.3
  54.2 0.1 constant_dynamic-slice_fusion.3
  54.3 0.3 fusion.29
  54.6 0.4 copy-done.2
  55.2 0.4 subtract_dynamic-update-slice_fusion.1
  56.0 0.1 constant_dynamic-update-slice_fusion.1
  56.1 0.1 constant_dynamic-update-slice_fusion
  56.2 0.8 slice.597.bottom_ref
  57.0 0.8 slice.596.top_ref
  57.8 9.5 %shard_map.75 = (f32[12,2,2048]{2,1,0:T(2,128)}, f32[12,3,2048]{2,1,0:T(4,128)}) custom-call(f32[12,2,2048]{2,1,0:T(2,128)} %slice.596.top_ref, f32[12,3,2048]{2,1,0:T(4,128)} %slice.597.bottom_ref), custom_call_target="tpu_custom_call" | custom-call | tf_op jit(solution)/shard_map/pallas_call | solution.py:355
  67.3 3.1 %fusion.6 = f32[12,16,2048]{2,1,0:T(8,128)S(1)} fusion(f32[12,2,2048]{2,1,0:T(2,128)} %get-tuple-element.11, f32[12,16,2048]{2,1,0:T(8,128)S(1)} %constant_dynamic-update-slice_fusion, f32[12,3,2048]{2,1,0:T(4,128)} %get-tuple-element.12, f32[12,16]{1,0:T(8,128)S(1)} %get-tuple-element.80, f32[12,16]{1,0:T(8,128)S(1)} %get-tuple-element.79, ...), kind=kLoop, calls=%fused_computation.18 | loop fusion | flops 6291456 | bytes 3641856 | tf_op jit(solution)/shard_map/add | solution.py:51
  70.5 0.1 fusion.89
  70.6 0.5 maximum_select_fusion.10
  71.2 0.5 maximum_select_fusion.11
  71.8 0.5 maximum_select_fusion.12
  72.4 0.5 maximum_select_fusion.13
  73.0 0.5 maximum_select_fusion.14
  73.6 0.5 maximum_select_fusion.15
  74.1 0.1 slice.617
  74.2 0.2 maximum_select_fusion.16
  74.5 0.1 slice.619
  74.6 0.2 maximum_select_fusion.17
  75.0 0.2 maximum_select_fusion.18
  75.2 0.2 fusion.228
  75.4 0.2 maximum_select_fusion.19
  75.6 0.6 fusion.226
  76.2 0.5 slice.628
  76.6 0.1 fusion.227
  76.8 0.9 fusion.32
  77.7 0.1 slice.630
  77.8 0.3 fusion.33
  78.1 0.4 subtract_dynamic-update-slice_fusion
  78.9 0.1 constant_dynamic-update-slice_fusion.12
  79.0 0.1 constant_dynamic-update-slice_fusion.11.src_ref
  79.1 1.1 copy-done.1
  80.3 30.5 %shard_map.76 = f32[12,64,512]{2,1,0:T(8,128)} custom-call(f32[12,16,2048]{2,1,0:T(8,128)} %copy-done.1, bf16[512,512]{1,0:T(8,128)(2,1)} %get-tuple-element.131.matrix_ref), custom_call_target="tpu_custom_call" | custom-call | tf_op jit(solution)/shard_map/pallas_call | solution.py:236
  110.8 2.7 %copy.482 = f32[12,64,512]{2,1,0:T(8,128)} copy(f32[12,64,512]{2,1,0:T(8,128)} %shard_map.76) | data formatting | bytes 3145728
  (57 shorter events, 2.4 us)
Async XLA Ops:
  28.3 14.8 %copy-start = (f32[12,16,2048]{2,1,0:T(8,128)S(1)}, f32[12,16,2048]{2,1,0:T(8,128)}, u32[]{:S(2)}) copy-start(f32[12,16,2048]{2,1,0:T(8,128)} %shard_map.73) | copy-start | bytes 4718596
  53.4 0.7 copy-start.3
  54.3 0.7 copy-start.2
  79.1 1.1 %copy-start.1 = (f32[12,16,2048]{2,1,0:T(8,128)}, f32[12,16,2048]{2,1,0:T(8,128)S(1)}, u32[]{:S(2)}) copy-start(f32[12,16,2048]{2,1,0:T(8,128)S(1)} %constant_dynamic-update-slice_fusion.11.src_ref) | copy-start | bytes 4718596

commit v5 on v3

--- a/solution.py
+++ b/solution.py
@@ -134,7 +134,7 @@
     return total + jnp.dot(low, matrix, preferred_element_type=jnp.float32)
 
 
-CHUNKS = 2
+CHUNKS = 4
 MESH_ID = pl.DeviceIdType.MESH
 
 
@@ -304,9 +304,9 @@
                 up.append((l * lat_n + b, (t * parts + nh) * lat_n + nb))
     down = [(d, s) for s, d in up]
     rows = field.shape[1]
-    below = lax.ppermute(field[:, rows - width :], ("lon", "lat"), up)
+    below = lax.ppermute(field[:, rows - width + 1 :], ("lon", "lat"), up)
     above = lax.ppermute(field[:, :width], ("lon", "lat"), down)
-    return jnp.concatenate([below, field, above], axis=1)
+    return jnp.concatenate([below[:, :1], below, field, above], axis=1)
 
 
 def roll_rows(field, amount):

time: 109 us -> 107 us (0.982); the launches traced: 107 us -> 107 us
  waiting for transfers between devices: 12.6 us -> 4.81 us
  starting transfers between devices: 11.6 us -> 16.5 us
  Pallas kernels: 54.7 us -> 56.5 us
    ppermute x2, waiting for transfers between devices: 9.09 us -> 0.01 us  [lat_halo(): above = lax.ppermute(field[:, :width], ('lon', 'lat'), down)]
    ppermute x2, starting transfers between devices: 4.98 us -> 10.3 us  [lat_halo(): above = lax.ppermute(field[:, :width], ('lon', 'lat'), down)]
    pallas_call x2, Pallas kernels: 54.7 us -> 56.5 us  [run_exchange(): pl.pallas_call(functools.partial(kernel, src_at=src_at, dst_at=dst_at), o...]
    ppermute x2, waiting for transfers between devices: 3.48 us -> 4.81 us  [lat_halo(): below = lax.ppermute(field[:, rows - width + 1:], ('lon', 'lat'), up)]
    slice x0 -> x2, local copies, waits for them, and re-layouts: none -> 1.33 us  [lat_halo(): below = lax.ppermute(field[:, rows - width + 1:], ('lon', 'lat'), up)]
  transfers between devices with their start and end apart: 4 -> 4, of which waited for: 4 -> 2; matrix products, arithmetic and copies ran while one was open for 1% -> 2% of each run, Pallas kernels for 0% -> 0%
where the time goes in v5:
time: 107 us
  Pallas kernels  56.5 us (53%)
  other arithmetic  16.9 us (16%)
  starting transfers between devices  16.5 us (15%)
  local copies, waits for them, and re-layouts  11.6 us (11%)
  waiting for transfers between devices  4.81 us (4%)
    pallas_call x2, Pallas kernels, run_exchange(): pl.pallas_call(functools.partial(kernel, src_at=src_at, dst_at=dst_at), o...  56.5 us
    ppermute x2, starting transfers between devices, lat_halo(): above = lax.ppermute(field[:, :width], ('lon', 'lat'), down)  10.3 us
    select_n x20, other arithmetic, roll_rows(): current = jnp.where(bit_mask(amount, position), moved, current)  7.75 us
    ppermute x2, starting transfers between devices, lat_halo(): below = lax.ppermute(field[:, rows - width + 1:], ('lon', 'lat'), up)  6.13 us
    ppermute x2, waiting for transfers between devices, lat_halo(): below = lax.ppermute(field[:, rows - width + 1:], ('lon', 'lat'), up)  4.81 us
    unnamed x27, local copies, waits for them, and re-layouts  3.95 us
    add x2, other arithmetic, lat_step(): summed = addend if summed is None else summed + addend  3.41 us
    slice x8, local copies, waits for them, and re-layouts, lon_cubic(): taps = [jnp.roll(shifted, PAIR * (1 - p), axis=2) for p in range(4)]  2.29 us
  transfers between devices with their start and end apart: 4, of which 2 were waited for; matrix products, arithmetic and copies ran while one was open for 2% of the time, Pallas kernels for 0%

profile of v5, /device:TPU:25, one launch (start us, length us, event | category | flops | bytes accessed | tf_op | source)
XLA Modules:
  0.0 107.0 jit_solution(6139568365759730059)
XLA Ops:
  0.0 1.1 %fusion.35 = (bf16[512,512]{1,0:T(8,128)(2,1)}, bf16[512,512]{1,0:T(8,128)(2,1)}) fusion(s32[512]{0:T(512)S(1)} %fusion.209), kind=kLoop, calls=%fused_computation.81 | loop fusion | flops 1048576 | bytes 1050624 | tf_op jit(solution)/shard_map/convert_element_type | solution.py:124
  1.2 25.9 %shard_map.73 = f32[12,16,2048]{2,1,0:T(8,128)} custom-call(f32[12,64,512]{2,1,0:T(8,128)} %x_ref.1, bf16[512,512]{1,0:T(8,128)(2,1)} %get-tuple-element.124.matrix_ref), custom_call_target="tpu_custom_call" | custom-call | tf_op jit(solution)/shard_map/pallas_call | solution.py:236
  27.0 1.3 %slice.435 = f32[12,3,2048]{2,1,0:T(4,128)S(1)} slice(f32[12,16,2048]{2,1,0:T(8,128)} %shard_map.73), slice={[0:12], [0:3], [0:2048]} | slice | bytes 589824 | tf_op jit(solution)/shard_map/slice | solution.py:308
  28.3 2.2 %collective-permute-start.1 = (f32[12,3,2048]{2,1,0:T(4,128)S(1)}, f32[12,3,2048]{2,1,0:T(4,128)S(1)}, u32[]{:S(2)}, u32[]{:S(2)}) collective-permute-start(f32[12,3,2048]{2,1,0:T(4,128)S(1)} %slice.435), channel_id=1, source_target_pairs={{8,0},{16,8},{24,16},{1,24},{40,32},{48,40},{56,48},{33,56},{72,64... | collective-permute-start | bytes 884744 | tf_op jit(solution)/shard_map/ppermute | solution.py:308
  30.5 1.2 %slice.432 = f32[12,2,2048]{2,1,0:T(2,128)S(1)} slice(f32[12,16,2048]{2,1,0:T(8,128)} %shard_map.73), slice={[0:12], [14:16], [0:2048]} | slice | bytes 393216 | tf_op jit(solution)/shard_map/slice | solution.py:307
  31.8 4.0 %collective-permute-start = (f32[12,2,2048]{2,1,0:T(2,128)S(1)}, f32[12,2,2048]{2,1,0:T(2,128)S(1)}, u32[]{:S(2)}, u32[]{:S(2)}) collective-permute-start(f32[12,2,2048]{2,1,0:T(2,128)S(1)} %slice.432), channel_id=1, source_target_pairs={{0,8},{8,16},{16,24},{24,1},{32,40},{40,48},{48,56},{56,33},{64,72... | collective-permute-start | bytes 589832 | tf_op jit(solution)/shard_map/ppermute | solution.py:307
  35.8 0.1 constant_dynamic-slice_fusion.3
  36.0 0.1 constant_dynamic-slice_fusion
  36.1 0.1 fusion.117
  36.2 0.1 constant_dynamic-slice_fusion.1
  36.6 2.5 %collective-permute-done = f32[12,2,2048]{2,1,0:T(2,128)S(1)} collective-permute-done((f32[12,2,2048]{2,1,0:T(2,128)S(1)}, f32[12,2,2048]{2,1,0:T(2,128)S(1)}, u32[]{:S(2)}, u32[]{:S(2)}) %collective-permute-start) | collective-permute-done | bytes 196640 | tf_op jit(solution)/shard_map/ppermute | solution.py:307
  39.1 1.7 %fusion.13 = f32[12,16,2048]{2,1,0:T(8,128)S(1)} fusion(f32[12,2,2048]{2,1,0:T(2,128)S(1)} %collective-permute-done, f32[12,16,2048]{2,1,0:T(8,128)S(1)} %copy-done, f32[12,3,2048]{2,1,0:T(4,128)S(1)} %collective-permute-done.1, f32[12,16]{1,0:T(8,128)S(1)} %get-tuple-element.82, f32[12,16]{1,0:T(8,128)S(1)} %get-tuple-element.81, ...), kind=kLoop, calls=%fused_computation.25 | loop fusion | flops 6291456 | bytes 3641856 | tf_op jit(solution)/shard_map/add | solution.py:51
  40.9 0.5 maximum_select_fusion
  41.5 0.5 maximum_select_fusion.1
  42.1 0.5 maximum_select_fusion.2
  42.7 0.5 maximum_select_fusion.3
  43.3 0.5 maximum_select_fusion.4
  43.9 0.5 maximum_select_fusion.5
  44.4 0.1 slice.558
  44.5 0.2 maximum_select_fusion.6
  44.7 0.1 slice.560
  44.9 0.2 maximum_select_fusion.7
  45.2 0.2 maximum_select_fusion.8
  45.5 0.2 fusion.231
  45.6 0.2 maximum_select_fusion.9
  45.9 0.6 fusion.229
  46.4 0.5 slice.569
  46.9 0.1 fusion.230
  47.0 0.9 fusion.28
  48.0 0.1 slice.571
  48.1 0.3 fusion.29
  48.4 0.4 subtract_dynamic-update-slice_fusion.1
  49.2 0.1 constant_dynamic-update-slice_fusion.1
  49.3 0.1 constant_dynamic-update-slice_fusion
  49.4 8.2 %collective-permute-start.3 = (f32[12,3,2048]{2,1,0:T(4,128)S(1)}, f32[12,3,2048]{2,1,0:T(4,128)S(1)}, u32[]{:S(2)}, u32[]{:S(2)}) collective-permute-start(f32[12,3,2048]{2,1,0:T(4,128)S(1)} %slice.599), channel_id=1, source_target_pairs={{8,0},{16,8},{24,16},{1,24},{40,32},{48,40},{56,48},{33,56},{72,64... | collective-permute-start | bytes 884744 | tf_op jit(solution)/shard_map/ppermute | solution.py:308
  57.6 0.1 slice.596
  57.8 2.1 %collective-permute-start.2 = (f32[12,2,2048]{2,1,0:T(2,128)S(1)}, f32[12,2,2048]{2,1,0:T(2,128)S(1)}, u32[]{:S(2)}, u32[]{:S(2)}) collective-permute-start(f32[12,2,2048]{2,1,0:T(2,128)S(1)} %slice.596), channel_id=1, source_target_pairs={{0,8},{8,16},{16,24},{24,1},{32,40},{40,48},{48,56},{56,33},{64,72... | collective-permute-start | bytes 589832 | tf_op jit(solution)/shard_map/ppermute | solution.py:307
  59.9 2.3 %collective-permute-done.2 = f32[12,2,2048]{2,1,0:T(2,128)S(1)} collective-permute-done((f32[12,2,2048]{2,1,0:T(2,128)S(1)}, f32[12,2,2048]{2,1,0:T(2,128)S(1)}, u32[]{:S(2)}, u32[]{:S(2)}) %collective-permute-start.2) | collective-permute-done | bytes 196640 | tf_op jit(solution)/shard_map/ppermute | solution.py:307
  62.3 1.7 %fusion.6 = f32[12,16,2048]{2,1,0:T(8,128)S(1)} fusion(f32[12,2,2048]{2,1,0:T(2,128)S(1)} %collective-permute-done.2, f32[12,16,2048]{2,1,0:T(8,128)S(1)} %constant_dynamic-update-slice_fusion, f32[12,3,2048]{2,1,0:T(4,128)S(1)} %collective-permute-done.3, f32[12,16]{1,0:T(8,128)S(1)} %get-tuple-element.72, f32[12,16]{1,0:T(8,128)S(1)} %get-tuple-element.71, ...), kind=kLoop, calls=%fused_computation.18 | loop fusion | flops 6291456 | bytes 3641856 | tf_op jit(solution)/shard_map/add | solution.py:51
  64.1 0.5 maximum_select_fusion.10
  64.7 0.5 maximum_select_fusion.11
  65.3 0.5 maximum_select_fusion.12
  65.9 0.5 maximum_select_fusion.13
  66.5 0.5 maximum_select_fusion.14
  67.1 0.5 maximum_select_fusion.15
  67.6 0.1 slice.617
  67.7 0.2 maximum_select_fusion.16
  68.0 0.1 slice.619
  68.1 0.2 maximum_select_fusion.17
  68.5 0.2 maximum_select_fusion.18
  68.7 0.2 fusion.228
  68.9 0.2 maximum_select_fusion.19
  69.1 0.6 fusion.226
  69.7 0.5 slice.628
  70.1 0.1 fusion.227
  70.3 0.9 fusion.32
  71.2 0.1 slice.630
  71.3 0.3 fusion.33
  71.6 0.4 subtract_dynamic-update-slice_fusion
  72.4 0.1 constant_dynamic-update-slice_fusion.12
  72.5 0.1 constant_dynamic-update-slice_fusion.11.src_ref
  72.6 1.1 %copy-done.1 = f32[12,16,2048]{2,1,0:T(8,128)} copy-done((f32[12,16,2048]{2,1,0:T(8,128)}, f32[12,16,2048]{2,1,0:T(8,128)S(1)}, u32[]{:S(2)}) %copy-start.1) | copy-done | bytes 1572888
  73.8 30.6 %shard_map.74 = f32[12,64,512]{2,1,0:T(8,128)} custom-call(f32[12,16,2048]{2,1,0:T(8,128)} %copy-done.1, bf16[512,512]{1,0:T(8,128)(2,1)} %get-tuple-element.123.matrix_ref), custom_call_target="tpu_custom_call" | custom-call | tf_op jit(solution)/shard_map/pallas_call | solution.py:236
  104.4 2.7 %copy.482 = f32[12,64,512]{2,1,0:T(8,128)} copy(f32[12,64,512]{2,1,0:T(8,128)} %shard_map.74) | data formatting | bytes 3145728
  (71 shorter events, 2.6 us)
Async XLA Ops:
  1.1 34.7 %copy-start.3 = (f32[2,12,64]{2,0,1:T(2,128)S(1)}, f32[2,12,64]{2,0,1:T(2,128)}, u32[]{:S(2)}) copy-start(f32[2,12,64]{2,0,1:T(2,128)} %param.12) | copy-start | bytes 18436
  1.1 34.8 %copy-start.4 = (s32[2,12,64]{2,0,1:T(2,128)S(1)}, s32[2,12,64]{2,0,1:T(2,128)}, u32[]{:S(2)}) copy-start(s32[2,12,64]{2,0,1:T(2,128)} %param.8) | copy-start | bytes 18436
  1.1 34.8 %copy-start.5 = (s32[2,12,64]{2,0,1:T(2,128)S(1)}, s32[2,12,64]{2,0,1:T(2,128)}, u32[]{:S(2)}) copy-start(s32[2,12,64]{2,0,1:T(2,128)} %param.10) | copy-start | bytes 18436
  1.1 35.0 %copy-start.6 = (f32[2,12,64]{2,0,1:T(2,128)S(1)}, f32[2,12,64]{2,0,1:T(2,128)}, u32[]{:S(2)}) copy-start(f32[2,12,64]{2,0,1:T(2,128)} %param.11) | copy-start | bytes 18436
  1.1 35.1 %copy-start.7 = (f32[2,12,64]{2,0,1:T(2,128)S(1)}, f32[2,12,64]{2,0,1:T(2,128)}, u32[]{:S(2)}) copy-start(f32[2,12,64]{2,0,1:T(2,128)} %param.9) | copy-start | bytes 18436
  1.2 35.2 %copy-start.2 = (f32[12,64]{1,0:T(8,128)S(1)}, f32[12,64]{1,0:T(8,128)}, u32[]{:S(2)}) copy-start(f32[12,64]{1,0:T(8,128)} %param.13) | copy-start | bytes 9220
  27.0 12.1 %copy-start = (f32[12,16,2048]{2,1,0:T(8,128)S(1)}, f32[12,16,2048]{2,1,0:T(8,128)}, u32[]{:S(2)}) copy-start(f32[12,16,2048]{2,1,0:T(8,128)} %shard_map.73) | copy-start | bytes 4718596
  28.3 10.7 %collective-permute-start.1 = (f32[12,3,2048]{2,1,0:T(4,128)S(1)}, f32[12,3,2048]{2,1,0:T(4,128)S(1)}, u32[]{:S(2)}, u32[]{:S(2)}) collective-permute-start(f32[12,3,2048]{2,1,0:T(4,128)S(1)} %slice.435), channel_id=1, source_target_pairs={{8,0},{16,8},{24,16},{1,24},{40,32},{48,40},{56,48},{33,56},{72,64... | collective-permute-start | bytes 884744 | tf_op jit(solution)/shard_map/ppermute | solution.py:308
  31.8 7.3 %collective-permute-start = (f32[12,2,2048]{2,1,0:T(2,128)S(1)}, f32[12,2,2048]{2,1,0:T(2,128)S(1)}, u32[]{:S(2)}, u32[]{:S(2)}) collective-permute-start(f32[12,2,2048]{2,1,0:T(2,128)S(1)} %slice.432), channel_id=1, source_target_pairs={{0,8},{8,16},{16,24},{24,1},{32,40},{40,48},{48,56},{56,33},{64,72... | collective-permute-start | bytes 589832 | tf_op jit(solution)/shard_map/ppermute | solution.py:307
  49.4 12.8 %collective-permute-start.3 = (f32[12,3,2048]{2,1,0:T(4,128)S(1)}, f32[12,3,2048]{2,1,0:T(4,128)S(1)}, u32[]{:S(2)}, u32[]{:S(2)}) collective-permute-start(f32[12,3,2048]{2,1,0:T(4,128)S(1)} %slice.599), channel_id=1, source_target_pairs={{8,0},{16,8},{24,16},{1,24},{40,32},{48,40},{56,48},{33,56},{72,64... | collective-permute-start | bytes 884744 | tf_op jit(solution)/shard_map/ppermute | solution.py:308
  57.8 4.5 %collective-permute-start.2 = (f32[12,2,2048]{2,1,0:T(2,128)S(1)}, f32[12,2,2048]{2,1,0:T(2,128)S(1)}, u32[]{:S(2)}, u32[]{:S(2)}) collective-permute-start(f32[12,2,2048]{2,1,0:T(2,128)S(1)} %slice.596), channel_id=1, source_target_pairs={{0,8},{8,16},{16,24},{24,1},{32,40},{40,48},{48,56},{56,33},{64,72... | collective-permute-start | bytes 589832 | tf_op jit(solution)/shard_map/ppermute | solution.py:307
  72.6 1.1 %copy-start.1 = (f32[12,16,2048]{2,1,0:T(8,128)}, f32[12,16,2048]{2,1,0:T(8,128)S(1)}, u32[]{:S(2)}) copy-start(f32[12,16,2048]{2,1,0:T(8,128)S(1)} %constant_dynamic-update-slice_fusion.11.src_ref) | copy-start | bytes 4718596

commit v6 on v5

--- a/solution.py
+++ b/solution.py
@@ -146,13 +146,39 @@
     return barrier
 
 
-def entry_kernel(x_ref, matrix_ref, dst_ref, moved, send_sem, recv_sem, local_sem, *, src_at, dst_at):
+def neighbours(parts):
+    lon = lax.axis_index("lon")
+    lat = lax.axis_index("lat")
+    bands = lax.axis_size("lat")
+    quarter = lon % parts
+    inside_up = quarter < parts - 1
+    inside_down = quarter > 0
+    has_up = jnp.logical_or(inside_up, lat < bands - 1)
+    has_down = jnp.logical_or(inside_down, lat > 0)
+    up = (jnp.where(inside_up, lon + 1, lon + 1 - parts), jnp.where(inside_up, lat, lat + 1))
+    down = (jnp.where(inside_down, lon - 1, lon + parts - 1), jnp.where(inside_down, lat, lat - 1))
+    return has_up, up, has_down, down
+
+
+def entry_kernel(x_ref, matrix_ref, field_ref, below_ref, above_ref, moved, landed, top_stage, bottom_stage,
+                 send_sem, recv_sem, local_sem, halo_send, halo_recv, *, src_at, dst_at, parts):
     count = lax.axis_size("lon")
     me = lax.axis_index("lon")
     lat = lax.axis_index("lat")
     levels = x_ref.shape[0]
+    rows = landed.shape[1]
     per = levels // CHUNKS
+    has_up, up, has_down, down = neighbours(parts)
     barrier = greet(count, me, lat)
+
+    @pl.when(has_up)
+    def _():
+        pl.semaphore_signal(barrier, 1, device_id=up, device_id_type=MESH_ID)
+
+    @pl.when(has_down)
+    def _():
+        pl.semaphore_signal(barrier, 1, device_id=down, device_id_type=MESH_ID)
+
     copies = []
     locals_ = []
     for chunk in range(CHUNKS):
@@ -162,13 +188,13 @@
 
         lax.fori_loop(chunk * per, (chunk + 1) * per, body, 0)
         if chunk == 0:
-            pl.semaphore_wait(barrier, count - 1)
+            pl.semaphore_wait(barrier, count - 1 + has_up.astype(jnp.int32) + has_down.astype(jnp.int32))
         part = pl.ds(chunk * per, per)
         for offset in range(1, count):
             peer = lax.rem(me + offset, count)
             copy = pltpu.make_async_remote_copy(
                 src_ref=src_at(moved, peer, part),
-                dst_ref=dst_at(dst_ref, me, part),
+                dst_ref=dst_at(landed, me, part),
                 send_sem=send_sem.at[chunk, offset],
                 recv_sem=recv_sem.at[chunk, offset],
                 device_id=(peer, lat),
@@ -176,15 +202,54 @@
             )
             copy.start()
             copies.append(copy)
-        local = pltpu.make_async_copy(src_at(moved, me, part), dst_at(dst_ref, me, part), local_sem.at[chunk])
+        local = pltpu.make_async_copy(src_at(moved, me, part), dst_at(landed, me, part), local_sem.at[chunk])
         local.start()
         locals_.append(local)
-    for copy in copies:
-        copy.wait_send()
     for copy in copies:
         copy.wait_recv()
     for local in locals_:
         local.wait()
+    top_stage[...] = landed[:, rows - top_stage.shape[1] :, :]
+    bottom_stage[...] = landed[:, : bottom_stage.shape[1], :]
+    to_up = pltpu.make_async_remote_copy(
+        src_ref=top_stage, dst_ref=below_ref, send_sem=halo_send.at[0], recv_sem=halo_recv.at[0],
+        device_id=up, device_id_type=MESH_ID,
+    )
+    to_down = pltpu.make_async_remote_copy(
+        src_ref=bottom_stage, dst_ref=above_ref, send_sem=halo_send.at[1], recv_sem=halo_recv.at[1],
+        device_id=down, device_id_type=MESH_ID,
+    )
+
+    @pl.when(has_up)
+    def _():
+        to_up.start()
+
+    @pl.when(has_down)
+    def _():
+        to_down.start()
+
+    field_ref[...] = landed[...]
+
+    @pl.when(jnp.logical_not(has_down))
+    def _():
+        below_ref[...] = jnp.zeros(below_ref.shape, below_ref.dtype)
+
+    @pl.when(jnp.logical_not(has_up))
+    def _():
+        above_ref[...] = jnp.zeros(above_ref.shape, above_ref.dtype)
+
+    for copy in copies:
+        copy.wait_send()
+
+    @pl.when(has_up)
+    def _():
+        to_up.wait_send()
+        to_down.wait_recv()
+
+    @pl.when(has_down)
+    def _():
+        to_down.wait_send()
+        to_up.wait_recv()
 
 
 def exit_kernel(src_ref, matrix_ref, out_ref, landed, send_sem, recv_sem, local_sem, *, src_at, dst_at):
@@ -262,11 +327,28 @@
     def dst_at(ref, sender, part):
         return ref.at[part, :, pl.ds(sender * lane, lane)]
 
-    return run_exchange(
-        entry_kernel, block, permutation(pair_order(cells), False), (levels, count, devices * lane),
-        pl.BlockSpec(memory_space=pltpu.VMEM), pl.BlockSpec(memory_space=pl.ANY), block.shape,
-        src_at, dst_at, 0,
-    )
+    vmem = pl.BlockSpec(memory_space=pltpu.VMEM)
+    field_shape = (levels, count, devices * lane)
+    below_shape = (levels, 2, devices * lane)
+    above_shape = (levels, 3, devices * lane)
+    return pl.pallas_call(
+        functools.partial(entry_kernel, src_at=src_at, dst_at=dst_at, parts=parts),
+        out_shape=tuple(jax.ShapeDtypeStruct(shape, block.dtype) for shape in (field_shape, below_shape, above_shape)),
+        in_specs=[vmem, vmem],
+        out_specs=(vmem, vmem, vmem),
+        scratch_shapes=[
+            pltpu.VMEM(block.shape, block.dtype),
+            pltpu.VMEM(field_shape, block.dtype),
+            pltpu.VMEM(below_shape, block.dtype),
+            pltpu.VMEM(above_shape, block.dtype),
+            pltpu.SemaphoreType.DMA((CHUNKS, devices)),
+            pltpu.SemaphoreType.DMA((CHUNKS, devices)),
+            pltpu.SemaphoreType.DMA((CHUNKS,)),
+            pltpu.SemaphoreType.DMA((2,)),
+            pltpu.SemaphoreType.DMA((2,)),
+        ],
+        compiler_params=pltpu.CompilerParams(collective_id=0, has_side_effects=True),
+    )(block, permutation(pair_order(cells), False))
 
 
 def from_columns(field, rows):
@@ -336,14 +418,17 @@
 
 def per_device(tracers, lon_shift, lon_frac, lat_shift, lat_frac, remap_frac, diffusivity):
     rows = tracers.shape[1]
-    field = to_columns(tracers)
+    field, below, above = to_columns(tracers)
     count = field.shape[1]
     width = field.shape[2]
     lon_shift, lon_frac, lat_shift, lat_frac, remap_frac, diffusivity = (
         own_rows(v, count) for v in (lon_shift, lon_frac, lat_shift, lat_frac, remap_frac, diffusivity)
     )
     for time_step in range(STEPS):
-        padded = lat_halo(field, 3)
+        if time_step == 0:
+            padded = jnp.concatenate([below[:, :1], below, field, above], axis=1)
+        else:
+            padded = lat_halo(field, 3)
         field = lat_step(padded, lat_shift[time_step], lat_frac[time_step], count)
         amount = jnp.remainder(lon_shift[time_step], width // PAIR)
         field = lon_cubic(roll_rows(field, amount), lon_frac[time_step])

time: 107 us -> 106 us (level)
  starting transfers between devices: 16.5 us -> 4.51 us
  Pallas kernels: 56.5 us -> 63.2 us
  other arithmetic: 16.9 us -> 19.3 us
  waiting for transfers between devices: 4.81 us -> 6.35 us
    pallas_call x0 -> x1, Pallas kernels: none -> 34.9 us  [to_columns(): pl.pallas_call(functools.partial(entry_kernel, src_at=src_at, dst_at=dst_...]
    pallas_call x2 -> x1, Pallas kernels: 56.5 us -> 28.4 us  [run_exchange(): pl.pallas_call(functools.partial(kernel, src_at=src_at, dst_at=dst_at), o...]
    ppermute x2 -> x1, starting transfers between devices: 10.3 us -> 2.59 us  [lat_halo(): above = lax.ppermute(field[:, :width], ('lon', 'lat'), down)]
    ppermute x2 -> x1, waiting for transfers between devices: 0.01 us -> 6.35 us  [lat_halo(): above = lax.ppermute(field[:, :width], ('lon', 'lat'), down)]
    ppermute x2 -> x1, waiting for transfers between devices: 4.81 us -> 0.01 us  [lat_halo(): below = lax.ppermute(field[:, rows - width + 1:], ('lon', 'lat'), up)]
    ppermute x2 -> x1, starting transfers between devices: 6.13 us -> 1.92 us  [lat_halo(): below = lax.ppermute(field[:, rows - width + 1:], ('lon', 'lat'), up)]
    add x2, other arithmetic: 3.41 us -> 5.79 us  [lat_step(): summed = addend if summed is None else summed + addend]
    unnamed x27 -> x30, local copies, waits for them, and re-layouts: 3.95 us -> 6.09 us
  transfers between devices with their start and end apart: 4 -> 2, of which waited for: 2 -> 1; matrix products, arithmetic and copies ran while one was open for 2% -> 0% of each run, Pallas kernels for 0% -> 0%
where the time goes in v6:
time: 106 us
  Pallas kernels  63.2 us (60%)
  other arithmetic  19.3 us (18%)
  local copies, waits for them, and re-layouts  11.3 us (11%)
  waiting for transfers between devices  6.35 us (6%)
  starting transfers between devices  4.51 us (4%)
    pallas_call x1, Pallas kernels, to_columns(): pl.pallas_call(functools.partial(entry_kernel, src_at=src_at, dst_at=dst_...  34.9 us
    pallas_call x1, Pallas kernels, run_exchange(): pl.pallas_call(functools.partial(kernel, src_at=src_at, dst_at=dst_at), o...  28.4 us
    select_n x20, other arithmetic, roll_rows(): current = jnp.where(bit_mask(amount, position), moved, current)  7.74 us
    ppermute x1, waiting for transfers between devices, lat_halo(): above = lax.ppermute(field[:, :width], ('lon', 'lat'), down)  6.35 us
    unnamed x30, local copies, waits for them, and re-layouts  6.09 us
    add x2, other arithmetic, lat_step(): summed = addend if summed is None else summed + addend  5.79 us
    ppermute x1, starting transfers between devices, lat_halo(): above = lax.ppermute(field[:, :width], ('lon', 'lat'), down)  2.59 us
    slice x8, local copies, waits for them, and re-layouts, lon_cubic(): taps = [jnp.roll(shifted, PAIR * (1 - p), axis=2) for p in range(4)]  2.29 us
  transfers between devices with their start and end apart: 2, of which 1 were waited for; matrix products, arithmetic and copies ran while one was open for 0% of the time, Pallas kernels for 0%

profile of v6, /device:TPU:25, one launch (start us, length us, event | category | flops | bytes accessed | tf_op | source)
XLA Modules:
  0.0 105.5 jit_solution(3412699777410412171)
XLA Ops:
  0.0 1.1 %fusion.30 = (bf16[512,512]{1,0:T(8,128)(2,1)}, bf16[512,512]{1,0:T(8,128)(2,1)}) fusion(s32[512]{0:T(512)S(1)} %fusion.204), kind=kLoop, calls=%fused_computation.74 | loop fusion | flops 1048576 | bytes 1050624 | tf_op jit(solution)/shard_map/convert_element_type | solution.py:124
  1.1 34.9 %shard_map.73 = (f32[12,16,2048]{2,1,0:T(8,128)}, f32[12,2,2048]{2,1,0:T(2,128)}, f32[12,3,2048]{2,1,0:T(4,128)}) custom-call(f32[12,64,512]{2,1,0:T(8,128)} %x_ref.1, bf16[512,512]{1,0:T(8,128)(2,1)} %get-tuple-element.130.matrix_ref), custom_call_target="tpu_custom_call" | custom-call | tf_op jit(solution)/shard_map/pallas_call | solution.py:334
  36.1 1.6 %constant_dynamic-update-slice_fusion.1 = f32[12,19,2048]{2,1,0:T(8,128)S(1)} fusion(f32[12,16,2048]{2,1,0:T(8,128)} %get-tuple-element.9), kind=kLoop, calls=%fused_computation.144 | loop fusion | bytes 3145728
  37.7 0.1 constant_dynamic-update-slice_fusion
  37.9 0.1 constant_dynamic-slice_fusion
  38.0 0.1 constant_dynamic-slice_fusion.1
  38.2 4.1 %fusion.13 = f32[12,16,2048]{2,1,0:T(8,128)S(1)} fusion(f32[12,2,2048]{2,1,0:T(2,128)S(1)} %copy-done.2, f32[12,16,2048]{2,1,0:T(8,128)} %get-tuple-element.9, f32[12,19,2048]{2,1,0:T(8,128)S(1)} %constant_dynamic-update-slice_fusion, f32[12,16]{1,0:T(8,128)S(1)} %get-tuple-element.88, f32[12,16]{1,0:T(8,128)S(1)} %get-tuple-element.87, ...), kind=kLoop, calls=%fused_computation.21 | loop fusion | flops 5111808 | bytes 8065536 | tf_op jit(solution)/shard_map/add | solution.py:51
  42.3 0.1 fusion.112
  42.4 0.5 maximum_select_fusion
  43.0 0.5 maximum_select_fusion.1
  43.5 0.1 slice.540
  43.6 0.5 maximum_select_fusion.2
  44.2 0.5 maximum_select_fusion.3
  44.8 0.5 maximum_select_fusion.4
  45.4 0.5 maximum_select_fusion.5
  45.9 0.1 slice.549
  46.0 0.2 maximum_select_fusion.6
  46.3 0.1 slice.551
  46.4 0.2 maximum_select_fusion.7
  46.8 0.2 maximum_select_fusion.8
  47.0 0.2 fusion.226
  47.1 0.2 maximum_select_fusion.9
  47.4 0.6 fusion.224
  48.0 0.1 fusion.225
  48.1 0.5 slice.560
  48.6 0.9 fusion.23
  49.5 0.1 slice.562
  49.6 0.6 copy-done.4
  50.2 0.1 constant_dynamic-slice_fusion.3
  50.5 0.3 fusion.24
  50.8 0.4 subtract_dynamic-update-slice_fusion.1
  51.6 0.1 constant_dynamic-update-slice_fusion.3
  51.7 0.1 constant_dynamic-update-slice_fusion.2
  51.8 0.1 slice.587
  51.9 1.9 %collective-permute-start = (f32[12,2,2048]{2,1,0:T(2,128)S(1)}, f32[12,2,2048]{2,1,0:T(2,128)S(1)}, u32[]{:S(2)}, u32[]{:S(2)}) collective-permute-start(f32[12,2,2048]{2,1,0:T(2,128)S(1)} %slice.587), channel_id=1, source_target_pairs={{0,8},{8,16},{16,24},{24,1},{32,40},{40,48},{48,56},{56,33},{64,72... | collective-permute-start | bytes 589832 | tf_op jit(solution)/shard_map/ppermute | solution.py:389
  53.9 2.6 %collective-permute-start.1 = (f32[12,3,2048]{2,1,0:T(4,128)S(1)}, f32[12,3,2048]{2,1,0:T(4,128)S(1)}, u32[]{:S(2)}, u32[]{:S(2)}) collective-permute-start(f32[12,3,2048]{2,1,0:T(4,128)S(1)} %slice.590), channel_id=1, source_target_pairs={{8,0},{16,8},{24,16},{1,24},{40,32},{48,40},{56,48},{33,56},{72,64... | collective-permute-start | bytes 884744 | tf_op jit(solution)/shard_map/ppermute | solution.py:390
  56.6 0.1 fusion.84
  56.7 6.4 %collective-permute-done.1 = f32[12,3,2048]{2,1,0:T(4,128)S(1)} collective-permute-done((f32[12,3,2048]{2,1,0:T(4,128)S(1)}, f32[12,3,2048]{2,1,0:T(4,128)S(1)}, u32[]{:S(2)}, u32[]{:S(2)}) %collective-permute-start.1) | collective-permute-done | bytes 294944 | tf_op jit(solution)/shard_map/ppermute | solution.py:390
  63.0 1.7 %fusion.6 = f32[12,16,2048]{2,1,0:T(8,128)S(1)} fusion(f32[12,2,2048]{2,1,0:T(2,128)S(1)} %collective-permute-done, f32[12,16,2048]{2,1,0:T(8,128)S(1)} %constant_dynamic-update-slice_fusion.2, f32[12,3,2048]{2,1,0:T(4,128)S(1)} %collective-permute-done.1, f32[12,16]{1,0:T(8,128)S(1)} %get-tuple-element.78, f32[12,16]{1,0:T(8,128)S(1)} %get-tuple-element.77, ...), kind=kLoop, calls=%fused_computation.14 | loop fusion | flops 6291456 | bytes 3641856 | tf_op jit(solution)/shard_map/add | solution.py:51
  64.8 0.5 maximum_select_fusion.10
  65.5 0.5 maximum_select_fusion.11
  66.0 0.5 maximum_select_fusion.12
  66.6 0.5 maximum_select_fusion.13
  67.2 0.5 maximum_select_fusion.14
  67.8 0.5 maximum_select_fusion.15
  68.4 0.1 slice.608
  68.5 0.2 maximum_select_fusion.16
  68.7 0.1 slice.610
  68.9 0.2 maximum_select_fusion.17
  69.2 0.2 maximum_select_fusion.18
  69.4 0.2 fusion.223
  69.6 0.2 maximum_select_fusion.19
  69.8 0.6 fusion.221
  70.4 0.1 fusion.222
  70.5 0.5 slice.619
  71.0 0.9 fusion.27
  72.0 0.1 slice.621
  72.1 0.3 fusion.28
  72.3 0.4 subtract_dynamic-update-slice_fusion
  73.2 0.1 constant_dynamic-update-slice_fusion.14
  73.3 0.1 constant_dynamic-update-slice_fusion.13.src_ref
  73.4 1.1 %copy-done = f32[12,16,2048]{2,1,0:T(8,128)} copy-done((f32[12,16,2048]{2,1,0:T(8,128)}, f32[12,16,2048]{2,1,0:T(8,128)S(1)}, u32[]{:S(2)}) %copy-start) | copy-done | bytes 1572888
  74.5 28.4 %shard_map.74 = f32[12,64,512]{2,1,0:T(8,128)} custom-call(f32[12,16,2048]{2,1,0:T(8,128)} %copy-done, bf16[512,512]{1,0:T(8,128)(2,1)} %get-tuple-element.129.matrix_ref), custom_call_target="tpu_custom_call" | custom-call | tf_op jit(solution)/shard_map/pallas_call | solution.py:301
  102.9 2.7 %copy.483 = f32[12,64,512]{2,1,0:T(8,128)} copy(f32[12,64,512]{2,1,0:T(8,128)} %shard_map.74) | data formatting | bytes 3145728
  (69 shorter events, 2.4 us)
Async XLA Ops:
  36.0 1.6 %copy-start.1 = (f32[12,3,2048]{2,1,0:T(4,128)S(1)}, f32[12,3,2048]{2,1,0:T(4,128)}, u32[]{:S(2)}) copy-start(f32[12,3,2048]{2,1,0:T(4,128)} %get-tuple-element.10) | copy-start | bytes 884740
  36.1 1.8 %copy-start.5 = (s32[2,12,64]{2,0,1:T(2,128)S(1)}, s32[2,12,64]{2,0,1:T(2,128)}, u32[]{:S(2)}) copy-start(s32[2,12,64]{2,0,1:T(2,128)} %param.8) | copy-start | bytes 18436
  36.1 1.8 %copy-start.6 = (s32[2,12,64]{2,0,1:T(2,128)S(1)}, s32[2,12,64]{2,0,1:T(2,128)}, u32[]{:S(2)}) copy-start(s32[2,12,64]{2,0,1:T(2,128)} %param.10) | copy-start | bytes 18436
  36.1 1.9 %copy-start.7 = (f32[2,12,64]{2,0,1:T(2,128)S(1)}, f32[2,12,64]{2,0,1:T(2,128)}, u32[]{:S(2)}) copy-start(f32[2,12,64]{2,0,1:T(2,128)} %param.11) | copy-start | bytes 18436
  36.1 1.9 %copy-start.8 = (f32[2,12,64]{2,0,1:T(2,128)S(1)}, f32[2,12,64]{2,0,1:T(2,128)}, u32[]{:S(2)}) copy-start(f32[2,12,64]{2,0,1:T(2,128)} %param.9) | copy-start | bytes 18436
  36.1 2.0 %copy-start.2 = (f32[12,2,2048]{2,1,0:T(2,128)S(1)}, f32[12,2,2048]{2,1,0:T(2,128)}, u32[]{:S(2)}) copy-start(f32[12,2,2048]{2,1,0:T(2,128)} %get-tuple-element.8) | copy-start | bytes 589828
  49.5 0.7 copy-start.4
  49.5 0.8 copy-start.3
  51.9 4.7 %collective-permute-start = (f32[12,2,2048]{2,1,0:T(2,128)S(1)}, f32[12,2,2048]{2,1,0:T(2,128)S(1)}, u32[]{:S(2)}, u32[]{:S(2)}) collective-permute-start(f32[12,2,2048]{2,1,0:T(2,128)S(1)} %slice.587), channel_id=1, source_target_pairs={{0,8},{8,16},{16,24},{24,1},{32,40},{40,48},{48,56},{56,33},{64,72... | collective-permute-start | bytes 589832 | tf_op jit(solution)/shard_map/ppermute | solution.py:389
  53.9 9.1 %collective-permute-start.1 = (f32[12,3,2048]{2,1,0:T(4,128)S(1)}, f32[12,3,2048]{2,1,0:T(4,128)S(1)}, u32[]{:S(2)}, u32[]{:S(2)}) collective-permute-start(f32[12,3,2048]{2,1,0:T(4,128)S(1)} %slice.590), channel_id=1, source_target_pairs={{8,0},{16,8},{24,16},{1,24},{40,32},{48,40},{56,48},{33,56},{72,64... | collective-permute-start | bytes 884744 | tf_op jit(solution)/shard_map/ppermute | solution.py:390
  73.4 1.1 %copy-start = (f32[12,16,2048]{2,1,0:T(8,128)}, f32[12,16,2048]{2,1,0:T(8,128)S(1)}, u32[]{:S(2)}) copy-start(f32[12,16,2048]{2,1,0:T(8,128)S(1)} %constant_dynamic-update-slice_fusion.13.src_ref) | copy-start | bytes 4718596

commit v7 on v6

--- a/solution.py
+++ b/solution.py
@@ -160,7 +160,7 @@
     return has_up, up, has_down, down
 
 
-def entry_kernel(x_ref, matrix_ref, field_ref, below_ref, above_ref, moved, landed, top_stage, bottom_stage,
+def entry_kernel(x_ref, matrix_ref, padded_ref, moved, landed, top_stage, bottom_stage, below_ref, above_ref,
                  send_sem, recv_sem, local_sem, halo_send, halo_recv, *, src_at, dst_at, parts):
     count = lax.axis_size("lon")
     me = lax.axis_index("lon")
@@ -228,15 +228,9 @@
     def _():
         to_down.start()
 
-    field_ref[...] = landed[...]
-
-    @pl.when(jnp.logical_not(has_down))
-    def _():
-        below_ref[...] = jnp.zeros(below_ref.shape, below_ref.dtype)
-
-    @pl.when(jnp.logical_not(has_up))
-    def _():
-        above_ref[...] = jnp.zeros(above_ref.shape, above_ref.dtype)
+    low = below_ref.shape[1] + 1
+    padded_ref[:, low : low + rows, :] = landed[...]
+    padded_ref[:, :1, :] = jnp.zeros((levels, 1, landed.shape[2]), landed.dtype)
 
     for copy in copies:
         copy.wait_send()
@@ -245,11 +239,21 @@
     def _():
         to_up.wait_send()
         to_down.wait_recv()
+        padded_ref[:, low + rows :, :] = above_ref[...]
+
+    @pl.when(jnp.logical_not(has_up))
+    def _():
+        padded_ref[:, low + rows :, :] = jnp.zeros(above_ref.shape, above_ref.dtype)
 
     @pl.when(has_down)
     def _():
         to_down.wait_send()
         to_up.wait_recv()
+        padded_ref[:, 1:low, :] = below_ref[...]
+
+    @pl.when(jnp.logical_not(has_down))
+    def _():
+        padded_ref[:, 1:low, :] = jnp.zeros(below_ref.shape, below_ref.dtype)
 
 
 def exit_kernel(src_ref, matrix_ref, out_ref, landed, send_sem, recv_sem, local_sem, *, src_at, dst_at):
@@ -331,14 +335,17 @@
     field_shape = (levels, count, devices * lane)
     below_shape = (levels, 2, devices * lane)
     above_shape = (levels, 3, devices * lane)
+    padded_shape = (levels, count + 6, devices * lane)
     return pl.pallas_call(
         functools.partial(entry_kernel, src_at=src_at, dst_at=dst_at, parts=parts),
-        out_shape=tuple(jax.ShapeDtypeStruct(shape, block.dtype) for shape in (field_shape, below_shape, above_shape)),
+        out_shape=jax.ShapeDtypeStruct(padded_shape, block.dtype),
         in_specs=[vmem, vmem],
-        out_specs=(vmem, vmem, vmem),
+        out_specs=vmem,
         scratch_shapes=[
             pltpu.VMEM(block.shape, block.dtype),
             pltpu.VMEM(field_shape, block.dtype),
+            pltpu.VMEM(below_shape, block.dtype),
+            pltpu.VMEM(above_shape, block.dtype),
             pltpu.VMEM(below_shape, block.dtype),
             pltpu.VMEM(above_shape, block.dtype),
             pltpu.SemaphoreType.DMA((CHUNKS, devices)),
@@ -418,15 +425,15 @@
 
 def per_device(tracers, lon_shift, lon_frac, lat_shift, lat_frac, remap_frac, diffusivity):
     rows = tracers.shape[1]
-    field, below, above = to_columns(tracers)
-    count = field.shape[1]
-    width = field.shape[2]
+    first = to_columns(tracers)
+    count = first.shape[1] - 6
+    width = first.shape[2]
     lon_shift, lon_frac, lat_shift, lat_frac, remap_frac, diffusivity = (
         own_rows(v, count) for v in (lon_shift, lon_frac, lat_shift, lat_frac, remap_frac, diffusivity)
     )
     for time_step in range(STEPS):
         if time_step == 0:
-            padded = jnp.concatenate([below[:, :1], below, field, above], axis=1)
+            padded = first
         else:
             padded = lat_halo(field, 3)
         field = lat_step(padded, lat_shift[time_step], lat_frac[time_step], count)

time: 106 us -> 110 us (1.038)
  other arithmetic: 19.3 us -> 23.6 us
  waiting for transfers between devices: 6.35 us -> 3.05 us
  Pallas kernels: 63.2 us -> 65.6 us
  starting transfers between devices: 4.51 us -> 5.78 us
    ppermute x1, waiting for transfers between devices: 6.35 us -> 0.82 us  [lat_halo(): above = lax.ppermute(field[:, :width], ('lon', 'lat'), down)]
    add x2, other arithmetic: 5.79 us -> 8.85 us  [lat_step(): summed = addend if summed is None else summed + addend]
    ppermute x1, waiting for transfers between devices: 0.01 us -> 2.23 us  [lat_halo(): below = lax.ppermute(field[:, rows - width + 1:], ('lon', 'lat'), up)]
    pallas_call x1, Pallas kernels: 28.4 us -> 30.2 us  [run_exchange(): pl.pallas_call(functools.partial(kernel, src_at=src_at, dst_at=dst_at), o...]
    ppermute x1, starting transfers between devices: 1.92 us -> 3.55 us  [lat_halo(): below = lax.ppermute(field[:, rows - width + 1:], ('lon', 'lat'), up)]
    unnamed x30 -> x19, local copies, waits for them, and re-layouts: 6.09 us -> 4.5 us
    select_n x20, other arithmetic: 7.74 us -> 8.98 us  [roll_rows(): current = jnp.where(bit_mask(amount, position), moved, current)]
  transfers between devices with their start and end apart: 2 -> 2, of which waited for: 1 -> 2; matrix products, arithmetic and copies ran while one was open for 0% -> 0% of each run, Pallas kernels for 0% -> 0%
where the time goes in v7:
time: 110 us
  Pallas kernels  65.6 us (60%)
  other arithmetic  23.6 us (21%)
  local copies, waits for them, and re-layouts  11.1 us (10%)
  starting transfers between devices  5.78 us (5%)
  waiting for transfers between devices  3.05 us (3%)
    pallas_call x1, Pallas kernels, to_columns(): pl.pallas_call(functools.partial(entry_kernel, src_at=src_at, dst_at=dst_...  35.3 us
    pallas_call x1, Pallas kernels, run_exchange(): pl.pallas_call(functools.partial(kernel, src_at=src_at, dst_at=dst_at), o...  30.2 us
    select_n x20, other arithmetic, roll_rows(): current = jnp.where(bit_mask(amount, position), moved, current)  8.98 us
    add x2, other arithmetic, lat_step(): summed = addend if summed is None else summed + addend  8.85 us
    unnamed x19, local copies, waits for them, and re-layouts  4.5 us
    ppermute x1, starting transfers between devices, lat_halo(): below = lax.ppermute(field[:, rows - width + 1:], ('lon', 'lat'), up)  3.55 us
    slice x8, local copies, waits for them, and re-layouts, lon_cubic(): taps = [jnp.roll(shifted, PAIR * (1 - p), axis=2) for p in range(4)]  2.29 us
    ppermute x1, waiting for transfers between devices, lat_halo(): below = lax.ppermute(field[:, rows - width + 1:], ('lon', 'lat'), up)  2.23 us
  transfers between devices with their start and end apart: 2, of which 2 were waited for; matrix products, arithmetic and copies ran while one was open for 0% of the time, Pallas kernels for 0%

profile of v7, /device:TPU:25, one launch (start us, length us, event | category | flops | bytes accessed | tf_op | source)
XLA Modules:
  0.0 109.9 jit_solution(2541433605442277467)
XLA Ops:
  0.0 1.1 %fusion.22 = (bf16[512,512]{1,0:T(8,128)(2,1)}, bf16[512,512]{1,0:T(8,128)(2,1)}) fusion(s32[512]{0:T(512)S(1)} %fusion.196), kind=kLoop, calls=%fused_computation.61 | loop fusion | flops 1048576 | bytes 1050624 | tf_op jit(solution)/shard_map/convert_element_type | solution.py:124
  1.2 0.9 constant_dynamic-slice_fusion
  2.1 0.9 constant_dynamic-slice_fusion.1
  3.0 35.3 %shard_map.73 = f32[12,22,2048]{2,1,0:T(8,128)} custom-call(f32[12,64,512]{2,1,0:T(8,128)} %x_ref.1, bf16[512,512]{1,0:T(8,128)(2,1)} %get-tuple-element.124.matrix_ref), custom_call_target="tpu_custom_call" | custom-call | tf_op jit(solution)/shard_map/pallas_call | solution.py:339
  38.4 7.1 %multiply_add_fusion = f32[12,16,2048]{2,1,0:T(8,128)S(1)} fusion(f32[12,22,2048]{2,1,0:T(8,128)} %shard_map.73, f32[12,16]{1,0:T(8,128)S(1)} %get-tuple-element.82, f32[12,16]{1,0:T(8,128)S(1)} %get-tuple-element.81, f32[12,16]{1,0:T(8,128)S(1)} %get-tuple-element.80, f32[12,16]{1,0:T(8,128)S(1)} %get-tuple-element.79, f32[12,16]{1,0:T(8,128)S(1)} %get-tuple-element.78, ...), kind=kLoop, calls=%fused_computation.57 | loop fusion | flops 4325376 | bytes 11014656 | tf_op jit(solution)/shard_map/add | solution.py:51
  45.6 0.1 fusion.104
  45.7 1.7 %maximum_select_fusion = f32[12,16,2048]{2,1,0:T(8,128)S(1)} fusion(f32[12,16,2046]{2,1,0:T(8,128)S(1)} %bitcast.558, f32[12,16,2]{2,1,0:T(8,128)S(1)} %slice.529, pred[12,16]{1,0:T(8,128)(4,1)S(1)} %get-tuple-element.120, f32[12,22,2048]{2,1,0:T(8,128)S(1)} %copy-done, f32[12,16]{1,0:T(8,128)S(1)} %get-tuple-element.82, f32[12,16]{1,0:T(8,128)S(1)} %get-tuple-element.81, ...), kind=kLoop, calls=%fused_computation.21 | loop fusion | flops 5111808 | bytes 12587712 | tf_op jit(solution)/shard_map/jit(_where)/select_n | solution.py:406
  47.5 0.5 maximum_select_fusion.1
  48.0 0.1 slice.533
  48.1 0.5 maximum_select_fusion.2
  48.7 0.5 maximum_select_fusion.3
  49.2 0.1 slice.537
  49.3 0.5 maximum_select_fusion.4
  49.9 0.5 maximum_select_fusion.5
  50.4 0.1 slice.542
  50.5 0.2 maximum_select_fusion.6
  50.8 0.1 slice.544
  50.9 0.2 maximum_select_fusion.7
  51.3 0.2 maximum_select_fusion.8
  51.5 0.2 fusion.218
  51.7 0.2 maximum_select_fusion.9
  51.9 0.6 fusion.216
  52.5 0.5 slice.553
  52.9 0.1 fusion.217
  53.1 0.9 fusion.15
  54.0 0.1 slice.555
  54.2 0.6 copy-done.3
  54.7 0.1 constant_dynamic-slice_fusion.3
  55.0 0.3 fusion.16
  55.3 0.4 subtract_dynamic-update-slice_fusion.1
  56.1 0.1 constant_dynamic-update-slice_fusion.1
  56.2 0.1 constant_dynamic-update-slice_fusion
  56.4 2.2 %collective-permute-start.1 = (f32[12,3,2048]{2,1,0:T(4,128)S(1)}, f32[12,3,2048]{2,1,0:T(4,128)S(1)}, u32[]{:S(2)}, u32[]{:S(2)}) collective-permute-start(f32[12,3,2048]{2,1,0:T(4,128)S(1)} %slice.583), channel_id=1, source_target_pairs={{8,0},{16,8},{24,16},{1,24},{40,32},{48,40},{56,48},{33,56},{72,64... | collective-permute-start | bytes 884744 | tf_op jit(solution)/shard_map/ppermute | solution.py:397
  58.6 0.1 slice.580
  58.7 3.6 %collective-permute-start = (f32[12,2,2048]{2,1,0:T(2,128)S(1)}, f32[12,2,2048]{2,1,0:T(2,128)S(1)}, u32[]{:S(2)}, u32[]{:S(2)}) collective-permute-start(f32[12,2,2048]{2,1,0:T(2,128)S(1)} %slice.580), channel_id=1, source_target_pairs={{0,8},{8,16},{16,24},{24,1},{32,40},{40,48},{48,56},{56,33},{64,72... | collective-permute-start | bytes 589832 | tf_op jit(solution)/shard_map/ppermute | solution.py:396
  62.4 0.1 fusion.76
  62.4 2.2 %collective-permute-done = f32[12,2,2048]{2,1,0:T(2,128)S(1)} collective-permute-done((f32[12,2,2048]{2,1,0:T(2,128)S(1)}, f32[12,2,2048]{2,1,0:T(2,128)S(1)}, u32[]{:S(2)}, u32[]{:S(2)}) %collective-permute-start) | collective-permute-done | bytes 196640 | tf_op jit(solution)/shard_map/ppermute | solution.py:396
  64.7 0.8 collective-permute-done.1
  65.5 1.7 %fusion.6 = f32[12,16,2048]{2,1,0:T(8,128)S(1)} fusion(f32[12,2,2048]{2,1,0:T(2,128)S(1)} %collective-permute-done, f32[12,16,2048]{2,1,0:T(8,128)S(1)} %constant_dynamic-update-slice_fusion, f32[12,3,2048]{2,1,0:T(4,128)S(1)} %collective-permute-done.1, f32[12,16]{1,0:T(8,128)S(1)} %get-tuple-element.72, f32[12,16]{1,0:T(8,128)S(1)} %get-tuple-element.71, ...), kind=kLoop, calls=%fused_computation.12 | loop fusion | flops 6291456 | bytes 3641856 | tf_op jit(solution)/shard_map/add | solution.py:51
  67.3 0.5 maximum_select_fusion.10
  67.9 0.5 maximum_select_fusion.11
  68.5 0.5 maximum_select_fusion.12
  69.1 0.5 maximum_select_fusion.13
  69.7 0.5 maximum_select_fusion.14
  70.3 0.5 maximum_select_fusion.15
  70.8 0.1 slice.601
  71.0 0.2 maximum_select_fusion.16
  71.2 0.1 slice.603
  71.3 0.2 maximum_select_fusion.17
  71.7 0.2 maximum_select_fusion.18
  71.9 0.2 fusion.215
  72.1 0.2 maximum_select_fusion.19
  72.3 0.6 fusion.213
  72.9 0.5 slice.612
  73.4 0.1 fusion.214
  73.5 0.9 fusion.19
  74.4 0.1 slice.614
  74.5 0.3 fusion.20
  74.8 0.4 subtract_dynamic-update-slice_fusion
  75.6 0.1 constant_dynamic-update-slice_fusion.12
  75.7 0.1 constant_dynamic-update-slice_fusion.11.src_ref
  75.8 1.1 %copy-done.1 = f32[12,16,2048]{2,1,0:T(8,128)} copy-done((f32[12,16,2048]{2,1,0:T(8,128)}, f32[12,16,2048]{2,1,0:T(8,128)S(1)}, u32[]{:S(2)}) %copy-start.1) | copy-done | bytes 1572888
  77.0 30.2 %shard_map.74 = f32[12,64,512]{2,1,0:T(8,128)} custom-call(f32[12,16,2048]{2,1,0:T(8,128)} %copy-done.1, bf16[512,512]{1,0:T(8,128)(2,1)} %get-tuple-element.123.matrix_ref), custom_call_target="tpu_custom_call" | custom-call | tf_op jit(solution)/shard_map/pallas_call | solution.py:305
  107.2 2.7 %copy.482 = f32[12,64,512]{2,1,0:T(8,128)} copy(f32[12,64,512]{2,1,0:T(8,128)} %shard_map.74) | data formatting | bytes 3145728
  (57 shorter events, 2.3 us)
Async XLA Ops:
  38.3 7.3 %copy-start = (f32[12,22,2048]{2,1,0:T(8,128)S(1)}, f32[12,22,2048]{2,1,0:T(8,128)}, u32[]{:S(2)}) copy-start(f32[12,22,2048]{2,1,0:T(8,128)} %shard_map.73) | copy-start | bytes 6488068
  54.0 0.7 copy-start.3
  54.0 0.8 copy-start.2
  56.4 9.1 %collective-permute-start.1 = (f32[12,3,2048]{2,1,0:T(4,128)S(1)}, f32[12,3,2048]{2,1,0:T(4,128)S(1)}, u32[]{:S(2)}, u32[]{:S(2)}) collective-permute-start(f32[12,3,2048]{2,1,0:T(4,128)S(1)} %slice.583), channel_id=1, source_target_pairs={{8,0},{16,8},{24,16},{1,24},{40,32},{48,40},{56,48},{33,56},{72,64... | collective-permute-start | bytes 884744 | tf_op jit(solution)/shard_map/ppermute | solution.py:397
  58.7 5.9 %collective-permute-start = (f32[12,2,2048]{2,1,0:T(2,128)S(1)}, f32[12,2,2048]{2,1,0:T(2,128)S(1)}, u32[]{:S(2)}, u32[]{:S(2)}) collective-permute-start(f32[12,2,2048]{2,1,0:T(2,128)S(1)} %slice.580), channel_id=1, source_target_pairs={{0,8},{8,16},{16,24},{24,1},{32,40},{40,48},{48,56},{56,33},{64,72... | collective-permute-start | bytes 589832 | tf_op jit(solution)/shard_map/ppermute | solution.py:396
  75.8 1.1 %copy-start.1 = (f32[12,16,2048]{2,1,0:T(8,128)}, f32[12,16,2048]{2,1,0:T(8,128)S(1)}, u32[]{:S(2)}) copy-start(f32[12,16,2048]{2,1,0:T(8,128)S(1)} %constant_dynamic-update-slice_fusion.11.src_ref) | copy-start | bytes 4718596

commit v8 on v6

--- a/solution.py
+++ b/solution.py
@@ -161,7 +161,8 @@
 
 
 def entry_kernel(x_ref, matrix_ref, field_ref, below_ref, above_ref, moved, landed, top_stage, bottom_stage,
-                 send_sem, recv_sem, local_sem, halo_send, halo_recv, *, src_at, dst_at, parts):
+                 zero_low, zero_high, send_sem, recv_sem, local_sem, halo_send, halo_recv, store_sem,
+                 *, src_at, dst_at, parts):
     count = lax.axis_size("lon")
     me = lax.axis_index("lon")
     lat = lax.axis_index("lat")
@@ -228,15 +229,24 @@
     def _():
         to_down.start()
 
-    field_ref[...] = landed[...]
+    store = pltpu.make_async_copy(landed, field_ref, store_sem.at[0])
+    store.start()
+    fill_low = pltpu.make_async_copy(zero_low, below_ref, store_sem.at[1])
+    fill_high = pltpu.make_async_copy(zero_high, above_ref, store_sem.at[2])
 
     @pl.when(jnp.logical_not(has_down))
     def _():
-        below_ref[...] = jnp.zeros(below_ref.shape, below_ref.dtype)
+        zero_low[...] = jnp.zeros(zero_low.shape, zero_low.dtype)
+        fill_low.start()
+        fill_low.wait()
 
     @pl.when(jnp.logical_not(has_up))
     def _():
-        above_ref[...] = jnp.zeros(above_ref.shape, above_ref.dtype)
+        zero_high[...] = jnp.zeros(zero_high.shape, zero_high.dtype)
+        fill_high.start()
+        fill_high.wait()
+
+    store.wait()
 
     for copy in copies:
         copy.wait_send()
@@ -328,6 +338,7 @@
         return ref.at[part, :, pl.ds(sender * lane, lane)]
 
     vmem = pl.BlockSpec(memory_space=pltpu.VMEM)
+    hbm = pl.BlockSpec(memory_space=pl.ANY)
     field_shape = (levels, count, devices * lane)
     below_shape = (levels, 2, devices * lane)
     above_shape = (levels, 3, devices * lane)
@@ -335,10 +346,12 @@
         functools.partial(entry_kernel, src_at=src_at, dst_at=dst_at, parts=parts),
         out_shape=tuple(jax.ShapeDtypeStruct(shape, block.dtype) for shape in (field_shape, below_shape, above_shape)),
         in_specs=[vmem, vmem],
-        out_specs=(vmem, vmem, vmem),
+        out_specs=(hbm, hbm, hbm),
         scratch_shapes=[
             pltpu.VMEM(block.shape, block.dtype),
             pltpu.VMEM(field_shape, block.dtype),
+            pltpu.VMEM(below_shape, block.dtype),
+            pltpu.VMEM(above_shape, block.dtype),
             pltpu.VMEM(below_shape, block.dtype),
             pltpu.VMEM(above_shape, block.dtype),
             pltpu.SemaphoreType.DMA((CHUNKS, devices)),
@@ -346,6 +359,7 @@
             pltpu.SemaphoreType.DMA((CHUNKS,)),
             pltpu.SemaphoreType.DMA((2,)),
             pltpu.SemaphoreType.DMA((2,)),
+            pltpu.SemaphoreType.DMA((3,)),
         ],
         compiler_params=pltpu.CompilerParams(collective_id=0, has_side_effects=True),
     )(block, permutation(pair_order(cells), False))

time: 106 us -> 105 us (level)
  Pallas kernels: 63.2 us -> 62 us
    pallas_call x1, Pallas kernels: 34.9 us -> 33.6 us  [to_columns(): pl.pallas_call(functools.partial(entry_kernel, src_at=src_at, dst_at=dst_...]
where the time goes in v8:
time: 105 us; the launch traced here: 104 us
  Pallas kernels  62 us (59%)
  other arithmetic  19.3 us (18%)
  local copies, waits for them, and re-layouts  11.3 us (11%)
  waiting for transfers between devices  6.35 us (6%)
  starting transfers between devices  4.51 us (4%)
    pallas_call x1, Pallas kernels, to_columns(): pl.pallas_call(functools.partial(entry_kernel, src_at=src_at, dst_at=dst_...  33.6 us
    pallas_call x1, Pallas kernels, run_exchange(): pl.pallas_call(functools.partial(kernel, src_at=src_at, dst_at=dst_at), o...  28.4 us
    select_n x20, other arithmetic, roll_rows(): current = jnp.where(bit_mask(amount, position), moved, current)  7.74 us
    ppermute x1, waiting for transfers between devices, lat_halo(): above = lax.ppermute(field[:, :width], ('lon', 'lat'), down)  6.35 us
    unnamed x30, local copies, waits for them, and re-layouts  6.09 us
    add x2, other arithmetic, lat_step(): summed = addend if summed is None else summed + addend  5.79 us
    ppermute x1, starting transfers between devices, lat_halo(): above = lax.ppermute(field[:, :width], ('lon', 'lat'), down)  2.59 us
    slice x8, local copies, waits for them, and re-layouts, lon_cubic(): taps = [jnp.roll(shifted, PAIR * (1 - p), axis=2) for p in range(4)]  2.29 us
  transfers between devices with their start and end apart: 2, of which 1 were waited for; matrix products, arithmetic and copies ran while one was open for 0% of the time, Pallas kernels for 0%

profile of v8, /device:TPU:25, one launch (start us, length us, event | category | flops | bytes accessed | tf_op | source)
XLA Modules:
  0.0 104.3 jit_solution(10420131216486614803)
XLA Ops:
  0.0 1.1 %fusion.30 = (bf16[512,512]{1,0:T(8,128)(2,1)}, bf16[512,512]{1,0:T(8,128)(2,1)}) fusion(s32[512]{0:T(512)S(1)} %fusion.204), kind=kLoop, calls=%fused_computation.74 | loop fusion | flops 1048576 | bytes 1050624 | tf_op jit(solution)/shard_map/convert_element_type | solution.py:124
  1.1 33.6 %shard_map.73 = (f32[12,16,2048]{2,1,0:T(8,128)}, f32[12,2,2048]{2,1,0:T(2,128)}, f32[12,3,2048]{2,1,0:T(4,128)}) custom-call(f32[12,64,512]{2,1,0:T(8,128)} %x_ref.1, bf16[512,512]{1,0:T(8,128)(2,1)} %get-tuple-element.130.matrix_ref), custom_call_target="tpu_custom_call" | custom-call | tf_op jit(solution)/shard_map/pallas_call | solution.py:345
  34.9 1.6 %constant_dynamic-update-slice_fusion.1 = f32[12,19,2048]{2,1,0:T(8,128)S(1)} fusion(f32[12,16,2048]{2,1,0:T(8,128)} %get-tuple-element.9), kind=kLoop, calls=%fused_computation.144 | loop fusion | bytes 3145728
  36.4 0.1 constant_dynamic-update-slice_fusion
  36.6 0.1 constant_dynamic-slice_fusion
  36.7 0.1 constant_dynamic-slice_fusion.1
  36.9 4.1 %fusion.13 = f32[12,16,2048]{2,1,0:T(8,128)S(1)} fusion(f32[12,2,2048]{2,1,0:T(2,128)S(1)} %copy-done.2, f32[12,16,2048]{2,1,0:T(8,128)} %get-tuple-element.9, f32[12,19,2048]{2,1,0:T(8,128)S(1)} %constant_dynamic-update-slice_fusion, f32[12,16]{1,0:T(8,128)S(1)} %get-tuple-element.88, f32[12,16]{1,0:T(8,128)S(1)} %get-tuple-element.87, ...), kind=kLoop, calls=%fused_computation.21 | loop fusion | flops 5111808 | bytes 8065536 | tf_op jit(solution)/shard_map/add | solution.py:51
  41.1 0.1 fusion.112
  41.2 0.5 maximum_select_fusion
  41.8 0.5 maximum_select_fusion.1
  42.3 0.1 slice.540
  42.4 0.5 maximum_select_fusion.2
  43.0 0.5 maximum_select_fusion.3
  43.5 0.5 maximum_select_fusion.4
  44.1 0.5 maximum_select_fusion.5
  44.7 0.1 slice.549
  44.8 0.2 maximum_select_fusion.6
  45.0 0.1 slice.551
  45.2 0.2 maximum_select_fusion.7
  45.5 0.2 maximum_select_fusion.8
  45.7 0.2 fusion.226
  45.9 0.2 maximum_select_fusion.9
  46.1 0.6 fusion.224
  46.7 0.1 fusion.225
  46.8 0.5 slice.560
  47.3 0.9 fusion.23
  48.3 0.1 slice.562
  48.4 0.6 copy-done.4
  49.0 0.1 constant_dynamic-slice_fusion.3
  49.3 0.3 fusion.24
  49.6 0.4 subtract_dynamic-update-slice_fusion.1
  50.4 0.1 constant_dynamic-update-slice_fusion.3
  50.5 0.1 constant_dynamic-update-slice_fusion.2
  50.6 0.1 slice.587
  50.7 1.9 %collective-permute-start = (f32[12,2,2048]{2,1,0:T(2,128)S(1)}, f32[12,2,2048]{2,1,0:T(2,128)S(1)}, u32[]{:S(2)}, u32[]{:S(2)}) collective-permute-start(f32[12,2,2048]{2,1,0:T(2,128)S(1)} %slice.587), channel_id=1, source_target_pairs={{0,8},{8,16},{16,24},{24,1},{32,40},{40,48},{48,56},{56,33},{64,72... | collective-permute-start | bytes 589832 | tf_op jit(solution)/shard_map/ppermute | solution.py:403
  52.7 2.6 %collective-permute-start.1 = (f32[12,3,2048]{2,1,0:T(4,128)S(1)}, f32[12,3,2048]{2,1,0:T(4,128)S(1)}, u32[]{:S(2)}, u32[]{:S(2)}) collective-permute-start(f32[12,3,2048]{2,1,0:T(4,128)S(1)} %slice.590), channel_id=1, source_target_pairs={{8,0},{16,8},{24,16},{1,24},{40,32},{48,40},{56,48},{33,56},{72,64... | collective-permute-start | bytes 884744 | tf_op jit(solution)/shard_map/ppermute | solution.py:404
  55.3 0.1 fusion.84
  55.4 6.4 %collective-permute-done.1 = f32[12,3,2048]{2,1,0:T(4,128)S(1)} collective-permute-done((f32[12,3,2048]{2,1,0:T(4,128)S(1)}, f32[12,3,2048]{2,1,0:T(4,128)S(1)}, u32[]{:S(2)}, u32[]{:S(2)}) %collective-permute-start.1) | collective-permute-done | bytes 294944 | tf_op jit(solution)/shard_map/ppermute | solution.py:404
  61.8 1.7 %fusion.6 = f32[12,16,2048]{2,1,0:T(8,128)S(1)} fusion(f32[12,2,2048]{2,1,0:T(2,128)S(1)} %collective-permute-done, f32[12,16,2048]{2,1,0:T(8,128)S(1)} %constant_dynamic-update-slice_fusion.2, f32[12,3,2048]{2,1,0:T(4,128)S(1)} %collective-permute-done.1, f32[12,16]{1,0:T(8,128)S(1)} %get-tuple-element.78, f32[12,16]{1,0:T(8,128)S(1)} %get-tuple-element.77, ...), kind=kLoop, calls=%fused_computation.14 | loop fusion | flops 6291456 | bytes 3641856 | tf_op jit(solution)/shard_map/add | solution.py:51
  63.6 0.5 maximum_select_fusion.10
  64.2 0.5 maximum_select_fusion.11
  64.8 0.5 maximum_select_fusion.12
  65.4 0.5 maximum_select_fusion.13
  66.0 0.5 maximum_select_fusion.14
  66.6 0.5 maximum_select_fusion.15
  67.1 0.1 slice.608
  67.2 0.2 maximum_select_fusion.16
  67.5 0.1 slice.610
  67.6 0.2 maximum_select_fusion.17
  68.0 0.2 maximum_select_fusion.18
  68.2 0.2 fusion.223
  68.4 0.2 maximum_select_fusion.19
  68.6 0.6 fusion.221
  69.2 0.1 fusion.222
  69.3 0.5 slice.619
  69.8 0.9 fusion.27
  70.7 0.1 slice.621
  70.8 0.3 fusion.28
  71.1 0.4 subtract_dynamic-update-slice_fusion
  71.9 0.1 constant_dynamic-update-slice_fusion.14
  72.0 0.1 constant_dynamic-update-slice_fusion.13.src_ref
  72.1 1.1 %copy-done = f32[12,16,2048]{2,1,0:T(8,128)} copy-done((f32[12,16,2048]{2,1,0:T(8,128)}, f32[12,16,2048]{2,1,0:T(8,128)S(1)}, u32[]{:S(2)}) %copy-start) | copy-done | bytes 1572888
  73.3 28.4 %shard_map.74 = f32[12,64,512]{2,1,0:T(8,128)} custom-call(f32[12,16,2048]{2,1,0:T(8,128)} %copy-done, bf16[512,512]{1,0:T(8,128)(2,1)} %get-tuple-element.129.matrix_ref), custom_call_target="tpu_custom_call" | custom-call | tf_op jit(solution)/shard_map/pallas_call | solution.py:311
  101.6 2.7 %copy.483 = f32[12,64,512]{2,1,0:T(8,128)} copy(f32[12,64,512]{2,1,0:T(8,128)} %shard_map.74) | data formatting | bytes 3145728
  (69 shorter events, 2.4 us)
Async XLA Ops:
  34.8 1.6 %copy-start.1 = (f32[12,3,2048]{2,1,0:T(4,128)S(1)}, f32[12,3,2048]{2,1,0:T(4,128)}, u32[]{:S(2)}) copy-start(f32[12,3,2048]{2,1,0:T(4,128)} %get-tuple-element.10) | copy-start | bytes 884740
  34.8 1.8 %copy-start.5 = (s32[2,12,64]{2,0,1:T(2,128)S(1)}, s32[2,12,64]{2,0,1:T(2,128)}, u32[]{:S(2)}) copy-start(s32[2,12,64]{2,0,1:T(2,128)} %param.8) | copy-start | bytes 18436
  34.8 1.8 %copy-start.6 = (s32[2,12,64]{2,0,1:T(2,128)S(1)}, s32[2,12,64]{2,0,1:T(2,128)}, u32[]{:S(2)}) copy-start(s32[2,12,64]{2,0,1:T(2,128)} %param.10) | copy-start | bytes 18436
  34.8 1.9 %copy-start.7 = (f32[2,12,64]{2,0,1:T(2,128)S(1)}, f32[2,12,64]{2,0,1:T(2,128)}, u32[]{:S(2)}) copy-start(f32[2,12,64]{2,0,1:T(2,128)} %param.11) | copy-start | bytes 18436
  34.8 1.9 %copy-start.8 = (f32[2,12,64]{2,0,1:T(2,128)S(1)}, f32[2,12,64]{2,0,1:T(2,128)}, u32[]{:S(2)}) copy-start(f32[2,12,64]{2,0,1:T(2,128)} %param.9) | copy-start | bytes 18436
  34.9 2.0 %copy-start.2 = (f32[12,2,2048]{2,1,0:T(2,128)S(1)}, f32[12,2,2048]{2,1,0:T(2,128)}, u32[]{:S(2)}) copy-start(f32[12,2,2048]{2,1,0:T(2,128)} %get-tuple-element.8) | copy-start | bytes 589828
  48.3 0.7 copy-start.4
  48.3 0.8 copy-start.3
  50.7 4.7 %collective-permute-start = (f32[12,2,2048]{2,1,0:T(2,128)S(1)}, f32[12,2,2048]{2,1,0:T(2,128)S(1)}, u32[]{:S(2)}, u32[]{:S(2)}) collective-permute-start(f32[12,2,2048]{2,1,0:T(2,128)S(1)} %slice.587), channel_id=1, source_target_pairs={{0,8},{8,16},{16,24},{24,1},{32,40},{40,48},{48,56},{56,33},{64,72... | collective-permute-start | bytes 589832 | tf_op jit(solution)/shard_map/ppermute | solution.py:403
  52.7 9.1 %collective-permute-start.1 = (f32[12,3,2048]{2,1,0:T(4,128)S(1)}, f32[12,3,2048]{2,1,0:T(4,128)S(1)}, u32[]{:S(2)}, u32[]{:S(2)}) collective-permute-start(f32[12,3,2048]{2,1,0:T(4,128)S(1)} %slice.590), channel_id=1, source_target_pairs={{8,0},{16,8},{24,16},{1,24},{40,32},{48,40},{56,48},{33,56},{72,64... | collective-permute-start | bytes 884744 | tf_op jit(solution)/shard_map/ppermute | solution.py:404
  72.1 1.1 %copy-start = (f32[12,16,2048]{2,1,0:T(8,128)}, f32[12,16,2048]{2,1,0:T(8,128)S(1)}, u32[]{:S(2)}) copy-start(f32[12,16,2048]{2,1,0:T(8,128)S(1)} %constant_dynamic-update-slice_fusion.13.src_ref) | copy-start | bytes 4718596

commit v9 on v8

--- a/solution.py
+++ b/solution.py
@@ -262,7 +262,7 @@
         to_up.wait_recv()
 
 
-def exit_kernel(src_ref, matrix_ref, out_ref, landed, send_sem, recv_sem, local_sem, *, src_at, dst_at):
+def exit_kernel(src_ref, out_ref, landed, send_sem, recv_sem, local_sem, *, src_at, dst_at):
     count = lax.axis_size("lon")
     me = lax.axis_index("lon")
     lat = lax.axis_index("lat")
@@ -295,15 +295,29 @@
         for copy in copies[chunk]:
             copy.wait_recv()
         locals_[chunk].wait()
-
-        def body(k, carry):
-            out_ref[k] = permute_block(landed[k], matrix_ref[...])
-            return carry
-
-        lax.fori_loop(chunk * per, (chunk + 1) * per, body, 0)
+        part = pl.ds(chunk * per, per)
+        out_ref[part] = landed[part]
     for row in copies:
         for copy in row:
             copy.wait_send()
+
+
+def unpermute_kernel(landed_ref, matrix_ref, out_ref, result, store_sem):
+    levels = landed_ref.shape[0]
+    per = levels // CHUNKS
+    stores = []
+    for chunk in range(CHUNKS):
+        def body(k, carry):
+            result[k] = permute_block(landed_ref[k], matrix_ref[...])
+            return carry
+
+        lax.fori_loop(chunk * per, (chunk + 1) * per, body, 0)
+        part = pl.ds(chunk * per, per)
+        store = pltpu.make_async_copy(result.at[part], out_ref.at[part], store_sem.at[chunk])
+        store.start()
+        stores.append(store)
+    for store in stores:
+        store.wait()
 
 
 def run_exchange(kernel, operand, matrix, out_shape, src_spec, out_spec, scratch, src_at, dst_at, ident):
@@ -379,11 +393,27 @@
         return ref.at[part, pl.ds((sender % parts) * count, count), pl.ds((sender // parts) * lane, lane)]
 
     shape = (levels, rows, cells * NTR)
-    return run_exchange(
-        exit_kernel, field, permutation(pair_order(cells), True), shape,
-        pl.BlockSpec(memory_space=pl.ANY), pl.BlockSpec(memory_space=pltpu.VMEM), shape,
-        src_at, dst_at, 1,
-    )
+    vmem = pl.BlockSpec(memory_space=pltpu.VMEM)
+    landed = pl.pallas_call(
+        functools.partial(exit_kernel, src_at=src_at, dst_at=dst_at),
+        out_shape=jax.ShapeDtypeStruct(shape, field.dtype),
+        in_specs=[pl.BlockSpec(memory_space=pl.ANY)],
+        out_specs=vmem,
+        scratch_shapes=[
+            pltpu.VMEM(shape, field.dtype),
+            pltpu.SemaphoreType.DMA((CHUNKS, devices)),
+            pltpu.SemaphoreType.DMA((CHUNKS, devices)),
+            pltpu.SemaphoreType.DMA((CHUNKS,)),
+        ],
+        compiler_params=pltpu.CompilerParams(collective_id=1, has_side_effects=True),
+    )(field)
+    return pl.pallas_call(
+        unpermute_kernel,
+        out_shape=jax.ShapeDtypeStruct(shape, field.dtype),
+        in_specs=[vmem, vmem],
+        out_specs=pl.BlockSpec(memory_space=pl.ANY),
+        scratch_shapes=[pltpu.VMEM(shape, field.dtype), pltpu.SemaphoreType.DMA((CHUNKS,))],
+    )(landed, permutation(pair_order(cells), True))
 
 
 def lat_halo(field, width):

time: 105 us -> 107 us (1.019)
  Pallas kernels: 62 us -> 66.7 us
  local copies, waits for them, and re-layouts: 11.3 us -> 8.62 us
    pallas_call x1 -> x2, Pallas kernels: 28.4 us -> 33.1 us  [the longest x1 26.2 us: from_columns(): pl.pallas_call(functools.partial(exit_kernel, src_at=src_at, dst_at=dst_a...]
    unnamed x30 -> x29, local copies, waits for them, and re-layouts: 6.09 us -> 3.42 us
where the time goes in v9:
time: 107 us
  Pallas kernels  66.7 us (62%)
  other arithmetic  19.3 us (18%)
  local copies, waits for them, and re-layouts  8.62 us (8%)
  waiting for transfers between devices  6.35 us (6%)
  starting transfers between devices  4.51 us (4%)
    pallas_call x1, Pallas kernels, to_columns(): pl.pallas_call(functools.partial(entry_kernel, src_at=src_at, dst_at=dst_...  33.6 us
    pallas_call x1, Pallas kernels, from_columns(): pl.pallas_call(functools.partial(exit_kernel, src_at=src_at, dst_at=dst_a...  26.2 us
    select_n x20, other arithmetic, roll_rows(): current = jnp.where(bit_mask(amount, position), moved, current)  7.74 us
    pallas_call x1, Pallas kernels, from_columns(): pl.pallas_call(unpermute_kernel, out_shape=jax.ShapeDtypeStruct(shape, fi...  6.9 us
    ppermute x1, waiting for transfers between devices, lat_halo(): above = lax.ppermute(field[:, :width], ('lon', 'lat'), down)  6.35 us
    add x2, other arithmetic, lat_step(): summed = addend if summed is None else summed + addend  5.79 us
    unnamed x29, local copies, waits for them, and re-layouts  3.42 us
    ppermute x1, starting transfers between devices, lat_halo(): above = lax.ppermute(field[:, :width], ('lon', 'lat'), down)  2.59 us
  transfers between devices with their start and end apart: 2, of which 1 were waited for; matrix products, arithmetic and copies ran while one was open for 0% of the time, Pallas kernels for 0%

profile of v9, /device:TPU:25, one launch (start us, length us, event | category | flops | bytes accessed | tf_op | source)
XLA Modules:
  0.0 106.5 jit_solution(17248071817592783947)
XLA Ops:
  0.0 1.1 %fusion.30 = (bf16[512,512]{1,0:T(8,128)(2,1)}, bf16[512,512]{1,0:T(8,128)(2,1)}) fusion(s32[512]{0:T(512)S(1)} %fusion.204), kind=kLoop, calls=%fused_computation.74 | loop fusion | flops 1048576 | bytes 1050624 | tf_op jit(solution)/shard_map/convert_element_type | solution.py:124
  1.1 33.6 %shard_map.73 = (f32[12,16,2048]{2,1,0:T(8,128)}, f32[12,2,2048]{2,1,0:T(2,128)}, f32[12,3,2048]{2,1,0:T(4,128)}) custom-call(f32[12,64,512]{2,1,0:T(8,128)} %x_ref.1, bf16[512,512]{1,0:T(8,128)(2,1)} %get-tuple-element.130.matrix_ref), custom_call_target="tpu_custom_call" | custom-call | tf_op jit(solution)/shard_map/pallas_call | solution.py:359
  34.9 1.6 %constant_dynamic-update-slice_fusion.1 = f32[12,19,2048]{2,1,0:T(8,128)S(1)} fusion(f32[12,16,2048]{2,1,0:T(8,128)} %get-tuple-element.9), kind=kLoop, calls=%fused_computation.144 | loop fusion | bytes 3145728
  36.4 0.1 constant_dynamic-update-slice_fusion
  36.6 0.1 constant_dynamic-slice_fusion
  36.7 0.1 constant_dynamic-slice_fusion.1
  36.9 4.1 %fusion.13 = f32[12,16,2048]{2,1,0:T(8,128)S(1)} fusion(f32[12,2,2048]{2,1,0:T(2,128)S(1)} %copy-done.2, f32[12,16,2048]{2,1,0:T(8,128)} %get-tuple-element.9, f32[12,19,2048]{2,1,0:T(8,128)S(1)} %constant_dynamic-update-slice_fusion, f32[12,16]{1,0:T(8,128)S(1)} %get-tuple-element.88, f32[12,16]{1,0:T(8,128)S(1)} %get-tuple-element.87, ...), kind=kLoop, calls=%fused_computation.21 | loop fusion | flops 5111808 | bytes 8065536 | tf_op jit(solution)/shard_map/add | solution.py:51
  41.1 0.1 fusion.112
  41.2 0.5 maximum_select_fusion
  41.8 0.5 maximum_select_fusion.1
  42.3 0.1 slice.540
  42.4 0.5 maximum_select_fusion.2
  43.0 0.5 maximum_select_fusion.3
  43.5 0.5 maximum_select_fusion.4
  44.1 0.5 maximum_select_fusion.5
  44.7 0.1 slice.549
  44.8 0.2 maximum_select_fusion.6
  45.0 0.1 slice.551
  45.2 0.2 maximum_select_fusion.7
  45.5 0.2 maximum_select_fusion.8
  45.7 0.2 fusion.226
  45.9 0.2 maximum_select_fusion.9
  46.1 0.6 fusion.224
  46.7 0.1 fusion.225
  46.8 0.5 slice.560
  47.3 0.9 fusion.23
  48.3 0.1 slice.562
  48.4 0.6 copy-done.4
  49.0 0.1 constant_dynamic-slice_fusion.3
  49.3 0.3 fusion.24
  49.6 0.4 subtract_dynamic-update-slice_fusion.1
  50.4 0.1 constant_dynamic-update-slice_fusion.3
  50.5 0.1 constant_dynamic-update-slice_fusion.2
  50.6 0.1 slice.587
  50.7 1.9 %collective-permute-start = (f32[12,2,2048]{2,1,0:T(2,128)S(1)}, f32[12,2,2048]{2,1,0:T(2,128)S(1)}, u32[]{:S(2)}, u32[]{:S(2)}) collective-permute-start(f32[12,2,2048]{2,1,0:T(2,128)S(1)} %slice.587), channel_id=1, source_target_pairs={{0,8},{8,16},{16,24},{24,1},{32,40},{40,48},{48,56},{56,33},{64,72... | collective-permute-start | bytes 589832 | tf_op jit(solution)/shard_map/ppermute | solution.py:433
  52.7 2.6 %collective-permute-start.1 = (f32[12,3,2048]{2,1,0:T(4,128)S(1)}, f32[12,3,2048]{2,1,0:T(4,128)S(1)}, u32[]{:S(2)}, u32[]{:S(2)}) collective-permute-start(f32[12,3,2048]{2,1,0:T(4,128)S(1)} %slice.590), channel_id=1, source_target_pairs={{8,0},{16,8},{24,16},{1,24},{40,32},{48,40},{56,48},{33,56},{72,64... | collective-permute-start | bytes 884744 | tf_op jit(solution)/shard_map/ppermute | solution.py:434
  55.3 0.1 fusion.84
  55.4 6.4 %collective-permute-done.1 = f32[12,3,2048]{2,1,0:T(4,128)S(1)} collective-permute-done((f32[12,3,2048]{2,1,0:T(4,128)S(1)}, f32[12,3,2048]{2,1,0:T(4,128)S(1)}, u32[]{:S(2)}, u32[]{:S(2)}) %collective-permute-start.1) | collective-permute-done | bytes 294944 | tf_op jit(solution)/shard_map/ppermute | solution.py:434
  61.8 1.7 %fusion.6 = f32[12,16,2048]{2,1,0:T(8,128)S(1)} fusion(f32[12,2,2048]{2,1,0:T(2,128)S(1)} %collective-permute-done, f32[12,16,2048]{2,1,0:T(8,128)S(1)} %constant_dynamic-update-slice_fusion.2, f32[12,3,2048]{2,1,0:T(4,128)S(1)} %collective-permute-done.1, f32[12,16]{1,0:T(8,128)S(1)} %get-tuple-element.78, f32[12,16]{1,0:T(8,128)S(1)} %get-tuple-element.77, ...), kind=kLoop, calls=%fused_computation.14 | loop fusion | flops 6291456 | bytes 3641856 | tf_op jit(solution)/shard_map/add | solution.py:51
  63.6 0.5 maximum_select_fusion.10
  64.2 0.5 maximum_select_fusion.11
  64.8 0.5 maximum_select_fusion.12
  65.4 0.5 maximum_select_fusion.13
  66.0 0.5 maximum_select_fusion.14
  66.6 0.5 maximum_select_fusion.15
  67.1 0.1 slice.608
  67.2 0.2 maximum_select_fusion.16
  67.5 0.1 slice.610
  67.6 0.2 maximum_select_fusion.17
  68.0 0.2 maximum_select_fusion.18
  68.2 0.2 fusion.223
  68.4 0.2 maximum_select_fusion.19
  68.6 0.6 fusion.221
  69.2 0.1 fusion.222
  69.3 0.5 slice.619
  69.8 0.9 fusion.27
  70.7 0.1 slice.621
  70.8 0.3 fusion.28
  71.1 0.4 subtract_dynamic-update-slice_fusion
  71.9 0.1 constant_dynamic-update-slice_fusion.14
  72.0 0.1 constant_dynamic-update-slice_fusion.13.src_ref
  72.1 1.1 %copy-done = f32[12,16,2048]{2,1,0:T(8,128)} copy-done((f32[12,16,2048]{2,1,0:T(8,128)}, f32[12,16,2048]{2,1,0:T(8,128)S(1)}, u32[]{:S(2)}) %copy-start) | copy-done | bytes 1572888
  73.3 26.2 %shard_map.74.landed_ref = f32[12,64,512]{2,1,0:T(8,128)} custom-call(f32[12,16,2048]{2,1,0:T(8,128)} %copy-done), custom_call_target="tpu_custom_call" | custom-call | tf_op jit(solution)/shard_map/pallas_call | solution.py:397
  99.4 6.9 %shard_map.75 = f32[12,64,512]{2,1,0:T(8,128)} custom-call(f32[12,64,512]{2,1,0:T(8,128)} %shard_map.74.landed_ref, bf16[512,512]{1,0:T(8,128)(2,1)} %get-tuple-element.129.matrix_ref), custom_call_target="tpu_custom_call" | custom-call | tf_op jit(solution)/shard_map/pallas_call | solution.py:410
  (69 shorter events, 2.4 us)
Async XLA Ops:
  34.8 1.6 %copy-start.1 = (f32[12,3,2048]{2,1,0:T(4,128)S(1)}, f32[12,3,2048]{2,1,0:T(4,128)}, u32[]{:S(2)}) copy-start(f32[12,3,2048]{2,1,0:T(4,128)} %get-tuple-element.10) | copy-start | bytes 884740
  34.8 1.8 %copy-start.5 = (s32[2,12,64]{2,0,1:T(2,128)S(1)}, s32[2,12,64]{2,0,1:T(2,128)}, u32[]{:S(2)}) copy-start(s32[2,12,64]{2,0,1:T(2,128)} %param.8) | copy-start | bytes 18436
  34.8 1.8 %copy-start.6 = (s32[2,12,64]{2,0,1:T(2,128)S(1)}, s32[2,12,64]{2,0,1:T(2,128)}, u32[]{:S(2)}) copy-start(s32[2,12,64]{2,0,1:T(2,128)} %param.10) | copy-start | bytes 18436
  34.8 1.9 %copy-start.7 = (f32[2,12,64]{2,0,1:T(2,128)S(1)}, f32[2,12,64]{2,0,1:T(2,128)}, u32[]{:S(2)}) copy-start(f32[2,12,64]{2,0,1:T(2,128)} %param.11) | copy-start | bytes 18436
  34.8 1.9 %copy-start.8 = (f32[2,12,64]{2,0,1:T(2,128)S(1)}, f32[2,12,64]{2,0,1:T(2,128)}, u32[]{:S(2)}) copy-start(f32[2,12,64]{2,0,1:T(2,128)} %param.9) | copy-start | bytes 18436
  34.9 2.0 %copy-start.2 = (f32[12,2,2048]{2,1,0:T(2,128)S(1)}, f32[12,2,2048]{2,1,0:T(2,128)}, u32[]{:S(2)}) copy-start(f32[12,2,2048]{2,1,0:T(2,128)} %get-tuple-element.8) | copy-start | bytes 589828
  48.3 0.7 copy-start.4
  48.3 0.8 copy-start.3
  50.7 4.7 %collective-permute-start = (f32[12,2,2048]{2,1,0:T(2,128)S(1)}, f32[12,2,2048]{2,1,0:T(2,128)S(1)}, u32[]{:S(2)}, u32[]{:S(2)}) collective-permute-start(f32[12,2,2048]{2,1,0:T(2,128)S(1)} %slice.587), channel_id=1, source_target_pairs={{0,8},{8,16},{16,24},{24,1},{32,40},{40,48},{48,56},{56,33},{64,72... | collective-permute-start | bytes 589832 | tf_op jit(solution)/shard_map/ppermute | solution.py:433
  52.7 9.1 %collective-permute-start.1 = (f32[12,3,2048]{2,1,0:T(4,128)S(1)}, f32[12,3,2048]{2,1,0:T(4,128)S(1)}, u32[]{:S(2)}, u32[]{:S(2)}) collective-permute-start(f32[12,3,2048]{2,1,0:T(4,128)S(1)} %slice.590), channel_id=1, source_target_pairs={{8,0},{16,8},{24,16},{1,24},{40,32},{48,40},{56,48},{33,56},{72,64... | collective-permute-start | bytes 884744 | tf_op jit(solution)/shard_map/ppermute | solution.py:434
  72.1 1.1 %copy-start = (f32[12,16,2048]{2,1,0:T(8,128)}, f32[12,16,2048]{2,1,0:T(8,128)S(1)}, u32[]{:S(2)}) copy-start(f32[12,16,2048]{2,1,0:T(8,128)S(1)} %constant_dynamic-update-slice_fusion.13.src_ref) | copy-start | bytes 4718596

commit v10 on v8

--- a/solution.py
+++ b/solution.py
@@ -48,6 +48,28 @@
         for tap_index in range(4):
             coeff = coeff + jnp.where(offset == tap_index - 1 - row_delta, weights[tap_index], 0.0)
         addend = coeff[:, :, None] * padded[:, 1 + place_index : 1 + place_index + row_count, :]
+        summed = addend if summed is None else summed + addend
+    return summed
+
+
+def lat_pieces(below, field, above, offset, fraction):
+    rows = field.shape[1]
+    low = below.shape[1]
+    weights = cubic_weights(fraction)
+    summed = None
+    for place_index in range(6):
+        row_delta = place_index - 2
+        coeff = jnp.zeros_like(fraction)
+        for tap_index in range(4):
+            coeff = coeff + jnp.where(offset == tap_index - 1 - row_delta, weights[tap_index], 0.0)
+        start = place_index - low
+        if start < 0:
+            window = jnp.concatenate([below[:, low + start :], field[:, : rows + start]], axis=1)
+        elif start > 0:
+            window = jnp.concatenate([field[:, start:], above[:, :start]], axis=1)
+        else:
+            window = field
+        addend = coeff[:, :, None] * window
         summed = addend if summed is None else summed + addend
     return summed
 
@@ -440,10 +462,10 @@
     )
     for time_step in range(STEPS):
         if time_step == 0:
-            padded = jnp.concatenate([below[:, :1], below, field, above], axis=1)
+            field = lat_pieces(below, field, above, lat_shift[time_step], lat_frac[time_step])
         else:
             padded = lat_halo(field, 3)
-        field = lat_step(padded, lat_shift[time_step], lat_frac[time_step], count)
+            field = lat_step(padded, lat_shift[time_step], lat_frac[time_step], count)
         amount = jnp.remainder(lon_shift[time_step], width // PAIR)
         field = lon_cubic(roll_rows(field, amount), lon_frac[time_step])
         field = remap(field, remap_frac[time_step])

time: 105 us -> 114 us (1.086)
  local copies, waits for them, and re-layouts: 11.3 us -> 21.3 us
  waiting for transfers between devices: 6.35 us -> 3.09 us
  Pallas kernels: 62 us -> 63.9 us
  starting transfers between devices: 4.51 us -> 5.74 us
    slice x0 -> x6, local copies, waits for them, and re-layouts: none -> 9.4 us  [the longest x5 7.73 us: lat_pieces(): window = jnp.concatenate([field[:, start:], above[:, :start]], axis=1)]
    ppermute x1, waiting for transfers between devices: 6.35 us -> 0.82 us  [lat_halo(): above = lax.ppermute(field[:, :width], ('lon', 'lat'), down)]
    add x2 -> x1, other arithmetic: 5.79 us -> 1.73 us  [lat_step(): summed = addend if summed is None else summed + addend]
    add x0 -> x2, other arithmetic: none -> 3.81 us  [the longest x1 3.79 us: lat_pieces(): summed = addend if summed is None else summed + addend]
    ppermute x1, waiting for transfers between devices: 0.01 us -> 2.27 us  [lat_halo(): below = lax.ppermute(field[:, rows - width + 1:], ('lon', 'lat'), up)]
    pallas_call x1, Pallas kernels: 28.4 us -> 30.2 us  [run_exchange(): pl.pallas_call(functools.partial(kernel, src_at=src_at, dst_at=dst_at), o...]
    ppermute x1, starting transfers between devices: 1.92 us -> 3.44 us  [lat_halo(): below = lax.ppermute(field[:, rows - width + 1:], ('lon', 'lat'), up)]
    unnamed x30 -> x23, local copies, waits for them, and re-layouts: 6.09 us -> 5.29 us
  transfers between devices with their start and end apart: 2 -> 2, of which waited for: 1 -> 2; matrix products, arithmetic and copies ran while one was open for 0% -> 0% of each run, Pallas kernels for 0% -> 0%
where the time goes in v10:
time: 114 us
  Pallas kernels  63.9 us (56%)
  local copies, waits for them, and re-layouts  21.3 us (19%)
  other arithmetic  19 us (17%)
  starting transfers between devices  5.74 us (5%)
  waiting for transfers between devices  3.09 us (3%)
    pallas_call x1, Pallas kernels, to_columns(): pl.pallas_call(functools.partial(entry_kernel, src_at=src_at, dst_at=dst_...  33.6 us
    pallas_call x1, Pallas kernels, run_exchange(): pl.pallas_call(functools.partial(kernel, src_at=src_at, dst_at=dst_at), o...  30.2 us
    select_n x20, other arithmetic, roll_rows(): current = jnp.where(bit_mask(amount, position), moved, current)  7.74 us
    slice x5, local copies, waits for them, and re-layouts, lat_pieces(): window = jnp.concatenate([field[:, start:], above[:, :start]], axis=1)  7.73 us
    unnamed x23, local copies, waits for them, and re-layouts  5.29 us
    add x1, other arithmetic, lat_pieces(): summed = addend if summed is None else summed + addend  3.79 us
    ppermute x1, starting transfers between devices, lat_halo(): below = lax.ppermute(field[:, rows - width + 1:], ('lon', 'lat'), up)  3.44 us
    ppermute x1, starting transfers between devices, lat_halo(): above = lax.ppermute(field[:, :width], ('lon', 'lat'), down)  2.3 us
  transfers between devices with their start and end apart: 2, of which 2 were waited for; matrix products, arithmetic and copies ran while one was open for 0% of the time, Pallas kernels for 0%

profile of v10, /device:TPU:25, one launch (start us, length us, event | category | flops | bytes accessed | tf_op | source)
XLA Modules:
  0.0 113.8 jit_solution(11680851178798880265)
XLA Ops:
  0.0 1.1 fusion.27
  1.1 33.6 %shard_map.73 = (f32[12,16,2048]{2,1,0:T(8,128)}, f32[12,2,2048]{2,1,0:T(2,128)}, f32[12,3,2048]{2,1,0:T(4,128)}) custom-call(f32[12,64,512]{2,1,0:T(8,128)} %x_ref.1, bf16[512,512]{1,0:T(8,128)(2,1)} %get-tuple-element.134.matrix_ref), custom_call_target="tpu_custom_call" | custom-call | tf_op jit(solution)/shard_map/pallas_call | solution.py:367
  34.8 4.2 %fusion.224 = (f32[12,14,2048]{2,1,0:T(8,128)}, f32[12,14,2048]{2,1,0:T(8,128)}) fusion(f32[12,16,2048]{2,1,0:T(8,128)} %get-tuple-element.9), kind=kLoop, calls=%fused_computation.554 | loop fusion | bytes 5505024 | tf_op jit(solution)/shard_map/slice | solution.py:69
  39.0 1.9 %fusion.225 = (f32[12,15,2048]{2,1,0:T(8,128)}, f32[12,15,2048]{2,1,0:T(8,128)}) fusion(f32[12,16,2048]{2,1,0:T(8,128)S(1)} %copy-done), kind=kLoop, calls=%fused_computation.555 | loop fusion | bytes 5898240 | tf_op jit(solution)/shard_map/slice | solution.py:69
  40.9 0.2 slice.436
  41.1 0.8 copy-done.2
  41.9 0.8 slice.435
  42.6 0.7 slice.433
  43.3 1.7 %slice.430 = f32[12,1,2048]{2,1,0:T(1,128)} slice(f32[12,2,2048]{2,1,0:T(2,128)} %get-tuple-element.8), slice={[0:12], [1:2], [0:2048]} | slice | bytes 196608 | tf_op jit(solution)/shard_map/slice | solution.py:67
  45.0 0.9 constant_dynamic-slice_fusion
  45.9 0.9 constant_dynamic-slice_fusion.1
  46.9 3.8 %fusion.17 = f32[12,16,2048]{2,1,0:T(8,128)S(1)} fusion(f32[12,14,2048]{2,1,0:T(8,128)} %get-tuple-element.68, f32[12,2,2048]{2,1,0:T(2,128)} %get-tuple-element.8, f32[12,15,2048]{2,1,0:T(8,128)} %get-tuple-element.70, f32[12,1,2048]{2,1,0:T(1,128)} %slice.430, f32[12,1,2048]{2,1,0:T(1,128)} %slice.433, f32[12,15,2048]{2,1,0:T(8,128)} %get-tuple-element.69, ...), kind=kLoop, calls=%fused_computation.26 | loop fusion | flops 6291456 | bytes 11014656 | tf_op jit(solution)/shard_map/add | solution.py:73
  50.8 0.5 maximum_select_fusion
  51.4 0.5 maximum_select_fusion.1
  52.0 0.5 maximum_select_fusion.2
  52.6 0.5 maximum_select_fusion.3
  53.2 0.5 maximum_select_fusion.4
  53.8 0.5 maximum_select_fusion.5
  54.3 0.1 slice.550
  54.5 0.2 maximum_select_fusion.6
  54.7 0.1 slice.552
  54.8 0.2 maximum_select_fusion.7
  55.2 0.2 maximum_select_fusion.8
  55.4 0.2 fusion.223
  55.6 0.2 maximum_select_fusion.9
  55.8 0.6 fusion.221
  56.4 0.5 slice.561
  57.0 0.9 fusion.20
  58.0 0.1 slice.563
  58.1 0.6 copy-done.4
  59.0 0.3 fusion.21
  59.2 0.4 subtract_dynamic-update-slice_fusion.1
  60.1 0.1 constant_dynamic-update-slice_fusion.1
  60.2 0.1 constant_dynamic-update-slice_fusion
  60.3 2.3 %collective-permute-start.1 = (f32[12,3,2048]{2,1,0:T(4,128)S(1)}, f32[12,3,2048]{2,1,0:T(4,128)S(1)}, u32[]{:S(2)}, u32[]{:S(2)}) collective-permute-start(f32[12,3,2048]{2,1,0:T(4,128)S(1)} %slice.591), channel_id=1, source_target_pairs={{8,0},{16,8},{24,16},{1,24},{40,32},{48,40},{56,48},{33,56},{72,64... | collective-permute-start | bytes 884744 | tf_op jit(solution)/shard_map/ppermute | solution.py:426
  62.6 0.1 slice.588
  62.7 3.4 %collective-permute-start = (f32[12,2,2048]{2,1,0:T(2,128)S(1)}, f32[12,2,2048]{2,1,0:T(2,128)S(1)}, u32[]{:S(2)}, u32[]{:S(2)}) collective-permute-start(f32[12,2,2048]{2,1,0:T(2,128)S(1)} %slice.588), channel_id=1, source_target_pairs={{0,8},{8,16},{16,24},{24,1},{32,40},{40,48},{48,56},{56,33},{64,72... | collective-permute-start | bytes 589832 | tf_op jit(solution)/shard_map/ppermute | solution.py:425
  66.3 2.3 %collective-permute-done = f32[12,2,2048]{2,1,0:T(2,128)S(1)} collective-permute-done((f32[12,2,2048]{2,1,0:T(2,128)S(1)}, f32[12,2,2048]{2,1,0:T(2,128)S(1)}, u32[]{:S(2)}, u32[]{:S(2)}) %collective-permute-start) | collective-permute-done | bytes 196640 | tf_op jit(solution)/shard_map/ppermute | solution.py:425
  68.6 0.8 collective-permute-done.1
  69.4 1.7 %fusion.6 = f32[12,16,2048]{2,1,0:T(8,128)S(1)} fusion(f32[12,2,2048]{2,1,0:T(2,128)S(1)} %collective-permute-done, f32[12,16,2048]{2,1,0:T(8,128)S(1)} %constant_dynamic-update-slice_fusion, f32[12,3,2048]{2,1,0:T(4,128)S(1)} %collective-permute-done.1, f32[12,16]{1,0:T(8,128)S(1)} %get-tuple-element.82, f32[12,16]{1,0:T(8,128)S(1)} %get-tuple-element.81, ...), kind=kLoop, calls=%fused_computation.12 | loop fusion | flops 6291456 | bytes 3641856 | tf_op jit(solution)/shard_map/add | solution.py:51
  71.3 0.5 maximum_select_fusion.10
  71.9 0.5 maximum_select_fusion.11
  72.5 0.5 maximum_select_fusion.12
  73.0 0.5 maximum_select_fusion.13
  73.6 0.5 maximum_select_fusion.14
  74.2 0.5 maximum_select_fusion.15
  74.8 0.1 slice.609
  74.9 0.2 maximum_select_fusion.16
  75.1 0.1 slice.611
  75.3 0.2 maximum_select_fusion.17
  75.6 0.2 maximum_select_fusion.18
  75.8 0.2 fusion.220
  76.0 0.2 maximum_select_fusion.19
  76.2 0.6 fusion.218
  76.8 0.5 slice.620
  77.4 0.9 fusion.24
  78.3 0.1 slice.622
  78.5 0.3 fusion.25
  78.7 0.4 subtract_dynamic-update-slice_fusion
  79.6 0.1 constant_dynamic-update-slice_fusion.12
  79.7 0.1 constant_dynamic-update-slice_fusion.11.src_ref
  79.8 1.1 copy-done.1
  80.9 30.2 %shard_map.74 = f32[12,64,512]{2,1,0:T(8,128)} custom-call(f32[12,16,2048]{2,1,0:T(8,128)} %copy-done.1, bf16[512,512]{1,0:T(8,128)(2,1)} %get-tuple-element.133.matrix_ref), custom_call_target="tpu_custom_call" | custom-call | tf_op jit(solution)/shard_map/pallas_call | solution.py:333
  111.2 2.7 %copy.482 = f32[12,64,512]{2,1,0:T(8,128)} copy(f32[12,64,512]{2,1,0:T(8,128)} %shard_map.74) | data formatting | bytes 3145728
  (67 shorter events, 2.9 us)
Async XLA Ops:
  34.8 4.2 %copy-start = (f32[12,16,2048]{2,1,0:T(8,128)S(1)}, f32[12,16,2048]{2,1,0:T(8,128)}, u32[]{:S(2)}) copy-start(f32[12,16,2048]{2,1,0:T(8,128)} %get-tuple-element.9) | copy-start | bytes 4718596
  40.9 1.0 copy-start.2
  40.9 4.1 %copy-start.5 = (s32[2,12,64]{2,0,1:T(2,128)S(1)}, s32[2,12,64]{2,0,1:T(2,128)}, u32[]{:S(2)}) copy-start(s32[2,12,64]{2,0,1:T(2,128)} %param.8) | copy-start | bytes 18436
  57.9 0.7 copy-start.4
  57.9 0.8 copy-start.3
  60.3 9.1 %collective-permute-start.1 = (f32[12,3,2048]{2,1,0:T(4,128)S(1)}, f32[12,3,2048]{2,1,0:T(4,128)S(1)}, u32[]{:S(2)}, u32[]{:S(2)}) collective-permute-start(f32[12,3,2048]{2,1,0:T(4,128)S(1)} %slice.591), channel_id=1, source_target_pairs={{8,0},{16,8},{24,16},{1,24},{40,32},{48,40},{56,48},{33,56},{72,64... | collective-permute-start | bytes 884744 | tf_op jit(solution)/shard_map/ppermute | solution.py:426
  62.7 5.9 %collective-permute-start = (f32[12,2,2048]{2,1,0:T(2,128)S(1)}, f32[12,2,2048]{2,1,0:T(2,128)S(1)}, u32[]{:S(2)}, u32[]{:S(2)}) collective-permute-start(f32[12,2,2048]{2,1,0:T(2,128)S(1)} %slice.588), channel_id=1, source_target_pairs={{0,8},{8,16},{16,24},{24,1},{32,40},{40,48},{48,56},{56,33},{64,72... | collective-permute-start | bytes 589832 | tf_op jit(solution)/shard_map/ppermute | solution.py:425
  79.8 1.1 %copy-start.1 = (f32[12,16,2048]{2,1,0:T(8,128)}, f32[12,16,2048]{2,1,0:T(8,128)S(1)}, u32[]{:S(2)}) copy-start(f32[12,16,2048]{2,1,0:T(8,128)S(1)} %constant_dynamic-update-slice_fusion.11.src_ref) | copy-start | bytes 4718596

commit v11 on v8

--- a/solution.py
+++ b/solution.py
@@ -1,6 +1,7 @@
 import functools
 
 import jax
+import numpy as np
 import jax.numpy as jnp
 from jax import lax
 from jax.experimental import pallas as pl
@@ -109,19 +110,18 @@
 
 
 def pair_order(cells):
-    cols = jnp.arange(cells * NTR)
+    cols = np.arange(cells * NTR)
     cell, tracer = cols // NTR, cols % NTR
-    target = (tracer // PAIR) * cells * PAIR + cell * PAIR + tracer % PAIR
-    return target
+    return (tracer // PAIR) * cells * PAIR + cell * PAIR + tracer % PAIR
 
 
 def permutation(target, inverse):
-    cols = jnp.arange(target.shape[0])
+    cols = np.arange(target.shape[0])
     if inverse:
         matrix = cols[:, None] == target[None, :]
     else:
         matrix = cols[None, :] == target[:, None]
-    return matrix.astype(jnp.bfloat16)
+    return jnp.asarray(matrix.astype(np.float32), dtype=jnp.bfloat16)
 
 
 def permute_block(block, matrix):

time: 105 us -> 104 us (level)
  other arithmetic: 19.3 us -> 18.2 us
    convert_element_type x1 -> x0, other arithmetic: 1.12 us -> none  [permutation(): return matrix.astype(jnp.bfloat16)]
where the time goes in v11:
time: 104 us; the launch traced here: 103 us
  Pallas kernels  62 us (60%)
  other arithmetic  18.2 us (18%)
  local copies, waits for them, and re-layouts  11.3 us (11%)
  waiting for transfers between devices  6.35 us (6%)
  starting transfers between devices  4.51 us (4%)
    pallas_call x1, Pallas kernels, to_columns(): pl.pallas_call(functools.partial(entry_kernel, src_at=src_at, dst_at=dst_...  33.6 us
    pallas_call x1, Pallas kernels, run_exchange(): pl.pallas_call(functools.partial(kernel, src_at=src_at, dst_at=dst_at), o...  28.4 us
    select_n x20, other arithmetic, roll_rows(): current = jnp.where(bit_mask(amount, position), moved, current)  7.74 us
    ppermute x1, waiting for transfers between devices, lat_halo(): above = lax.ppermute(field[:, :width], ('lon', 'lat'), down)  6.35 us
    unnamed x30, local copies, waits for them, and re-layouts  6.09 us
    add x2, other arithmetic, lat_step(): summed = addend if summed is None else summed + addend  5.81 us
    ppermute x1, starting transfers between devices, lat_halo(): above = lax.ppermute(field[:, :width], ('lon', 'lat'), down)  2.59 us
    slice x8, local copies, waits for them, and re-layouts, lon_cubic(): taps = [jnp.roll(shifted, PAIR * (1 - p), axis=2) for p in range(4)]  2.29 us
  transfers between devices with their start and end apart: 2, of which 1 were waited for; matrix products, arithmetic and copies ran while one was open for 0% of the time, Pallas kernels for 0%

profile of v11, /device:TPU:25, one launch (start us, length us, event | category | flops | bytes accessed | tf_op | source)
XLA Modules:
  0.0 103.2 jit_solution(16832505610644114890)
XLA Ops:
  0.0 33.6 %shard_map.91 = (f32[12,16,2048]{2,1,0:T(8,128)}, f32[12,2,2048]{2,1,0:T(2,128)}, f32[12,3,2048]{2,1,0:T(4,128)}) custom-call(f32[12,64,512]{2,1,0:T(8,128)} %x_ref.1, bf16[512,512]{1,0:T(8,128)(2,1)} %constant.381.clone.matrix_ref), custom_call_target="tpu_custom_call" | custom-call | tf_op jit(solution)/shard_map/pallas_call | solution.py:345
  33.7 1.6 %constant_dynamic-update-slice_fusion.1 = f32[12,19,2048]{2,1,0:T(8,128)S(1)} fusion(f32[12,16,2048]{2,1,0:T(8,128)} %get-tuple-element.9), kind=kLoop, calls=%fused_computation.140 | loop fusion | bytes 3145728
  35.3 0.1 constant_dynamic-update-slice_fusion
  35.5 0.1 constant_dynamic-slice_fusion
  35.6 0.1 constant_dynamic-slice_fusion.1
  35.8 4.1 %fusion.13 = f32[12,16,2048]{2,1,0:T(8,128)S(1)} fusion(f32[12,2,2048]{2,1,0:T(2,128)S(1)} %copy-done.2, f32[12,16,2048]{2,1,0:T(8,128)} %get-tuple-element.9, f32[12,19,2048]{2,1,0:T(8,128)S(1)} %constant_dynamic-update-slice_fusion, f32[12,16]{1,0:T(8,128)S(1)} %get-tuple-element.88, f32[12,16]{1,0:T(8,128)S(1)} %get-tuple-element.87, ...), kind=kLoop, calls=%fused_computation.21 | loop fusion | flops 5111808 | bytes 8065536 | tf_op jit(solution)/shard_map/add | solution.py:52
  39.9 0.1 slice.536
  39.9 0.1 fusion.110
  40.0 0.5 maximum_select_fusion
  40.5 0.1 slice.538
  40.6 0.5 maximum_select_fusion.1
  41.2 0.5 maximum_select_fusion.2
  41.8 0.5 maximum_select_fusion.3
  42.4 0.5 maximum_select_fusion.4
  43.0 0.5 maximum_select_fusion.5
  43.5 0.1 slice.549
  43.7 0.2 maximum_select_fusion.6
  43.9 0.1 slice.551
  44.0 0.2 maximum_select_fusion.7
  44.4 0.2 maximum_select_fusion.8
  44.6 0.2 fusion.211
  44.8 0.2 maximum_select_fusion.9
  45.0 0.6 fusion.209
  45.6 0.1 fusion.210
  45.7 0.5 slice.560
  46.2 0.9 fusion.23
  47.2 0.1 slice.562
  47.3 0.6 copy-done.4
  47.8 0.1 constant_dynamic-slice_fusion.3
  48.2 0.3 fusion.24
  48.4 0.4 subtract_dynamic-update-slice_fusion.1
  49.3 0.1 constant_dynamic-update-slice_fusion.3
  49.4 0.1 constant_dynamic-update-slice_fusion.2
  49.5 0.1 slice.587
  49.6 1.9 %collective-permute-start = (f32[12,2,2048]{2,1,0:T(2,128)S(1)}, f32[12,2,2048]{2,1,0:T(2,128)S(1)}, u32[]{:S(2)}, u32[]{:S(2)}) collective-permute-start(f32[12,2,2048]{2,1,0:T(2,128)S(1)} %slice.587), channel_id=1, source_target_pairs={{0,8},{8,16},{16,24},{24,1},{32,40},{40,48},{48,56},{56,33},{64,72... | collective-permute-start | bytes 589832 | tf_op jit(solution)/shard_map/ppermute | solution.py:403
  51.6 2.6 %collective-permute-start.1 = (f32[12,3,2048]{2,1,0:T(4,128)S(1)}, f32[12,3,2048]{2,1,0:T(4,128)S(1)}, u32[]{:S(2)}, u32[]{:S(2)}) collective-permute-start(f32[12,3,2048]{2,1,0:T(4,128)S(1)} %slice.590), channel_id=1, source_target_pairs={{8,0},{16,8},{24,16},{1,24},{40,32},{48,40},{56,48},{33,56},{72,64... | collective-permute-start | bytes 884744 | tf_op jit(solution)/shard_map/ppermute | solution.py:404
  54.2 0.1 fusion.82
  54.3 6.4 %collective-permute-done.1 = f32[12,3,2048]{2,1,0:T(4,128)S(1)} collective-permute-done((f32[12,3,2048]{2,1,0:T(4,128)S(1)}, f32[12,3,2048]{2,1,0:T(4,128)S(1)}, u32[]{:S(2)}, u32[]{:S(2)}) %collective-permute-start.1) | collective-permute-done | bytes 294944 | tf_op jit(solution)/shard_map/ppermute | solution.py:404
  60.7 1.7 %fusion.6 = f32[12,16,2048]{2,1,0:T(8,128)S(1)} fusion(f32[12,2,2048]{2,1,0:T(2,128)S(1)} %collective-permute-done, f32[12,16,2048]{2,1,0:T(8,128)S(1)} %constant_dynamic-update-slice_fusion.2, f32[12,3,2048]{2,1,0:T(4,128)S(1)} %collective-permute-done.1, f32[12,16]{1,0:T(8,128)S(1)} %get-tuple-element.78, f32[12,16]{1,0:T(8,128)S(1)} %get-tuple-element.77, ...), kind=kLoop, calls=%fused_computation.14 | loop fusion | flops 6291456 | bytes 3641856 | tf_op jit(solution)/shard_map/add | solution.py:52
  62.5 0.5 maximum_select_fusion.10
  63.1 0.5 maximum_select_fusion.11
  63.7 0.5 maximum_select_fusion.12
  64.3 0.5 maximum_select_fusion.13
  64.9 0.5 maximum_select_fusion.14
  65.5 0.5 maximum_select_fusion.15
  66.0 0.1 slice.608
  66.1 0.2 maximum_select_fusion.16
  66.4 0.1 slice.610
  66.5 0.2 maximum_select_fusion.17
  66.8 0.2 maximum_select_fusion.18
  67.1 0.2 fusion.208
  67.2 0.2 maximum_select_fusion.19
  67.5 0.6 fusion.206
  68.0 0.1 fusion.207
  68.2 0.5 slice.619
  68.6 0.9 fusion.27
  69.6 0.1 slice.621
  69.7 0.3 fusion.28
  70.0 0.4 subtract_dynamic-update-slice_fusion
  70.8 0.1 constant_dynamic-update-slice_fusion.14
  70.9 0.1 constant_dynamic-update-slice_fusion.13.src_ref
  71.0 1.1 %copy-done = f32[12,16,2048]{2,1,0:T(8,128)} copy-done((f32[12,16,2048]{2,1,0:T(8,128)}, f32[12,16,2048]{2,1,0:T(8,128)S(1)}, u32[]{:S(2)}) %copy-start) | copy-done | bytes 1572888
  72.1 28.4 %shard_map.92 = f32[12,64,512]{2,1,0:T(8,128)} custom-call(f32[12,16,2048]{2,1,0:T(8,128)} %copy-done, bf16[512,512]{1,0:T(8,128)(2,1)} %constant.382.clone.matrix_ref), custom_call_target="tpu_custom_call" | custom-call | tf_op jit(solution)/shard_map/pallas_call | solution.py:311
  100.5 2.7 %copy.485 = f32[12,64,512]{2,1,0:T(8,128)} copy(f32[12,64,512]{2,1,0:T(8,128)} %shard_map.92) | data formatting | bytes 3145728
  (67 shorter events, 2.3 us)
Async XLA Ops:
  33.7 1.6 %copy-start.1 = (f32[12,3,2048]{2,1,0:T(4,128)S(1)}, f32[12,3,2048]{2,1,0:T(4,128)}, u32[]{:S(2)}) copy-start(f32[12,3,2048]{2,1,0:T(4,128)} %get-tuple-element.10) | copy-start | bytes 884740
  33.7 1.8 %copy-start.5 = (s32[2,12,64]{2,0,1:T(2,128)S(1)}, s32[2,12,64]{2,0,1:T(2,128)}, u32[]{:S(2)}) copy-start(s32[2,12,64]{2,0,1:T(2,128)} %param.10) | copy-start | bytes 18436
  33.7 1.8 %copy-start.6 = (s32[2,12,64]{2,0,1:T(2,128)S(1)}, s32[2,12,64]{2,0,1:T(2,128)}, u32[]{:S(2)}) copy-start(s32[2,12,64]{2,0,1:T(2,128)} %param.12) | copy-start | bytes 18436
  33.7 1.9 %copy-start.7 = (f32[2,12,64]{2,0,1:T(2,128)S(1)}, f32[2,12,64]{2,0,1:T(2,128)}, u32[]{:S(2)}) copy-start(f32[2,12,64]{2,0,1:T(2,128)} %param.13) | copy-start | bytes 18436
  33.7 1.9 %copy-start.8 = (f32[2,12,64]{2,0,1:T(2,128)S(1)}, f32[2,12,64]{2,0,1:T(2,128)}, u32[]{:S(2)}) copy-start(f32[2,12,64]{2,0,1:T(2,128)} %param.11) | copy-start | bytes 18436
  33.7 2.0 %copy-start.2 = (f32[12,2,2048]{2,1,0:T(2,128)S(1)}, f32[12,2,2048]{2,1,0:T(2,128)}, u32[]{:S(2)}) copy-start(f32[12,2,2048]{2,1,0:T(2,128)} %get-tuple-element.8) | copy-start | bytes 589828
  47.1 0.7 copy-start.4
  47.1 0.8 copy-start.3
  49.6 4.7 %collective-permute-start = (f32[12,2,2048]{2,1,0:T(2,128)S(1)}, f32[12,2,2048]{2,1,0:T(2,128)S(1)}, u32[]{:S(2)}, u32[]{:S(2)}) collective-permute-start(f32[12,2,2048]{2,1,0:T(2,128)S(1)} %slice.587), channel_id=1, source_target_pairs={{0,8},{8,16},{16,24},{24,1},{32,40},{40,48},{48,56},{56,33},{64,72... | collective-permute-start | bytes 589832 | tf_op jit(solution)/shard_map/ppermute | solution.py:403
  51.6 9.1 %collective-permute-start.1 = (f32[12,3,2048]{2,1,0:T(4,128)S(1)}, f32[12,3,2048]{2,1,0:T(4,128)S(1)}, u32[]{:S(2)}, u32[]{:S(2)}) collective-permute-start(f32[12,3,2048]{2,1,0:T(4,128)S(1)} %slice.590), channel_id=1, source_target_pairs={{8,0},{16,8},{24,16},{1,24},{40,32},{48,40},{56,48},{33,56},{72,64... | collective-permute-start | bytes 884744 | tf_op jit(solution)/shard_map/ppermute | solution.py:404
  71.0 1.1 %copy-start = (f32[12,16,2048]{2,1,0:T(8,128)}, f32[12,16,2048]{2,1,0:T(8,128)S(1)}, u32[]{:S(2)}) copy-start(f32[12,16,2048]{2,1,0:T(8,128)S(1)} %constant_dynamic-update-slice_fusion.13.src_ref) | copy-start | bytes 4718596

commit v12 on v11

--- a/solution.py
+++ b/solution.py
@@ -134,7 +134,7 @@
     return total + jnp.dot(low, matrix, preferred_element_type=jnp.float32)
 
 
-CHUNKS = 4
+CHUNKS = 6
 MESH_ID = pl.DeviceIdType.MESH
 
 

time: 104 us -> 104 us (level)
  no operation moved by 1% of the time
where the time goes in v12:
time: 104 us
  Pallas kernels  62.6 us (60%)
  other arithmetic  18.2 us (18%)
  local copies, waits for them, and re-layouts  11.3 us (11%)
  waiting for transfers between devices  6.36 us (6%)
  starting transfers between devices  4.55 us (4%)
    pallas_call x1, Pallas kernels, to_columns(): pl.pallas_call(functools.partial(entry_kernel, src_at=src_at, dst_at=dst_...  34 us
    pallas_call x1, Pallas kernels, run_exchange(): pl.pallas_call(functools.partial(kernel, src_at=src_at, dst_at=dst_at), o...  28.6 us
    select_n x20, other arithmetic, roll_rows(): current = jnp.where(bit_mask(amount, position), moved, current)  7.74 us
    ppermute x1, waiting for transfers between devices, lat_halo(): above = lax.ppermute(field[:, :width], ('lon', 'lat'), down)  6.36 us
    unnamed x30, local copies, waits for them, and re-layouts  6.09 us
    add x2, other arithmetic, lat_step(): summed = addend if summed is None else summed + addend  5.81 us
    ppermute x1, starting transfers between devices, lat_halo(): above = lax.ppermute(field[:, :width], ('lon', 'lat'), down)  2.63 us
    slice x8, local copies, waits for them, and re-layouts, lon_cubic(): taps = [jnp.roll(shifted, PAIR * (1 - p), axis=2) for p in range(4)]  2.29 us
  transfers between devices with their start and end apart: 2, of which 1 were waited for; matrix products, arithmetic and copies ran while one was open for 0% of the time, Pallas kernels for 0%

profile of v12, /device:TPU:25, one launch (start us, length us, event | category | flops | bytes accessed | tf_op | source)
XLA Modules:
  0.0 103.9 jit_solution(4739537071948334773)
XLA Ops:
  0.0 34.0 %shard_map.91 = (f32[12,16,2048]{2,1,0:T(8,128)}, f32[12,2,2048]{2,1,0:T(2,128)}, f32[12,3,2048]{2,1,0:T(4,128)}) custom-call(f32[12,64,512]{2,1,0:T(8,128)} %x_ref.1, bf16[512,512]{1,0:T(8,128)(2,1)} %constant.381.clone.matrix_ref), custom_call_target="tpu_custom_call" | custom-call | tf_op jit(solution)/shard_map/pallas_call | solution.py:345
  34.1 1.6 %constant_dynamic-update-slice_fusion.1 = f32[12,19,2048]{2,1,0:T(8,128)S(1)} fusion(f32[12,16,2048]{2,1,0:T(8,128)} %get-tuple-element.9), kind=kLoop, calls=%fused_computation.140 | loop fusion | bytes 3145728
  35.7 0.1 constant_dynamic-update-slice_fusion
  35.8 0.1 constant_dynamic-slice_fusion
  36.0 0.1 constant_dynamic-slice_fusion.1
  36.1 4.1 %fusion.13 = f32[12,16,2048]{2,1,0:T(8,128)S(1)} fusion(f32[12,2,2048]{2,1,0:T(2,128)S(1)} %copy-done.2, f32[12,16,2048]{2,1,0:T(8,128)} %get-tuple-element.9, f32[12,19,2048]{2,1,0:T(8,128)S(1)} %constant_dynamic-update-slice_fusion, f32[12,16]{1,0:T(8,128)S(1)} %get-tuple-element.88, f32[12,16]{1,0:T(8,128)S(1)} %get-tuple-element.87, ...), kind=kLoop, calls=%fused_computation.21 | loop fusion | flops 5111808 | bytes 8065536 | tf_op jit(solution)/shard_map/add | solution.py:52
  40.3 0.1 fusion.110
  40.4 0.5 maximum_select_fusion
  41.0 0.5 maximum_select_fusion.1
  41.5 0.1 slice.540
  41.6 0.5 maximum_select_fusion.2
  42.2 0.5 maximum_select_fusion.3
  42.8 0.5 maximum_select_fusion.4
  43.3 0.1 slice.546
  43.4 0.5 maximum_select_fusion.5
  43.9 0.1 slice.549
  44.1 0.2 maximum_select_fusion.6
  44.3 0.1 slice.551
  44.4 0.2 maximum_select_fusion.7
  44.8 0.2 maximum_select_fusion.8
  45.0 0.2 fusion.211
  45.2 0.2 maximum_select_fusion.9
  45.4 0.6 fusion.209
  46.0 0.1 fusion.210
  46.1 0.5 slice.560
  46.6 0.9 fusion.23
  47.5 0.1 slice.562
  47.7 0.6 copy-done.4
  48.2 0.1 constant_dynamic-slice_fusion.3
  48.5 0.3 fusion.24
  48.8 0.4 subtract_dynamic-update-slice_fusion.1
  49.6 0.1 constant_dynamic-update-slice_fusion.3
  49.7 0.1 constant_dynamic-update-slice_fusion.2
  49.8 0.1 slice.587
  49.9 1.9 %collective-permute-start = (f32[12,2,2048]{2,1,0:T(2,128)S(1)}, f32[12,2,2048]{2,1,0:T(2,128)S(1)}, u32[]{:S(2)}, u32[]{:S(2)}) collective-permute-start(f32[12,2,2048]{2,1,0:T(2,128)S(1)} %slice.587), channel_id=1, source_target_pairs={{0,8},{8,16},{16,24},{24,1},{32,40},{40,48},{48,56},{56,33},{64,72... | collective-permute-start | bytes 589832 | tf_op jit(solution)/shard_map/ppermute | solution.py:403
  51.9 2.6 %collective-permute-start.1 = (f32[12,3,2048]{2,1,0:T(4,128)S(1)}, f32[12,3,2048]{2,1,0:T(4,128)S(1)}, u32[]{:S(2)}, u32[]{:S(2)}) collective-permute-start(f32[12,3,2048]{2,1,0:T(4,128)S(1)} %slice.590), channel_id=1, source_target_pairs={{8,0},{16,8},{24,16},{1,24},{40,32},{48,40},{56,48},{33,56},{72,64... | collective-permute-start | bytes 884744 | tf_op jit(solution)/shard_map/ppermute | solution.py:404
  54.6 0.1 fusion.82
  54.7 6.4 %collective-permute-done.1 = f32[12,3,2048]{2,1,0:T(4,128)S(1)} collective-permute-done((f32[12,3,2048]{2,1,0:T(4,128)S(1)}, f32[12,3,2048]{2,1,0:T(4,128)S(1)}, u32[]{:S(2)}, u32[]{:S(2)}) %collective-permute-start.1) | collective-permute-done | bytes 294944 | tf_op jit(solution)/shard_map/ppermute | solution.py:404
  61.1 1.7 %fusion.6 = f32[12,16,2048]{2,1,0:T(8,128)S(1)} fusion(f32[12,2,2048]{2,1,0:T(2,128)S(1)} %collective-permute-done, f32[12,16,2048]{2,1,0:T(8,128)S(1)} %constant_dynamic-update-slice_fusion.2, f32[12,3,2048]{2,1,0:T(4,128)S(1)} %collective-permute-done.1, f32[12,16]{1,0:T(8,128)S(1)} %get-tuple-element.78, f32[12,16]{1,0:T(8,128)S(1)} %get-tuple-element.77, ...), kind=kLoop, calls=%fused_computation.14 | loop fusion | flops 6291456 | bytes 3641856 | tf_op jit(solution)/shard_map/add | solution.py:52
  62.9 0.5 maximum_select_fusion.10
  63.5 0.5 maximum_select_fusion.11
  64.1 0.5 maximum_select_fusion.12
  64.7 0.5 maximum_select_fusion.13
  65.3 0.5 maximum_select_fusion.14
  65.9 0.5 maximum_select_fusion.15
  66.4 0.1 slice.608
  66.6 0.2 maximum_select_fusion.16
  66.8 0.1 slice.610
  66.9 0.2 maximum_select_fusion.17
  67.3 0.2 maximum_select_fusion.18
  67.5 0.2 fusion.208
  67.7 0.2 maximum_select_fusion.19
  67.9 0.6 fusion.206
  68.5 0.1 fusion.207
  68.6 0.5 slice.619
  69.1 0.9 fusion.27
  70.0 0.1 slice.621
  70.1 0.3 fusion.28
  70.4 0.4 subtract_dynamic-update-slice_fusion
  71.2 0.1 constant_dynamic-update-slice_fusion.14
  71.3 0.1 constant_dynamic-update-slice_fusion.13.src_ref
  71.4 1.1 %copy-done = f32[12,16,2048]{2,1,0:T(8,128)} copy-done((f32[12,16,2048]{2,1,0:T(8,128)}, f32[12,16,2048]{2,1,0:T(8,128)S(1)}, u32[]{:S(2)}) %copy-start) | copy-done | bytes 1572888
  72.6 28.6 %shard_map.92 = f32[12,64,512]{2,1,0:T(8,128)} custom-call(f32[12,16,2048]{2,1,0:T(8,128)} %copy-done, bf16[512,512]{1,0:T(8,128)(2,1)} %constant.382.clone.matrix_ref), custom_call_target="tpu_custom_call" | custom-call | tf_op jit(solution)/shard_map/pallas_call | solution.py:311
  101.2 2.7 %copy.485 = f32[12,64,512]{2,1,0:T(8,128)} copy(f32[12,64,512]{2,1,0:T(8,128)} %shard_map.92) | data formatting | bytes 3145728
  (67 shorter events, 2.3 us)
Async XLA Ops:
  34.0 1.6 %copy-start.1 = (f32[12,3,2048]{2,1,0:T(4,128)S(1)}, f32[12,3,2048]{2,1,0:T(4,128)}, u32[]{:S(2)}) copy-start(f32[12,3,2048]{2,1,0:T(4,128)} %get-tuple-element.10) | copy-start | bytes 884740
  34.0 1.8 %copy-start.5 = (s32[2,12,64]{2,0,1:T(2,128)S(1)}, s32[2,12,64]{2,0,1:T(2,128)}, u32[]{:S(2)}) copy-start(s32[2,12,64]{2,0,1:T(2,128)} %param.10) | copy-start | bytes 18436
  34.0 1.8 %copy-start.6 = (s32[2,12,64]{2,0,1:T(2,128)S(1)}, s32[2,12,64]{2,0,1:T(2,128)}, u32[]{:S(2)}) copy-start(s32[2,12,64]{2,0,1:T(2,128)} %param.12) | copy-start | bytes 18436
  34.1 1.9 %copy-start.7 = (f32[2,12,64]{2,0,1:T(2,128)S(1)}, f32[2,12,64]{2,0,1:T(2,128)}, u32[]{:S(2)}) copy-start(f32[2,12,64]{2,0,1:T(2,128)} %param.13) | copy-start | bytes 18436
  34.1 1.9 %copy-start.8 = (f32[2,12,64]{2,0,1:T(2,128)S(1)}, f32[2,12,64]{2,0,1:T(2,128)}, u32[]{:S(2)}) copy-start(f32[2,12,64]{2,0,1:T(2,128)} %param.11) | copy-start | bytes 18436
  34.1 2.0 %copy-start.2 = (f32[12,2,2048]{2,1,0:T(2,128)S(1)}, f32[12,2,2048]{2,1,0:T(2,128)}, u32[]{:S(2)}) copy-start(f32[12,2,2048]{2,1,0:T(2,128)} %get-tuple-element.8) | copy-start | bytes 589828
  47.5 0.7 copy-start.4
  47.5 0.8 copy-start.3
  49.9 4.8 %collective-permute-start = (f32[12,2,2048]{2,1,0:T(2,128)S(1)}, f32[12,2,2048]{2,1,0:T(2,128)S(1)}, u32[]{:S(2)}, u32[]{:S(2)}) collective-permute-start(f32[12,2,2048]{2,1,0:T(2,128)S(1)} %slice.587), channel_id=1, source_target_pairs={{0,8},{8,16},{16,24},{24,1},{32,40},{40,48},{48,56},{56,33},{64,72... | collective-permute-start | bytes 589832 | tf_op jit(solution)/shard_map/ppermute | solution.py:403
  51.9 9.1 %collective-permute-start.1 = (f32[12,3,2048]{2,1,0:T(4,128)S(1)}, f32[12,3,2048]{2,1,0:T(4,128)S(1)}, u32[]{:S(2)}, u32[]{:S(2)}) collective-permute-start(f32[12,3,2048]{2,1,0:T(4,128)S(1)} %slice.590), channel_id=1, source_target_pairs={{8,0},{16,8},{24,16},{1,24},{40,32},{48,40},{56,48},{33,56},{72,64... | collective-permute-start | bytes 884744 | tf_op jit(solution)/shard_map/ppermute | solution.py:404
  71.4 1.1 %copy-start = (f32[12,16,2048]{2,1,0:T(8,128)}, f32[12,16,2048]{2,1,0:T(8,128)S(1)}, u32[]{:S(2)}) copy-start(f32[12,16,2048]{2,1,0:T(8,128)S(1)} %constant_dynamic-update-slice_fusion.13.src_ref) | copy-start | bytes 4718596

commit v13 on v11

--- a/solution.py
+++ b/solution.py
@@ -405,10 +405,12 @@
     return jnp.concatenate([below[:, :1], below, field, above], axis=1)
 
 
-def roll_rows(field, amount):
+def roll_rows(field, shift):
     cells = field.shape[2] // PAIR
-    current = field
-    for position in range(cells.bit_length() - 1):
+    reach = cells // 4
+    amount = shift + reach
+    current = jnp.roll(field, -PAIR * reach, axis=2)
+    for position in range((2 * reach - 1).bit_length()):
         moved = jnp.roll(current, PAIR * 2**position, axis=2)
         current = jnp.where(bit_mask(amount, position), moved, current)
     return current
@@ -444,8 +446,7 @@
         else:
             padded = lat_halo(field, 3)
         field = lat_step(padded, lat_shift[time_step], lat_frac[time_step], count)
-        amount = jnp.remainder(lon_shift[time_step], width // PAIR)
-        field = lon_cubic(roll_rows(field, amount), lon_frac[time_step])
+        field = lon_cubic(roll_rows(field, lon_shift[time_step]), lon_frac[time_step])
         field = remap(field, remap_frac[time_step])
         field = diffuse(field, diffusivity)
     return from_columns(field, rows)

time: 104 us -> 104 us (level)
    select_n x20 -> x18, other arithmetic: 7.74 us -> 7.32 us  [roll_rows(): current = jnp.where(bit_mask(amount, position), moved, current)]
where the time goes in v13:
time: 104 us; the launch traced here: 103 us
  Pallas kernels  62 us (60%)
  other arithmetic  17.8 us (17%)
  local copies, waits for them, and re-layouts  11.2 us (11%)
  waiting for transfers between devices  6.37 us (6%)
  starting transfers between devices  4.51 us (4%)
    pallas_call x1, Pallas kernels, to_columns(): pl.pallas_call(functools.partial(entry_kernel, src_at=src_at, dst_at=dst_...  33.6 us
    pallas_call x1, Pallas kernels, run_exchange(): pl.pallas_call(functools.partial(kernel, src_at=src_at, dst_at=dst_at), o...  28.4 us
    select_n x18, other arithmetic, roll_rows(): current = jnp.where(bit_mask(amount, position), moved, current)  7.32 us
    ppermute x1, waiting for transfers between devices, lat_halo(): above = lax.ppermute(field[:, :width], ('lon', 'lat'), down)  6.36 us
    unnamed x30, local copies, waits for them, and re-layouts  6.09 us
    add x2, other arithmetic, lat_step(): summed = addend if summed is None else summed + addend  5.73 us
    ppermute x1, starting transfers between devices, lat_halo(): above = lax.ppermute(field[:, :width], ('lon', 'lat'), down)  2.59 us
    slice x8, local copies, waits for them, and re-layouts, lon_cubic(): taps = [jnp.roll(shifted, PAIR * (1 - p), axis=2) for p in range(4)]  2.29 us
  transfers between devices with their start and end apart: 2, of which 1 were waited for; matrix products, arithmetic and copies ran while one was open for 0% of the time, Pallas kernels for 0%

profile of v13, /device:TPU:25, one launch (start us, length us, event | category | flops | bytes accessed | tf_op | source)
XLA Modules:
  0.0 102.8 jit_solution(12451029522692030745)
XLA Ops:
  0.0 33.6 %shard_map.91 = (f32[12,16,2048]{2,1,0:T(8,128)}, f32[12,2,2048]{2,1,0:T(2,128)}, f32[12,3,2048]{2,1,0:T(4,128)}) custom-call(f32[12,64,512]{2,1,0:T(8,128)} %x_ref.1, bf16[512,512]{1,0:T(8,128)(2,1)} %constant.339.clone.matrix_ref), custom_call_target="tpu_custom_call" | custom-call | tf_op jit(solution)/shard_map/pallas_call | solution.py:345
  33.7 1.6 %constant_dynamic-update-slice_fusion.1 = f32[12,19,2048]{2,1,0:T(8,128)S(1)} fusion(f32[12,16,2048]{2,1,0:T(8,128)} %get-tuple-element.9), kind=kLoop, calls=%fused_computation.146 | loop fusion | bytes 3145728
  35.3 0.1 constant_dynamic-update-slice_fusion
  35.5 0.1 constant_dynamic-slice_fusion
  35.6 0.1 constant_dynamic-slice_fusion.1
  35.8 4.0 %fusion.17 = f32[12,16,2048]{2,1,0:T(8,128)S(1)} fusion(f32[12,2,2048]{2,1,0:T(2,128)S(1)} %copy-done.2, f32[12,16,2048]{2,1,0:T(8,128)} %get-tuple-element.9, f32[12,19,2048]{2,1,0:T(8,128)S(1)} %constant_dynamic-update-slice_fusion, f32[12,16]{1,0:T(8,128)S(1)} %get-tuple-element.84, f32[12,16]{1,0:T(8,128)S(1)} %get-tuple-element.83, ...), kind=kLoop, calls=%fused_computation.31 | loop fusion | flops 5111808 | bytes 8065536 | tf_op jit(solution)/shard_map/add | solution.py:52
  40.1 0.1 fusion.1
  40.2 0.5 fusion.3
  40.7 0.1 slice.545
  40.8 0.5 maximum_select_fusion
  41.4 0.5 maximum_select_fusion.1
  41.9 0.1 slice.549
  42.0 0.5 maximum_select_fusion.2
  42.6 0.5 maximum_select_fusion.3
  43.1 0.1 slice.553
  43.2 0.5 maximum_select_fusion.4
  43.7 0.1 slice.556
  43.8 0.2 maximum_select_fusion.5
  44.1 0.1 slice.558
  44.2 0.2 maximum_select_fusion.6
  44.4 0.1 slice.560
  44.6 0.2 maximum_select_fusion.7
  44.8 0.6 fusion.210
  45.4 0.1 fusion.211
  45.5 0.5 slice.565
  46.0 0.9 fusion.27
  47.0 0.1 slice.567
  47.1 0.6 copy-done.4
  47.6 0.1 constant_dynamic-slice_fusion.3
  48.0 0.3 fusion.28
  48.2 0.4 subtract_dynamic-update-slice_fusion.1
  49.1 0.1 constant_dynamic-update-slice_fusion.3
  49.2 0.1 constant_dynamic-update-slice_fusion.2
  49.2 0.1 slice.592
  49.4 1.9 %collective-permute-start = (f32[12,2,2048]{2,1,0:T(2,128)S(1)}, f32[12,2,2048]{2,1,0:T(2,128)S(1)}, u32[]{:S(2)}, u32[]{:S(2)}) collective-permute-start(f32[12,2,2048]{2,1,0:T(2,128)S(1)} %slice.592), channel_id=1, source_target_pairs={{0,8},{8,16},{16,24},{24,1},{32,40},{40,48},{48,56},{56,33},{64,72... | collective-permute-start | bytes 589832 | tf_op jit(solution)/shard_map/ppermute | solution.py:403
  51.3 2.6 %collective-permute-start.1 = (f32[12,3,2048]{2,1,0:T(4,128)S(1)}, f32[12,3,2048]{2,1,0:T(4,128)S(1)}, u32[]{:S(2)}, u32[]{:S(2)}) collective-permute-start(f32[12,3,2048]{2,1,0:T(4,128)S(1)} %slice.595), channel_id=1, source_target_pairs={{8,0},{16,8},{24,16},{1,24},{40,32},{48,40},{56,48},{33,56},{72,64... | collective-permute-start | bytes 884744 | tf_op jit(solution)/shard_map/ppermute | solution.py:404
  54.1 6.4 %collective-permute-done.1 = f32[12,3,2048]{2,1,0:T(4,128)S(1)} collective-permute-done((f32[12,3,2048]{2,1,0:T(4,128)S(1)}, f32[12,3,2048]{2,1,0:T(4,128)S(1)}, u32[]{:S(2)}, u32[]{:S(2)}) %collective-permute-start.1) | collective-permute-done | bytes 294944 | tf_op jit(solution)/shard_map/ppermute | solution.py:404
  60.4 1.7 %fusion.10 = f32[12,16,2048]{2,1,0:T(8,128)S(1)} fusion(f32[12,2,2048]{2,1,0:T(2,128)S(1)} %collective-permute-done, f32[12,16,2048]{2,1,0:T(8,128)S(1)} %constant_dynamic-update-slice_fusion.2, f32[12,3,2048]{2,1,0:T(4,128)S(1)} %collective-permute-done.1, f32[12,16]{1,0:T(8,128)S(1)} %get-tuple-element.74, f32[12,16]{1,0:T(8,128)S(1)} %get-tuple-element.73, ...), kind=kLoop, calls=%fused_computation.24 | loop fusion | flops 6291456 | bytes 3641856 | tf_op jit(solution)/shard_map/add | solution.py:52
  62.4 0.1 fusion
  62.5 0.5 fusion.2
  63.0 0.1 slice.605
  63.1 0.5 maximum_select_fusion.8
  63.7 0.5 maximum_select_fusion.9
  64.3 0.5 maximum_select_fusion.10
  64.9 0.5 maximum_select_fusion.11
  65.5 0.5 maximum_select_fusion.12
  66.0 0.1 slice.616
  66.2 0.2 maximum_select_fusion.13
  66.4 0.1 slice.618
  66.5 0.2 maximum_select_fusion.14
  66.8 0.1 slice.620
  66.9 0.2 maximum_select_fusion.15
  67.1 0.6 fusion.208
  67.7 0.1 fusion.209
  67.8 0.5 slice.625
  68.3 0.9 fusion.31
  69.3 0.1 slice.627
  69.4 0.3 fusion.32
  69.6 0.4 subtract_dynamic-update-slice_fusion
  70.5 0.1 constant_dynamic-update-slice_fusion.14
  70.6 0.1 constant_dynamic-update-slice_fusion.13.src_ref
  70.7 1.1 %copy-done = f32[12,16,2048]{2,1,0:T(8,128)} copy-done((f32[12,16,2048]{2,1,0:T(8,128)}, f32[12,16,2048]{2,1,0:T(8,128)S(1)}, u32[]{:S(2)}) %copy-start) | copy-done | bytes 1572888
  71.8 28.4 %shard_map.92 = f32[12,64,512]{2,1,0:T(8,128)} custom-call(f32[12,16,2048]{2,1,0:T(8,128)} %copy-done, bf16[512,512]{1,0:T(8,128)(2,1)} %constant.340.clone.matrix_ref), custom_call_target="tpu_custom_call" | custom-call | tf_op jit(solution)/shard_map/pallas_call | solution.py:311
  100.2 2.7 %copy.562 = f32[12,64,512]{2,1,0:T(8,128)} copy(f32[12,64,512]{2,1,0:T(8,128)} %shard_map.92) | data formatting | bytes 3145728
  (69 shorter events, 2.4 us)
Async XLA Ops:
  33.7 1.6 %copy-start.1 = (f32[12,3,2048]{2,1,0:T(4,128)S(1)}, f32[12,3,2048]{2,1,0:T(4,128)}, u32[]{:S(2)}) copy-start(f32[12,3,2048]{2,1,0:T(4,128)} %get-tuple-element.10) | copy-start | bytes 884740
  33.7 1.8 %copy-start.5 = (s32[2,12,64]{2,0,1:T(2,128)S(1)}, s32[2,12,64]{2,0,1:T(2,128)}, u32[]{:S(2)}) copy-start(s32[2,12,64]{2,0,1:T(2,128)} %param.10) | copy-start | bytes 18436
  33.7 1.8 %copy-start.6 = (s32[2,12,64]{2,0,1:T(2,128)S(1)}, s32[2,12,64]{2,0,1:T(2,128)}, u32[]{:S(2)}) copy-start(s32[2,12,64]{2,0,1:T(2,128)} %param.12) | copy-start | bytes 18436
  33.7 1.9 %copy-start.7 = (f32[2,12,64]{2,0,1:T(2,128)S(1)}, f32[2,12,64]{2,0,1:T(2,128)}, u32[]{:S(2)}) copy-start(f32[2,12,64]{2,0,1:T(2,128)} %param.13) | copy-start | bytes 18436
  33.7 1.9 %copy-start.8 = (f32[2,12,64]{2,0,1:T(2,128)S(1)}, f32[2,12,64]{2,0,1:T(2,128)}, u32[]{:S(2)}) copy-start(f32[2,12,64]{2,0,1:T(2,128)} %param.11) | copy-start | bytes 18436
  33.7 2.0 %copy-start.2 = (f32[12,2,2048]{2,1,0:T(2,128)S(1)}, f32[12,2,2048]{2,1,0:T(2,128)}, u32[]{:S(2)}) copy-start(f32[12,2,2048]{2,1,0:T(2,128)} %get-tuple-element.8) | copy-start | bytes 589828
  46.9 0.7 copy-start.4
  46.9 0.8 copy-start.3
  49.4 4.7 %collective-permute-start = (f32[12,2,2048]{2,1,0:T(2,128)S(1)}, f32[12,2,2048]{2,1,0:T(2,128)S(1)}, u32[]{:S(2)}, u32[]{:S(2)}) collective-permute-start(f32[12,2,2048]{2,1,0:T(2,128)S(1)} %slice.592), channel_id=1, source_target_pairs={{0,8},{8,16},{16,24},{24,1},{32,40},{40,48},{48,56},{56,33},{64,72... | collective-permute-start | bytes 589832 | tf_op jit(solution)/shard_map/ppermute | solution.py:403
  51.3 9.1 %collective-permute-start.1 = (f32[12,3,2048]{2,1,0:T(4,128)S(1)}, f32[12,3,2048]{2,1,0:T(4,128)S(1)}, u32[]{:S(2)}, u32[]{:S(2)}) collective-permute-start(f32[12,3,2048]{2,1,0:T(4,128)S(1)} %slice.595), channel_id=1, source_target_pairs={{8,0},{16,8},{24,16},{1,24},{40,32},{48,40},{56,48},{33,56},{72,64... | collective-permute-start | bytes 884744 | tf_op jit(solution)/shard_map/ppermute | solution.py:404
  70.7 1.1 %copy-start = (f32[12,16,2048]{2,1,0:T(8,128)}, f32[12,16,2048]{2,1,0:T(8,128)S(1)}, u32[]{:S(2)}) copy-start(f32[12,16,2048]{2,1,0:T(8,128)S(1)} %constant_dynamic-update-slice_fusion.13.src_ref) | copy-start | bytes 4718596

commit v14 on v13

--- a/solution.py
+++ b/solution.py
@@ -381,7 +381,7 @@
     shape = (levels, rows, cells * NTR)
     return run_exchange(
         exit_kernel, field, permutation(pair_order(cells), True), shape,
-        pl.BlockSpec(memory_space=pl.ANY), pl.BlockSpec(memory_space=pltpu.VMEM), shape,
+        pl.BlockSpec(memory_space=pltpu.VMEM), pl.BlockSpec(memory_space=pltpu.VMEM), shape,
         src_at, dst_at, 1,
     )
 

time: 104 us -> 104 us (level)
  no operation moved by 1% of the time
where the time goes in v14:
time: 104 us; the launch traced here: 103 us
  Pallas kernels  62.3 us (60%)
  other arithmetic  17.8 us (17%)
  local copies, waits for them, and re-layouts  11.2 us (11%)
  waiting for transfers between devices  6.37 us (6%)
  starting transfers between devices  4.51 us (4%)
    pallas_call x1, Pallas kernels, to_columns(): pl.pallas_call(functools.partial(entry_kernel, src_at=src_at, dst_at=dst_...  33.6 us
    pallas_call x1, Pallas kernels, run_exchange(): pl.pallas_call(functools.partial(kernel, src_at=src_at, dst_at=dst_at), o...  28.6 us
    select_n x18, other arithmetic, roll_rows(): current = jnp.where(bit_mask(amount, position), moved, current)  7.32 us
    ppermute x1, waiting for transfers between devices, lat_halo(): above = lax.ppermute(field[:, :width], ('lon', 'lat'), down)  6.36 us
    unnamed x30, local copies, waits for them, and re-layouts  6.09 us
    add x2, other arithmetic, lat_step(): summed = addend if summed is None else summed + addend  5.73 us
    ppermute x1, starting transfers between devices, lat_halo(): above = lax.ppermute(field[:, :width], ('lon', 'lat'), down)  2.59 us
    slice x8, local copies, waits for them, and re-layouts, lon_cubic(): taps = [jnp.roll(shifted, PAIR * (1 - p), axis=2) for p in range(4)]  2.29 us
  transfers between devices with their start and end apart: 2, of which 1 were waited for; matrix products, arithmetic and copies ran while one was open for 0% of the time, Pallas kernels for 0%

profile of v14, /device:TPU:25, one launch (start us, length us, event | category | flops | bytes accessed | tf_op | source)
XLA Modules:
  0.0 103.1 jit_solution(17647511361366976902)
XLA Ops:
  0.0 33.6 %shard_map.91 = (f32[12,16,2048]{2,1,0:T(8,128)}, f32[12,2,2048]{2,1,0:T(2,128)}, f32[12,3,2048]{2,1,0:T(4,128)}) custom-call(f32[12,64,512]{2,1,0:T(8,128)} %x_ref.1, bf16[512,512]{1,0:T(8,128)(2,1)} %constant.339.clone.matrix_ref), custom_call_target="tpu_custom_call" | custom-call | tf_op jit(solution)/shard_map/pallas_call | solution.py:345
  33.7 1.6 %constant_dynamic-update-slice_fusion.1 = f32[12,19,2048]{2,1,0:T(8,128)S(1)} fusion(f32[12,16,2048]{2,1,0:T(8,128)} %get-tuple-element.9), kind=kLoop, calls=%fused_computation.146 | loop fusion | bytes 3145728
  35.3 0.1 constant_dynamic-update-slice_fusion
  35.5 0.1 constant_dynamic-slice_fusion
  35.6 0.1 constant_dynamic-slice_fusion.1
  35.8 4.0 %fusion.17 = f32[12,16,2048]{2,1,0:T(8,128)S(1)} fusion(f32[12,2,2048]{2,1,0:T(2,128)S(1)} %copy-done.2, f32[12,16,2048]{2,1,0:T(8,128)} %get-tuple-element.9, f32[12,19,2048]{2,1,0:T(8,128)S(1)} %constant_dynamic-update-slice_fusion, f32[12,16]{1,0:T(8,128)S(1)} %get-tuple-element.84, f32[12,16]{1,0:T(8,128)S(1)} %get-tuple-element.83, ...), kind=kLoop, calls=%fused_computation.31 | loop fusion | flops 5111808 | bytes 8065536 | tf_op jit(solution)/shard_map/add | solution.py:52
  39.9 0.1 slice.540
  40.1 0.1 fusion.1
  40.2 0.5 fusion.3
  40.8 0.5 maximum_select_fusion
  41.3 0.1 slice.547
  41.4 0.5 maximum_select_fusion.1
  42.0 0.5 maximum_select_fusion.2
  42.5 0.1 slice.551
  42.6 0.5 maximum_select_fusion.3
  43.2 0.5 maximum_select_fusion.4
  43.7 0.1 slice.556
  43.8 0.2 maximum_select_fusion.5
  44.1 0.1 slice.558
  44.2 0.2 maximum_select_fusion.6
  44.4 0.1 slice.560
  44.6 0.2 maximum_select_fusion.7
  44.8 0.6 fusion.210
  45.4 0.1 fusion.211
  45.5 0.5 slice.565
  46.0 0.9 fusion.27
  47.0 0.1 slice.567
  47.1 0.6 copy-done.4
  47.6 0.1 constant_dynamic-slice_fusion.3
  48.0 0.3 fusion.28
  48.2 0.4 subtract_dynamic-update-slice_fusion.1
  49.1 0.1 constant_dynamic-update-slice_fusion.3
  49.2 0.1 constant_dynamic-update-slice_fusion.2
  49.2 0.1 slice.592
  49.4 1.9 %collective-permute-start = (f32[12,2,2048]{2,1,0:T(2,128)S(1)}, f32[12,2,2048]{2,1,0:T(2,128)S(1)}, u32[]{:S(2)}, u32[]{:S(2)}) collective-permute-start(f32[12,2,2048]{2,1,0:T(2,128)S(1)} %slice.592), channel_id=1, source_target_pairs={{0,8},{8,16},{16,24},{24,1},{32,40},{40,48},{48,56},{56,33},{64,72... | collective-permute-start | bytes 589832 | tf_op jit(solution)/shard_map/ppermute | solution.py:403
  51.3 2.6 %collective-permute-start.1 = (f32[12,3,2048]{2,1,0:T(4,128)S(1)}, f32[12,3,2048]{2,1,0:T(4,128)S(1)}, u32[]{:S(2)}, u32[]{:S(2)}) collective-permute-start(f32[12,3,2048]{2,1,0:T(4,128)S(1)} %slice.595), channel_id=1, source_target_pairs={{8,0},{16,8},{24,16},{1,24},{40,32},{48,40},{56,48},{33,56},{72,64... | collective-permute-start | bytes 884744 | tf_op jit(solution)/shard_map/ppermute | solution.py:404
  54.1 6.4 %collective-permute-done.1 = f32[12,3,2048]{2,1,0:T(4,128)S(1)} collective-permute-done((f32[12,3,2048]{2,1,0:T(4,128)S(1)}, f32[12,3,2048]{2,1,0:T(4,128)S(1)}, u32[]{:S(2)}, u32[]{:S(2)}) %collective-permute-start.1) | collective-permute-done | bytes 294944 | tf_op jit(solution)/shard_map/ppermute | solution.py:404
  60.4 1.7 %fusion.10 = f32[12,16,2048]{2,1,0:T(8,128)S(1)} fusion(f32[12,2,2048]{2,1,0:T(2,128)S(1)} %collective-permute-done, f32[12,16,2048]{2,1,0:T(8,128)S(1)} %constant_dynamic-update-slice_fusion.2, f32[12,3,2048]{2,1,0:T(4,128)S(1)} %collective-permute-done.1, f32[12,16]{1,0:T(8,128)S(1)} %get-tuple-element.74, f32[12,16]{1,0:T(8,128)S(1)} %get-tuple-element.73, ...), kind=kLoop, calls=%fused_computation.24 | loop fusion | flops 6291456 | bytes 3641856 | tf_op jit(solution)/shard_map/add | solution.py:52
  62.3 0.1 slice.600
  62.4 0.1 fusion
  62.5 0.5 fusion.2
  63.1 0.5 maximum_select_fusion.8
  63.7 0.5 maximum_select_fusion.9
  64.3 0.5 maximum_select_fusion.10
  64.9 0.5 maximum_select_fusion.11
  65.5 0.5 maximum_select_fusion.12
  66.0 0.1 slice.616
  66.2 0.2 maximum_select_fusion.13
  66.4 0.1 slice.618
  66.5 0.2 maximum_select_fusion.14
  66.8 0.1 slice.620
  66.9 0.2 maximum_select_fusion.15
  67.1 0.6 fusion.208
  67.7 0.1 fusion.209
  67.8 0.5 slice.625
  68.3 0.9 fusion.31
  69.3 0.1 slice.627
  69.4 0.3 fusion.32
  69.6 0.4 subtract_dynamic-update-slice_fusion
  70.5 0.1 constant_dynamic-update-slice_fusion.14
  70.6 0.1 constant_dynamic-update-slice_fusion.13.src_ref
  70.7 1.1 %copy-done = f32[12,16,2048]{2,1,0:T(8,128)} copy-done((f32[12,16,2048]{2,1,0:T(8,128)}, f32[12,16,2048]{2,1,0:T(8,128)S(1)}, u32[]{:S(2)}) %copy-start) | copy-done | bytes 1572888
  71.8 28.6 %shard_map.92 = f32[12,64,512]{2,1,0:T(8,128)} custom-call(f32[12,16,2048]{2,1,0:T(8,128)} %copy-done, bf16[512,512]{1,0:T(8,128)(2,1)} %constant.340.clone.matrix_ref), custom_call_target="tpu_custom_call" | custom-call | tf_op jit(solution)/shard_map/pallas_call | solution.py:311
  100.4 2.7 %copy.562 = f32[12,64,512]{2,1,0:T(8,128)} copy(f32[12,64,512]{2,1,0:T(8,128)} %shard_map.92) | data formatting | bytes 3145728
  (69 shorter events, 2.4 us)
Async XLA Ops:
  33.7 1.6 %copy-start.1 = (f32[12,3,2048]{2,1,0:T(4,128)S(1)}, f32[12,3,2048]{2,1,0:T(4,128)}, u32[]{:S(2)}) copy-start(f32[12,3,2048]{2,1,0:T(4,128)} %get-tuple-element.10) | copy-start | bytes 884740
  33.7 1.8 %copy-start.5 = (s32[2,12,64]{2,0,1:T(2,128)S(1)}, s32[2,12,64]{2,0,1:T(2,128)}, u32[]{:S(2)}) copy-start(s32[2,12,64]{2,0,1:T(2,128)} %param.10) | copy-start | bytes 18436
  33.7 1.8 %copy-start.6 = (s32[2,12,64]{2,0,1:T(2,128)S(1)}, s32[2,12,64]{2,0,1:T(2,128)}, u32[]{:S(2)}) copy-start(s32[2,12,64]{2,0,1:T(2,128)} %param.12) | copy-start | bytes 18436
  33.7 1.9 %copy-start.7 = (f32[2,12,64]{2,0,1:T(2,128)S(1)}, f32[2,12,64]{2,0,1:T(2,128)}, u32[]{:S(2)}) copy-start(f32[2,12,64]{2,0,1:T(2,128)} %param.13) | copy-start | bytes 18436
  33.7 1.9 %copy-start.8 = (f32[2,12,64]{2,0,1:T(2,128)S(1)}, f32[2,12,64]{2,0,1:T(2,128)}, u32[]{:S(2)}) copy-start(f32[2,12,64]{2,0,1:T(2,128)} %param.11) | copy-start | bytes 18436
  33.7 2.0 %copy-start.2 = (f32[12,2,2048]{2,1,0:T(2,128)S(1)}, f32[12,2,2048]{2,1,0:T(2,128)}, u32[]{:S(2)}) copy-start(f32[12,2,2048]{2,1,0:T(2,128)} %get-tuple-element.8) | copy-start | bytes 589828
  46.9 0.7 copy-start.4
  46.9 0.8 copy-start.3
  49.4 4.7 %collective-permute-start = (f32[12,2,2048]{2,1,0:T(2,128)S(1)}, f32[12,2,2048]{2,1,0:T(2,128)S(1)}, u32[]{:S(2)}, u32[]{:S(2)}) collective-permute-start(f32[12,2,2048]{2,1,0:T(2,128)S(1)} %slice.592), channel_id=1, source_target_pairs={{0,8},{8,16},{16,24},{24,1},{32,40},{40,48},{48,56},{56,33},{64,72... | collective-permute-start | bytes 589832 | tf_op jit(solution)/shard_map/ppermute | solution.py:403
  51.3 9.1 %collective-permute-start.1 = (f32[12,3,2048]{2,1,0:T(4,128)S(1)}, f32[12,3,2048]{2,1,0:T(4,128)S(1)}, u32[]{:S(2)}, u32[]{:S(2)}) collective-permute-start(f32[12,3,2048]{2,1,0:T(4,128)S(1)} %slice.595), channel_id=1, source_target_pairs={{8,0},{16,8},{24,16},{1,24},{40,32},{48,40},{56,48},{33,56},{72,64... | collective-permute-start | bytes 884744 | tf_op jit(solution)/shard_map/ppermute | solution.py:404
  70.7 1.1 %copy-start = (f32[12,16,2048]{2,1,0:T(8,128)}, f32[12,16,2048]{2,1,0:T(8,128)S(1)}, u32[]{:S(2)}) copy-start(f32[12,16,2048]{2,1,0:T(8,128)S(1)} %constant_dynamic-update-slice_fusion.13.src_ref) | copy-start | bytes 4718596

commit v15 on v13

--- a/solution.py
+++ b/solution.py
@@ -40,7 +40,7 @@
     return (w_zero, w_one, w_two, w_three)
 
 
-def lat_step(padded, offset, fraction, row_count):
+def lat_step(padded, offset, fraction, row_count, first=1):
     weights = cubic_weights(fraction)
     summed = None
     for place_index in range(6):
@@ -48,7 +48,7 @@
         coeff = jnp.zeros_like(fraction)
         for tap_index in range(4):
             coeff = coeff + jnp.where(offset == tap_index - 1 - row_delta, weights[tap_index], 0.0)
-        addend = coeff[:, :, None] * padded[:, 1 + place_index : 1 + place_index + row_count, :]
+        addend = coeff[:, :, None] * padded[:, first + place_index : first + place_index + row_count, :]
         summed = addend if summed is None else summed + addend
     return summed
 
@@ -158,6 +158,21 @@
     up = (jnp.where(inside_up, lon + 1, lon + 1 - parts), jnp.where(inside_up, lat, lat + 1))
     down = (jnp.where(inside_down, lon - 1, lon + parts - 1), jnp.where(inside_down, lat, lat - 1))
     return has_up, up, has_down, down
+
+
+TOP = 8
+
+
+def entry_padded(x_ref, matrix_ref, padded_ref, *scratch, **kw):
+    rows = scratch[1].shape[1]
+    low, high = scratch[4].shape[1], scratch[5].shape[1]
+    entry_kernel(
+        x_ref, matrix_ref,
+        padded_ref.at[:, pl.ds(TOP, rows), :],
+        padded_ref.at[:, pl.ds(TOP - low, low), :],
+        padded_ref.at[:, pl.ds(TOP + rows, high), :],
+        *scratch, **kw,
+    )
 
 
 def entry_kernel(x_ref, matrix_ref, field_ref, below_ref, above_ref, moved, landed, top_stage, bottom_stage,
@@ -343,10 +358,10 @@
     below_shape = (levels, 2, devices * lane)
     above_shape = (levels, 3, devices * lane)
     return pl.pallas_call(
-        functools.partial(entry_kernel, src_at=src_at, dst_at=dst_at, parts=parts),
-        out_shape=tuple(jax.ShapeDtypeStruct(shape, block.dtype) for shape in (field_shape, below_shape, above_shape)),
+        functools.partial(entry_padded, src_at=src_at, dst_at=dst_at, parts=parts),
+        out_shape=jax.ShapeDtypeStruct((levels, 2 * TOP + count, devices * lane), block.dtype),
         in_specs=[vmem, vmem],
-        out_specs=(hbm, hbm, hbm),
+        out_specs=hbm,
         scratch_shapes=[
             pltpu.VMEM(block.shape, block.dtype),
             pltpu.VMEM(field_shape, block.dtype),
@@ -434,18 +449,19 @@
 
 def per_device(tracers, lon_shift, lon_frac, lat_shift, lat_frac, remap_frac, diffusivity):
     rows = tracers.shape[1]
-    field, below, above = to_columns(tracers)
-    count = field.shape[1]
+    first = to_columns(tracers)
+    count = first.shape[1] - 2 * TOP
+    field = first[:, TOP : TOP + count]
     width = field.shape[2]
     lon_shift, lon_frac, lat_shift, lat_frac, remap_frac, diffusivity = (
         own_rows(v, count) for v in (lon_shift, lon_frac, lat_shift, lat_frac, remap_frac, diffusivity)
     )
     for time_step in range(STEPS):
         if time_step == 0:
-            padded = jnp.concatenate([below[:, :1], below, field, above], axis=1)
+            padded, start = first, TOP - 2
         else:
-            padded = lat_halo(field, 3)
-        field = lat_step(padded, lat_shift[time_step], lat_frac[time_step], count)
+            padded, start = lat_halo(field, 3), 1
+        field = lat_step(padded, lat_shift[time_step], lat_frac[time_step], count, start)
         field = lon_cubic(roll_rows(field, lon_shift[time_step]), lon_frac[time_step])
         field = remap(field, remap_frac[time_step])
         field = diffuse(field, diffusivity)

time: 104 us -> 104 us (level)
  waiting for transfers between devices: 6.37 us -> 3.1 us
  other arithmetic: 17.8 us -> 20.2 us
  starting transfers between devices: 4.51 us -> 5.74 us
    ppermute x1, waiting for transfers between devices: 6.36 us -> 0.82 us  [lat_halo(): above = lax.ppermute(field[:, :width], ('lon', 'lat'), down)]
    add x2, other arithmetic: 5.73 us -> 8.14 us  [lat_step(): summed = addend if summed is None else summed + addend]
    ppermute x1, waiting for transfers between devices: 0.01 us -> 2.28 us  [lat_halo(): below = lax.ppermute(field[:, rows - width + 1:], ('lon', 'lat'), up)]
    pallas_call x1, Pallas kernels: 28.4 us -> 30 us  [run_exchange(): pl.pallas_call(functools.partial(kernel, src_at=src_at, dst_at=dst_at), o...]
    unnamed x30 -> x17, local copies, waits for them, and re-layouts: 6.09 us -> 4.5 us
  transfers between devices with their start and end apart: 2 -> 2, of which waited for: 1 -> 2; matrix products, arithmetic and copies ran while one was open for 0% -> 0% of each run, Pallas kernels for 0% -> 0%
where the time goes in v15:
time: 104 us
  Pallas kernels  62.9 us (60%)
  other arithmetic  20.2 us (19%)
  local copies, waits for them, and re-layouts  11.1 us (11%)
  starting transfers between devices  5.74 us (6%)
  waiting for transfers between devices  3.1 us (3%)
    pallas_call x1, Pallas kernels, to_columns(): pl.pallas_call(functools.partial(entry_padded, src_at=src_at, dst_at=dst_...  32.9 us
    pallas_call x1, Pallas kernels, run_exchange(): pl.pallas_call(functools.partial(kernel, src_at=src_at, dst_at=dst_at), o...  30 us
    add x2, other arithmetic, lat_step(): summed = addend if summed is None else summed + addend  8.14 us
    select_n x18, other arithmetic, roll_rows(): current = jnp.where(bit_mask(amount, position), moved, current)  7.31 us
    unnamed x17, local copies, waits for them, and re-layouts  4.5 us
    ppermute x1, starting transfers between devices, lat_halo(): above = lax.ppermute(field[:, :width], ('lon', 'lat'), down)  3.16 us
    ppermute x1, starting transfers between devices, lat_halo(): below = lax.ppermute(field[:, rows - width + 1:], ('lon', 'lat'), up)  2.58 us
    slice x8, local copies, waits for them, and re-layouts, lon_cubic(): taps = [jnp.roll(shifted, PAIR * (1 - p), axis=2) for p in range(4)]  2.29 us
  transfers between devices with their start and end apart: 2, of which 2 were waited for; matrix products, arithmetic and copies ran while one was open for 0% of the time, Pallas kernels for 0%

profile of v15, /device:TPU:25, one launch (start us, length us, event | category | flops | bytes accessed | tf_op | source)
XLA Modules:
  0.0 103.8 jit_solution(8193543612863760126)
XLA Ops:
  0.0 0.9 constant_dynamic-slice_fusion
  0.9 0.9 constant_dynamic-slice_fusion.1
  1.8 32.9 %shard_map.91 = f32[12,32,2048]{2,1,0:T(8,128)} custom-call(f32[12,64,512]{2,1,0:T(8,128)} %x_ref.1, bf16[512,512]{1,0:T(8,128)(2,1)} %constant.339.clone.matrix_ref), custom_call_target="tpu_custom_call" | custom-call | tf_op jit(solution)/shard_map/pallas_call | solution.py:360
  34.7 6.4 %multiply_add_fusion = f32[12,16,2048]{2,1,0:T(8,128)S(1)} fusion(f32[12,32,2048]{2,1,0:T(8,128)} %shard_map.91, f32[12,16]{1,0:T(8,128)S(1)} %get-tuple-element.78, f32[12,16]{1,0:T(8,128)S(1)} %get-tuple-element.77, f32[12,16]{1,0:T(8,128)S(1)} %get-tuple-element.76, f32[12,16]{1,0:T(8,128)S(1)} %get-tuple-element.75, f32[12,16]{1,0:T(8,128)S(1)} %get-tuple-element.74, ...), kind=kLoop, calls=%fused_computation.63 | loop fusion | flops 4325376 | bytes 11014656 | tf_op jit(solution)/shard_map/add | solution.py:52
  41.4 0.1 fusion.1
  41.5 0.5 fusion.3
  42.1 0.5 maximum_select_fusion
  42.6 0.1 slice.540
  42.7 0.5 maximum_select_fusion.1
  43.3 0.5 maximum_select_fusion.2
  43.8 0.1 slice.544
  43.9 0.5 maximum_select_fusion.3
  44.5 0.5 maximum_select_fusion.4
  45.0 0.1 slice.549
  45.2 0.2 maximum_select_fusion.5
  45.4 0.1 slice.551
  45.5 0.2 maximum_select_fusion.6
  45.8 0.1 slice.553
  45.9 0.2 maximum_select_fusion.7
  46.1 0.6 fusion.202
  46.7 0.5 slice.558
  47.2 0.1 fusion.203
  47.3 0.9 fusion.19
  48.3 0.1 slice.560
  48.4 0.6 copy-done.2
  49.0 0.1 constant_dynamic-slice_fusion.3
  49.3 0.3 fusion.20
  49.6 0.4 subtract_dynamic-update-slice_fusion.1
  50.4 0.1 constant_dynamic-update-slice_fusion.1
  50.5 0.1 constant_dynamic-update-slice_fusion
  50.7 3.2 %collective-permute-start.1 = (f32[12,3,2048]{2,1,0:T(4,128)S(1)}, f32[12,3,2048]{2,1,0:T(4,128)S(1)}, u32[]{:S(2)}, u32[]{:S(2)}) collective-permute-start(f32[12,3,2048]{2,1,0:T(4,128)S(1)} %slice.588), channel_id=1, source_target_pairs={{8,0},{16,8},{24,16},{1,24},{40,32},{48,40},{56,48},{33,56},{72,64... | collective-permute-start | bytes 884744 | tf_op jit(solution)/shard_map/ppermute | solution.py:419
  53.8 0.1 slice.585
  53.9 2.6 %collective-permute-start = (f32[12,2,2048]{2,1,0:T(2,128)S(1)}, f32[12,2,2048]{2,1,0:T(2,128)S(1)}, u32[]{:S(2)}, u32[]{:S(2)}) collective-permute-start(f32[12,2,2048]{2,1,0:T(2,128)S(1)} %slice.585), channel_id=1, source_target_pairs={{0,8},{8,16},{16,24},{24,1},{32,40},{40,48},{48,56},{56,33},{64,72... | collective-permute-start | bytes 589832 | tf_op jit(solution)/shard_map/ppermute | solution.py:418
  56.7 2.3 %collective-permute-done = f32[12,2,2048]{2,1,0:T(2,128)S(1)} collective-permute-done((f32[12,2,2048]{2,1,0:T(2,128)S(1)}, f32[12,2,2048]{2,1,0:T(2,128)S(1)}, u32[]{:S(2)}, u32[]{:S(2)}) %collective-permute-start) | collective-permute-done | bytes 196640 | tf_op jit(solution)/shard_map/ppermute | solution.py:418
  58.9 0.8 collective-permute-done.1
  59.8 1.7 %fusion.10 = f32[12,16,2048]{2,1,0:T(8,128)S(1)} fusion(f32[12,2,2048]{2,1,0:T(2,128)S(1)} %collective-permute-done, f32[12,16,2048]{2,1,0:T(8,128)S(1)} %constant_dynamic-update-slice_fusion, f32[12,3,2048]{2,1,0:T(4,128)S(1)} %collective-permute-done.1, f32[12,16]{1,0:T(8,128)S(1)} %get-tuple-element.68, f32[12,16]{1,0:T(8,128)S(1)} %get-tuple-element.67, ...), kind=kLoop, calls=%fused_computation.22 | loop fusion | flops 6291456 | bytes 3641856 | tf_op jit(solution)/shard_map/add | solution.py:52
  61.6 0.1 slice.593
  61.7 0.1 fusion
  61.8 0.5 fusion.2
  62.3 0.1 slice.598
  62.4 0.5 maximum_select_fusion.8
  62.9 0.1 slice.600
  63.0 0.5 maximum_select_fusion.9
  63.6 0.5 maximum_select_fusion.10
  64.2 0.5 maximum_select_fusion.11
  64.8 0.5 maximum_select_fusion.12
  65.3 0.1 slice.609
  65.5 0.2 maximum_select_fusion.13
  65.7 0.1 slice.611
  65.8 0.2 maximum_select_fusion.14
  66.1 0.1 slice.613
  66.2 0.2 maximum_select_fusion.15
  66.4 0.6 fusion.200
  67.0 0.5 slice.618
  67.5 0.1 fusion.201
  67.6 0.9 fusion.23
  68.5 0.1 slice.620
  68.7 0.3 fusion.24
  68.9 0.4 subtract_dynamic-update-slice_fusion
  69.8 0.1 constant_dynamic-update-slice_fusion.12
  69.9 0.1 constant_dynamic-update-slice_fusion.11.src_ref
  70.0 1.1 %copy-done = f32[12,16,2048]{2,1,0:T(8,128)} copy-done((f32[12,16,2048]{2,1,0:T(8,128)}, f32[12,16,2048]{2,1,0:T(8,128)S(1)}, u32[]{:S(2)}) %copy-start) | copy-done | bytes 1572888
  71.1 30.0 %shard_map.92 = f32[12,64,512]{2,1,0:T(8,128)} custom-call(f32[12,16,2048]{2,1,0:T(8,128)} %copy-done, bf16[512,512]{1,0:T(8,128)(2,1)} %constant.340.clone.matrix_ref), custom_call_target="tpu_custom_call" | custom-call | tf_op jit(solution)/shard_map/pallas_call | solution.py:326
  101.2 2.7 %copy.561 = f32[12,64,512]{2,1,0:T(8,128)} copy(f32[12,64,512]{2,1,0:T(8,128)} %shard_map.92) | data formatting | bytes 3145728
  (55 shorter events, 2.2 us)
Async XLA Ops:
  48.3 0.7 copy-start.2
  48.3 0.8 copy-start.1
  50.7 9.1 %collective-permute-start.1 = (f32[12,3,2048]{2,1,0:T(4,128)S(1)}, f32[12,3,2048]{2,1,0:T(4,128)S(1)}, u32[]{:S(2)}, u32[]{:S(2)}) collective-permute-start(f32[12,3,2048]{2,1,0:T(4,128)S(1)} %slice.588), channel_id=1, source_target_pairs={{8,0},{16,8},{24,16},{1,24},{40,32},{48,40},{56,48},{33,56},{72,64... | collective-permute-start | bytes 884744 | tf_op jit(solution)/shard_map/ppermute | solution.py:419
  53.9 5.0 %collective-permute-start = (f32[12,2,2048]{2,1,0:T(2,128)S(1)}, f32[12,2,2048]{2,1,0:T(2,128)S(1)}, u32[]{:S(2)}, u32[]{:S(2)}) collective-permute-start(f32[12,2,2048]{2,1,0:T(2,128)S(1)} %slice.585), channel_id=1, source_target_pairs={{0,8},{8,16},{16,24},{24,1},{32,40},{40,48},{48,56},{56,33},{64,72... | collective-permute-start | bytes 589832 | tf_op jit(solution)/shard_map/ppermute | solution.py:418
  70.0 1.1 %copy-start = (f32[12,16,2048]{2,1,0:T(8,128)}, f32[12,16,2048]{2,1,0:T(8,128)S(1)}, u32[]{:S(2)}) copy-start(f32[12,16,2048]{2,1,0:T(8,128)S(1)} %constant_dynamic-update-slice_fusion.11.src_ref) | copy-start | bytes 4718596

commit v16 on v13

--- a/solution.py
+++ b/solution.py
@@ -51,6 +51,42 @@
         addend = coeff[:, :, None] * padded[:, 1 + place_index : 1 + place_index + row_count, :]
         summed = addend if summed is None else summed + addend
     return summed
+
+
+def lat_split(field, below, above, offset, fraction):
+    rows = field.shape[1]
+    low, high = below.shape[1], above.shape[1]
+    weights = cubic_weights(fraction)
+    coeffs = []
+    for place_index in range(6):
+        row_delta = place_index - 2
+        coeff = jnp.zeros_like(fraction)
+        for tap_index in range(4):
+            coeff = coeff + jnp.where(offset == tap_index - 1 - row_delta, weights[tap_index], 0.0)
+        coeffs.append(coeff)
+    padded = jnp.pad(field, ((0, 0), (low, high), (0, 0)))
+    summed = None
+    for place_index in range(6):
+        addend = coeffs[place_index][:, :, None] * padded[:, place_index : place_index + rows, :]
+        summed = addend if summed is None else summed + addend
+    low_fix = []
+    for row in range(low):
+        total = None
+        for place_index in range(low - row):
+            term = coeffs[place_index][:, row, None] * below[:, row + place_index]
+            total = term if total is None else total + term
+        low_fix.append(total)
+    high_fix = []
+    for row in range(rows - high, rows):
+        total = None
+        for place_index in range(6):
+            source = row + place_index - low - rows
+            if 0 <= source < high:
+                term = coeffs[place_index][:, row, None] * above[:, source]
+                total = term if total is None else total + term
+        high_fix.append(total)
+    summed = summed.at[:, :low].add(jnp.stack(low_fix, axis=1))
+    return summed.at[:, rows - high :].add(jnp.stack(high_fix, axis=1))
 
 
 def lon_step(wrapped, fraction, tracer_count):
@@ -442,10 +478,10 @@
     )
     for time_step in range(STEPS):
         if time_step == 0:
-            padded = jnp.concatenate([below[:, :1], below, field, above], axis=1)
+            field = lat_split(field, below, above, lat_shift[time_step], lat_frac[time_step])
         else:
             padded = lat_halo(field, 3)
-        field = lat_step(padded, lat_shift[time_step], lat_frac[time_step], count)
+            field = lat_step(padded, lat_shift[time_step], lat_frac[time_step], count)
         field = lon_cubic(roll_rows(field, lon_shift[time_step]), lon_frac[time_step])
         field = remap(field, remap_frac[time_step])
         field = diffuse(field, diffusivity)

time: 104 us -> 108 us (1.038); the launches traced: 103 us -> 108 us
  other arithmetic: 17.8 us -> 21.3 us
  waiting for transfers between devices: 6.37 us -> 3.1 us
  Pallas kernels: 62 us -> 63.9 us
  local copies, waits for them, and re-layouts: 11.2 us -> 13 us
  starting transfers between devices: 4.51 us -> 5.74 us
    add x0 -> x4, other arithmetic: none -> 6.71 us  [the longest x1 6.11 us: lat_split(): summed = addend if summed is None else summed + addend]
    ppermute x1, waiting for transfers between devices: 6.36 us -> 0.82 us  [lat_halo(): above = lax.ppermute(field[:, :width], ('lon', 'lat'), down)]
    add x2 -> x1, other arithmetic: 5.73 us -> 1.73 us  [lat_step(): summed = addend if summed is None else summed + addend]
    ppermute x1, waiting for transfers between devices: 0.01 us -> 2.28 us  [lat_halo(): below = lax.ppermute(field[:, rows - width + 1:], ('lon', 'lat'), up)]
    pallas_call x1, Pallas kernels: 28.4 us -> 30.2 us  [run_exchange(): pl.pallas_call(functools.partial(kernel, src_at=src_at, dst_at=dst_at), o...]
    unnamed x30 -> x21, local copies, waits for them, and re-layouts: 6.09 us -> 4.5 us
    ppermute x1, starting transfers between devices: 1.92 us -> 3.44 us  [lat_halo(): below = lax.ppermute(field[:, rows - width + 1:], ('lon', 'lat'), up)]
  transfers between devices with their start and end apart: 2 -> 2, of which waited for: 1 -> 2; matrix products, arithmetic and copies ran while one was open for 0% -> 0% of each run, Pallas kernels for 0% -> 0%
where the time goes in v16:
time: 108 us
  Pallas kernels  63.9 us (59%)
  other arithmetic  21.3 us (20%)
  local copies, waits for them, and re-layouts  13 us (12%)
  starting transfers between devices  5.74 us (5%)
  waiting for transfers between devices  3.1 us (3%)
    pallas_call x1, Pallas kernels, to_columns(): pl.pallas_call(functools.partial(entry_kernel, src_at=src_at, dst_at=dst_...  33.7 us
    pallas_call x1, Pallas kernels, run_exchange(): pl.pallas_call(functools.partial(kernel, src_at=src_at, dst_at=dst_at), o...  30.2 us
    select_n x18, other arithmetic, roll_rows(): current = jnp.where(bit_mask(amount, position), moved, current)  7.31 us
    add x1, other arithmetic, lat_split(): summed = addend if summed is None else summed + addend  6.11 us
    unnamed x21, local copies, waits for them, and re-layouts  4.5 us
    ppermute x1, starting transfers between devices, lat_halo(): below = lax.ppermute(field[:, rows - width + 1:], ('lon', 'lat'), up)  3.44 us
    ppermute x1, starting transfers between devices, lat_halo(): above = lax.ppermute(field[:, :width], ('lon', 'lat'), down)  2.3 us
    slice x8, local copies, waits for them, and re-layouts, lon_cubic(): taps = [jnp.roll(shifted, PAIR * (1 - p), axis=2) for p in range(4)]  2.29 us
  transfers between devices with their start and end apart: 2, of which 2 were waited for; matrix products, arithmetic and copies ran while one was open for 0% of the time, Pallas kernels for 0%

profile of v16, /device:TPU:25, one launch (start us, length us, event | category | flops | bytes accessed | tf_op | source)
XLA Modules:
  0.0 107.9 jit_solution(450450856198479951)
XLA Ops:
  0.0 0.9 constant_dynamic-slice_fusion.1
  0.9 0.9 constant_dynamic-slice_fusion
  1.8 0.2 slice_reduce_fusion.8
  2.0 0.1 slice_reduce_fusion.7
  2.1 0.2 slice_reduce_fusion.5
  2.4 0.2 slice_reduce_fusion.4
  2.5 0.2 slice_reduce_fusion.2
  2.7 33.7 %shard_map.91 = (f32[12,16,2048]{2,1,0:T(8,128)}, f32[12,2,2048]{2,1,0:T(2,128)}, f32[12,3,2048]{2,1,0:T(4,128)}) custom-call(f32[12,64,512]{2,1,0:T(8,128)} %x_ref.1, bf16[512,512]{1,0:T(8,128)(2,1)} %constant.394.clone.matrix_ref), custom_call_target="tpu_custom_call" | custom-call | tf_op jit(solution)/shard_map/pallas_call | solution.py:381
  36.5 6.1 %fusion.20 = f32[12,16,2048]{2,1,0:T(8,128)S(1)} fusion(f32[12,16,2048]{2,1,0:T(8,128)} %get-tuple-element.32, f32[12,16]{1,0:T(8,128)S(1)} %get-tuple-element.120, f32[12,16]{1,0:T(8,128)S(1)} %get-tuple-element.119, f32[12,16]{1,0:T(8,128)S(1)} %get-tuple-element.118, f32[12,16]{1,0:T(8,128)S(1)} %get-tuple-element.117, ...), kind=kLoop, calls=%fused_computation.37 | loop fusion | flops 4325376 | bytes 3150336 | tf_op jit(solution)/shard_map/add | solution.py:71
  42.6 0.2 multiply_add_fusion.2
  42.9 0.3 fusion.35
  43.1 0.5 broadcast_multiply_fusion
  43.6 0.3 slice_add_fusion
  44.0 1.1 scatter-add.9
  45.4 0.1 fusion.1
  45.5 0.5 fusion.3
  46.1 0.5 maximum_select_fusion
  46.7 0.5 maximum_select_fusion.1
  47.3 0.5 maximum_select_fusion.2
  47.9 0.5 maximum_select_fusion.3
  48.5 0.5 maximum_select_fusion.4
  49.0 0.1 slice.694
  49.1 0.2 maximum_select_fusion.5
  49.3 0.1 slice.696
  49.5 0.2 maximum_select_fusion.6
  49.7 0.1 slice.698
  49.8 0.2 maximum_select_fusion.7
  50.1 0.6 fusion.213
  50.6 0.5 slice.703
  51.3 0.9 fusion.29
  52.2 0.1 slice.705
  52.3 0.6 copy-done.4
  53.2 0.3 fusion.30
  53.5 0.4 subtract_dynamic-update-slice_fusion.1
  54.3 0.1 constant_dynamic-update-slice_fusion.1
  54.6 2.3 %collective-permute-start.1 = (f32[12,3,2048]{2,1,0:T(4,128)S(1)}, f32[12,3,2048]{2,1,0:T(4,128)S(1)}, u32[]{:S(2)}, u32[]{:S(2)}) collective-permute-start(f32[12,3,2048]{2,1,0:T(4,128)S(1)} %slice.733), channel_id=1, source_target_pairs={{8,0},{16,8},{24,16},{1,24},{40,32},{48,40},{56,48},{33,56},{72,64... | collective-permute-start | bytes 884744 | tf_op jit(solution)/shard_map/ppermute | solution.py:440
  56.9 0.1 slice.730
  57.0 3.4 %collective-permute-start = (f32[12,2,2048]{2,1,0:T(2,128)S(1)}, f32[12,2,2048]{2,1,0:T(2,128)S(1)}, u32[]{:S(2)}, u32[]{:S(2)}) collective-permute-start(f32[12,2,2048]{2,1,0:T(2,128)S(1)} %slice.730), channel_id=1, source_target_pairs={{0,8},{8,16},{16,24},{24,1},{32,40},{40,48},{48,56},{56,33},{64,72... | collective-permute-start | bytes 589832 | tf_op jit(solution)/shard_map/ppermute | solution.py:439
  60.6 2.3 %collective-permute-done = f32[12,2,2048]{2,1,0:T(2,128)S(1)} collective-permute-done((f32[12,2,2048]{2,1,0:T(2,128)S(1)}, f32[12,2,2048]{2,1,0:T(2,128)S(1)}, u32[]{:S(2)}, u32[]{:S(2)}) %collective-permute-start) | collective-permute-done | bytes 196640 | tf_op jit(solution)/shard_map/ppermute | solution.py:439
  62.9 0.8 collective-permute-done.1
  63.7 1.7 %fusion.10 = f32[12,16,2048]{2,1,0:T(8,128)S(1)} fusion(f32[12,2,2048]{2,1,0:T(2,128)S(1)} %collective-permute-done, f32[12,16,2048]{2,1,0:T(8,128)S(1)} %constant_dynamic-update-slice_fusion, f32[12,3,2048]{2,1,0:T(4,128)S(1)} %collective-permute-done.1, f32[12,16]{1,0:T(8,128)S(1)} %get-tuple-element.110, f32[12,16]{1,0:T(8,128)S(1)} %get-tuple-element.109, ...), kind=kLoop, calls=%fused_computation.27 | loop fusion | flops 6291456 | bytes 3641856 | tf_op jit(solution)/shard_map/add | solution.py:52
  65.6 0.1 fusion
  65.8 0.5 fusion.2
  66.4 0.5 maximum_select_fusion.8
  67.0 0.5 maximum_select_fusion.9
  67.6 0.5 maximum_select_fusion.10
  68.2 0.5 maximum_select_fusion.11
  68.8 0.5 maximum_select_fusion.12
  69.3 0.1 slice.754
  69.4 0.2 maximum_select_fusion.13
  69.6 0.1 slice.756
  69.8 0.2 maximum_select_fusion.14
  70.0 0.1 slice.758
  70.1 0.2 maximum_select_fusion.15
  70.4 0.6 fusion.211
  70.9 0.5 slice.763
  71.5 0.9 fusion.33
  72.5 0.1 slice.765
  72.6 0.3 fusion.34
  72.9 0.4 subtract_dynamic-update-slice_fusion
  73.7 0.1 constant_dynamic-update-slice_fusion.12
  73.9 1.1 %copy-done = f32[12,16,2048]{2,1,0:T(8,128)} copy-done((f32[12,16,2048]{2,1,0:T(8,128)}, f32[12,16,2048]{2,1,0:T(8,128)S(1)}, u32[]{:S(2)}) %copy-start) | copy-done | bytes 1572888
  75.0 30.2 %shard_map.92 = f32[12,64,512]{2,1,0:T(8,128)} custom-call(f32[12,16,2048]{2,1,0:T(8,128)} %copy-done, bf16[512,512]{1,0:T(8,128)(2,1)} %constant.395.clone.matrix_ref), custom_call_target="tpu_custom_call" | custom-call | tf_op jit(solution)/shard_map/pallas_call | solution.py:347
  105.3 2.7 %copy.563 = f32[12,64,512]{2,1,0:T(8,128)} copy(f32[12,64,512]{2,1,0:T(8,128)} %shard_map.92) | data formatting | bytes 3145728
  (69 shorter events, 3.1 us)
Async XLA Ops:
  36.5 6.1 %copy-start.2 = (f32[12,2,2048]{2,1,0:T(2,128)S(1)}, f32[12,2,2048]{2,1,0:T(2,128)}, u32[]{:S(2)}) copy-start(f32[12,2,2048]{2,1,0:T(2,128)} %get-tuple-element.33) | copy-start | bytes 589828
  36.5 6.7 %copy-start.1 = (f32[12,3,2048]{2,1,0:T(4,128)S(1)}, f32[12,3,2048]{2,1,0:T(4,128)}, u32[]{:S(2)}) copy-start(f32[12,3,2048]{2,1,0:T(4,128)} %get-tuple-element.34) | copy-start | bytes 884740
  52.2 0.7 copy-start.4
  52.2 0.8 copy-start.3
  54.6 9.1 %collective-permute-start.1 = (f32[12,3,2048]{2,1,0:T(4,128)S(1)}, f32[12,3,2048]{2,1,0:T(4,128)S(1)}, u32[]{:S(2)}, u32[]{:S(2)}) collective-permute-start(f32[12,3,2048]{2,1,0:T(4,128)S(1)} %slice.733), channel_id=1, source_target_pairs={{8,0},{16,8},{24,16},{1,24},{40,32},{48,40},{56,48},{33,56},{72,64... | collective-permute-start | bytes 884744 | tf_op jit(solution)/shard_map/ppermute | solution.py:440
  57.0 5.9 %collective-permute-start = (f32[12,2,2048]{2,1,0:T(2,128)S(1)}, f32[12,2,2048]{2,1,0:T(2,128)S(1)}, u32[]{:S(2)}, u32[]{:S(2)}) collective-permute-start(f32[12,2,2048]{2,1,0:T(2,128)S(1)} %slice.730), channel_id=1, source_target_pairs={{0,8},{8,16},{16,24},{24,1},{32,40},{40,48},{48,56},{56,33},{64,72... | collective-permute-start | bytes 589832 | tf_op jit(solution)/shard_map/ppermute | solution.py:439
  73.9 1.1 %copy-start = (f32[12,16,2048]{2,1,0:T(8,128)}, f32[12,16,2048]{2,1,0:T(8,128)S(1)}, u32[]{:S(2)}) copy-start(f32[12,16,2048]{2,1,0:T(8,128)S(1)} %constant_dynamic-update-slice_fusion.11.src_ref) | copy-start | bytes 4718596

commit v17 on v13

--- a/solution.py
+++ b/solution.py
@@ -40,7 +40,7 @@
     return (w_zero, w_one, w_two, w_three)
 
 
-def lat_step(padded, offset, fraction, row_count):
+def lat_step(padded, offset, fraction, row_count, first=1):
     weights = cubic_weights(fraction)
     summed = None
     for place_index in range(6):
@@ -48,7 +48,7 @@
         coeff = jnp.zeros_like(fraction)
         for tap_index in range(4):
             coeff = coeff + jnp.where(offset == tap_index - 1 - row_delta, weights[tap_index], 0.0)
-        addend = coeff[:, :, None] * padded[:, 1 + place_index : 1 + place_index + row_count, :]
+        addend = coeff[:, :, None] * padded[:, first + place_index : first + place_index + row_count, :]
         summed = addend if summed is None else summed + addend
     return summed
 
@@ -402,7 +402,7 @@
     rows = field.shape[1]
     below = lax.ppermute(field[:, rows - width + 1 :], ("lon", "lat"), up)
     above = lax.ppermute(field[:, :width], ("lon", "lat"), down)
-    return jnp.concatenate([below[:, :1], below, field, above], axis=1)
+    return jnp.concatenate([below, field, above], axis=1)
 
 
 def roll_rows(field, shift):
@@ -445,7 +445,7 @@
             padded = jnp.concatenate([below[:, :1], below, field, above], axis=1)
         else:
             padded = lat_halo(field, 3)
-        field = lat_step(padded, lat_shift[time_step], lat_frac[time_step], count)
+        field = lat_step(padded, lat_shift[time_step], lat_frac[time_step], count, padded.shape[1] - count - 5)
         field = lon_cubic(roll_rows(field, lon_shift[time_step]), lon_frac[time_step])
         field = remap(field, remap_frac[time_step])
         field = diffuse(field, diffusivity)

time: 104 us -> 104 us (level)
  no operation moved by 1% of the time
where the time goes in v17:
time: 104 us; the launch traced here: 103 us
  Pallas kernels  62 us (60%)
  other arithmetic  17.8 us (17%)
  local copies, waits for them, and re-layouts  11.2 us (11%)
  waiting for transfers between devices  6.37 us (6%)
  starting transfers between devices  4.51 us (4%)
    pallas_call x1, Pallas kernels, to_columns(): pl.pallas_call(functools.partial(entry_kernel, src_at=src_at, dst_at=dst_...  33.6 us
    pallas_call x1, Pallas kernels, run_exchange(): pl.pallas_call(functools.partial(kernel, src_at=src_at, dst_at=dst_at), o...  28.4 us
    select_n x18, other arithmetic, roll_rows(): current = jnp.where(bit_mask(amount, position), moved, current)  7.32 us
    ppermute x1, waiting for transfers between devices, lat_halo(): above = lax.ppermute(field[:, :width], ('lon', 'lat'), down)  6.36 us
    unnamed x30, local copies, waits for them, and re-layouts  6.09 us
    add x2, other arithmetic, lat_step(): summed = addend if summed is None else summed + addend  5.73 us
    ppermute x1, starting transfers between devices, lat_halo(): above = lax.ppermute(field[:, :width], ('lon', 'lat'), down)  2.59 us
    slice x8, local copies, waits for them, and re-layouts, lon_cubic(): taps = [jnp.roll(shifted, PAIR * (1 - p), axis=2) for p in range(4)]  2.29 us
  transfers between devices with their start and end apart: 2, of which 1 were waited for; matrix products, arithmetic and copies ran while one was open for 0% of the time, Pallas kernels for 0%

profile of v17, /device:TPU:25, one launch (start us, length us, event | category | flops | bytes accessed | tf_op | source)
XLA Modules:
  0.0 102.8 jit_solution(12451029522692030745)
XLA Ops:
  0.0 33.6 %shard_map.91 = (f32[12,16,2048]{2,1,0:T(8,128)}, f32[12,2,2048]{2,1,0:T(2,128)}, f32[12,3,2048]{2,1,0:T(4,128)}) custom-call(f32[12,64,512]{2,1,0:T(8,128)} %x_ref.1, bf16[512,512]{1,0:T(8,128)(2,1)} %constant.339.clone.matrix_ref), custom_call_target="tpu_custom_call" | custom-call | tf_op jit(solution)/shard_map/pallas_call | solution.py:345
  33.7 1.6 %constant_dynamic-update-slice_fusion.1 = f32[12,19,2048]{2,1,0:T(8,128)S(1)} fusion(f32[12,16,2048]{2,1,0:T(8,128)} %get-tuple-element.9), kind=kLoop, calls=%fused_computation.146 | loop fusion | bytes 3145728
  35.3 0.1 constant_dynamic-update-slice_fusion
  35.5 0.1 constant_dynamic-slice_fusion
  35.6 0.1 constant_dynamic-slice_fusion.1
  35.8 4.0 %fusion.17 = f32[12,16,2048]{2,1,0:T(8,128)S(1)} fusion(f32[12,2,2048]{2,1,0:T(2,128)S(1)} %copy-done.2, f32[12,16,2048]{2,1,0:T(8,128)} %get-tuple-element.9, f32[12,19,2048]{2,1,0:T(8,128)S(1)} %constant_dynamic-update-slice_fusion, f32[12,16]{1,0:T(8,128)S(1)} %get-tuple-element.84, f32[12,16]{1,0:T(8,128)S(1)} %get-tuple-element.83, ...), kind=kLoop, calls=%fused_computation.31 | loop fusion | flops 5111808 | bytes 8065536 | tf_op jit(solution)/shard_map/add | solution.py:52
  39.9 0.1 slice.539
  40.1 0.1 fusion.1
  40.2 0.5 fusion.3
  40.8 0.5 maximum_select_fusion
  41.3 0.1 slice.546
  41.4 0.5 maximum_select_fusion.1
  42.0 0.5 maximum_select_fusion.2
  42.5 0.1 slice.550
  42.6 0.5 maximum_select_fusion.3
  43.2 0.5 maximum_select_fusion.4
  43.7 0.1 slice.555
  43.8 0.2 maximum_select_fusion.5
  44.1 0.1 slice.557
  44.2 0.2 maximum_select_fusion.6
  44.4 0.1 slice.559
  44.6 0.2 maximum_select_fusion.7
  44.8 0.6 fusion.210
  45.4 0.1 fusion.211
  45.5 0.5 slice.564
  46.0 0.9 fusion.27
  47.0 0.1 slice.566
  47.1 0.6 copy-done.4
  47.6 0.1 constant_dynamic-slice_fusion.3
  48.0 0.3 fusion.28
  48.2 0.4 subtract_dynamic-update-slice_fusion.1
  49.1 0.1 constant_dynamic-update-slice_fusion.3
  49.2 0.1 constant_dynamic-update-slice_fusion.2
  49.2 0.1 slice.591
  49.4 1.9 %collective-permute-start = (f32[12,2,2048]{2,1,0:T(2,128)S(1)}, f32[12,2,2048]{2,1,0:T(2,128)S(1)}, u32[]{:S(2)}, u32[]{:S(2)}) collective-permute-start(f32[12,2,2048]{2,1,0:T(2,128)S(1)} %slice.591), channel_id=1, source_target_pairs={{0,8},{8,16},{16,24},{24,1},{32,40},{40,48},{48,56},{56,33},{64,72... | collective-permute-start | bytes 589832 | tf_op jit(solution)/shard_map/ppermute | solution.py:403
  51.3 2.6 %collective-permute-start.1 = (f32[12,3,2048]{2,1,0:T(4,128)S(1)}, f32[12,3,2048]{2,1,0:T(4,128)S(1)}, u32[]{:S(2)}, u32[]{:S(2)}) collective-permute-start(f32[12,3,2048]{2,1,0:T(4,128)S(1)} %slice.594), channel_id=1, source_target_pairs={{8,0},{16,8},{24,16},{1,24},{40,32},{48,40},{56,48},{33,56},{72,64... | collective-permute-start | bytes 884744 | tf_op jit(solution)/shard_map/ppermute | solution.py:404
  54.1 6.4 %collective-permute-done.1 = f32[12,3,2048]{2,1,0:T(4,128)S(1)} collective-permute-done((f32[12,3,2048]{2,1,0:T(4,128)S(1)}, f32[12,3,2048]{2,1,0:T(4,128)S(1)}, u32[]{:S(2)}, u32[]{:S(2)}) %collective-permute-start.1) | collective-permute-done | bytes 294944 | tf_op jit(solution)/shard_map/ppermute | solution.py:404
  60.4 1.7 %fusion.10 = f32[12,16,2048]{2,1,0:T(8,128)S(1)} fusion(f32[12,2,2048]{2,1,0:T(2,128)S(1)} %collective-permute-done, f32[12,16,2048]{2,1,0:T(8,128)S(1)} %constant_dynamic-update-slice_fusion.2, f32[12,3,2048]{2,1,0:T(4,128)S(1)} %collective-permute-done.1, f32[12,16]{1,0:T(8,128)S(1)} %get-tuple-element.74, f32[12,16]{1,0:T(8,128)S(1)} %get-tuple-element.73, ...), kind=kLoop, calls=%fused_computation.24 | loop fusion | flops 6291456 | bytes 3641856 | tf_op jit(solution)/shard_map/add | solution.py:52
  62.3 0.1 slice.599
  62.4 0.1 fusion
  62.5 0.5 fusion.2
  63.1 0.5 maximum_select_fusion.8
  63.7 0.5 maximum_select_fusion.9
  64.3 0.5 maximum_select_fusion.10
  64.9 0.5 maximum_select_fusion.11
  65.5 0.5 maximum_select_fusion.12
  66.0 0.1 slice.615
  66.2 0.2 maximum_select_fusion.13
  66.4 0.1 slice.617
  66.5 0.2 maximum_select_fusion.14
  66.8 0.1 slice.619
  66.9 0.2 maximum_select_fusion.15
  67.1 0.6 fusion.208
  67.7 0.1 fusion.209
  67.8 0.5 slice.624
  68.3 0.9 fusion.31
  69.3 0.1 slice.626
  69.4 0.3 fusion.32
  69.6 0.4 subtract_dynamic-update-slice_fusion
  70.5 0.1 constant_dynamic-update-slice_fusion.14
  70.6 0.1 constant_dynamic-update-slice_fusion.13.src_ref
  70.7 1.1 %copy-done = f32[12,16,2048]{2,1,0:T(8,128)} copy-done((f32[12,16,2048]{2,1,0:T(8,128)}, f32[12,16,2048]{2,1,0:T(8,128)S(1)}, u32[]{:S(2)}) %copy-start) | copy-done | bytes 1572888
  71.8 28.4 %shard_map.92 = f32[12,64,512]{2,1,0:T(8,128)} custom-call(f32[12,16,2048]{2,1,0:T(8,128)} %copy-done, bf16[512,512]{1,0:T(8,128)(2,1)} %constant.340.clone.matrix_ref), custom_call_target="tpu_custom_call" | custom-call | tf_op jit(solution)/shard_map/pallas_call | solution.py:311
  100.2 2.7 %copy.562 = f32[12,64,512]{2,1,0:T(8,128)} copy(f32[12,64,512]{2,1,0:T(8,128)} %shard_map.92) | data formatting | bytes 3145728
  (69 shorter events, 2.4 us)
Async XLA Ops:
  33.7 1.6 %copy-start.1 = (f32[12,3,2048]{2,1,0:T(4,128)S(1)}, f32[12,3,2048]{2,1,0:T(4,128)}, u32[]{:S(2)}) copy-start(f32[12,3,2048]{2,1,0:T(4,128)} %get-tuple-element.10) | copy-start | bytes 884740
  33.7 1.8 %copy-start.5 = (s32[2,12,64]{2,0,1:T(2,128)S(1)}, s32[2,12,64]{2,0,1:T(2,128)}, u32[]{:S(2)}) copy-start(s32[2,12,64]{2,0,1:T(2,128)} %param.10) | copy-start | bytes 18436
  33.7 1.8 %copy-start.6 = (s32[2,12,64]{2,0,1:T(2,128)S(1)}, s32[2,12,64]{2,0,1:T(2,128)}, u32[]{:S(2)}) copy-start(s32[2,12,64]{2,0,1:T(2,128)} %param.12) | copy-start | bytes 18436
  33.7 1.9 %copy-start.7 = (f32[2,12,64]{2,0,1:T(2,128)S(1)}, f32[2,12,64]{2,0,1:T(2,128)}, u32[]{:S(2)}) copy-start(f32[2,12,64]{2,0,1:T(2,128)} %param.13) | copy-start | bytes 18436
  33.7 1.9 %copy-start.8 = (f32[2,12,64]{2,0,1:T(2,128)S(1)}, f32[2,12,64]{2,0,1:T(2,128)}, u32[]{:S(2)}) copy-start(f32[2,12,64]{2,0,1:T(2,128)} %param.11) | copy-start | bytes 18436
  33.7 2.0 %copy-start.2 = (f32[12,2,2048]{2,1,0:T(2,128)S(1)}, f32[12,2,2048]{2,1,0:T(2,128)}, u32[]{:S(2)}) copy-start(f32[12,2,2048]{2,1,0:T(2,128)} %get-tuple-element.8) | copy-start | bytes 589828
  46.9 0.7 copy-start.4
  46.9 0.8 copy-start.3
  49.4 4.7 %collective-permute-start = (f32[12,2,2048]{2,1,0:T(2,128)S(1)}, f32[12,2,2048]{2,1,0:T(2,128)S(1)}, u32[]{:S(2)}, u32[]{:S(2)}) collective-permute-start(f32[12,2,2048]{2,1,0:T(2,128)S(1)} %slice.591), channel_id=1, source_target_pairs={{0,8},{8,16},{16,24},{24,1},{32,40},{40,48},{48,56},{56,33},{64,72... | collective-permute-start | bytes 589832 | tf_op jit(solution)/shard_map/ppermute | solution.py:403
  51.3 9.1 %collective-permute-start.1 = (f32[12,3,2048]{2,1,0:T(4,128)S(1)}, f32[12,3,2048]{2,1,0:T(4,128)S(1)}, u32[]{:S(2)}, u32[]{:S(2)}) collective-permute-start(f32[12,3,2048]{2,1,0:T(4,128)S(1)} %slice.594), channel_id=1, source_target_pairs={{8,0},{16,8},{24,16},{1,24},{40,32},{48,40},{56,48},{33,56},{72,64... | collective-permute-start | bytes 884744 | tf_op jit(solution)/shard_map/ppermute | solution.py:404
  70.7 1.1 %copy-start = (f32[12,16,2048]{2,1,0:T(8,128)}, f32[12,16,2048]{2,1,0:T(8,128)S(1)}, u32[]{:S(2)}) copy-start(f32[12,16,2048]{2,1,0:T(8,128)S(1)} %constant_dynamic-update-slice_fusion.13.src_ref) | copy-start | bytes 4718596

commit v18 on v14

--- a/solution.py
+++ b/solution.py
@@ -262,7 +262,7 @@
         to_up.wait_recv()
 
 
-def exit_kernel(src_ref, matrix_ref, out_ref, landed, send_sem, recv_sem, local_sem, *, src_at, dst_at):
+def exit_kernel(src_ref, matrix_ref, out_ref, landed, result, send_sem, recv_sem, local_sem, store_sem, *, src_at, dst_at):
     count = lax.axis_size("lon")
     me = lax.axis_index("lon")
     lat = lax.axis_index("lat")
@@ -272,6 +272,7 @@
     pl.semaphore_wait(barrier, count - 1)
     copies = []
     locals_ = []
+    stores = []
     for chunk in range(CHUNKS):
         part = pl.ds(chunk * per, per)
         row = []
@@ -297,28 +298,33 @@
         locals_[chunk].wait()
 
         def body(k, carry):
-            out_ref[k] = permute_block(landed[k], matrix_ref[...])
+            result[k] = permute_block(landed[k], matrix_ref[...])
             return carry
 
         lax.fori_loop(chunk * per, (chunk + 1) * per, body, 0)
+        part = pl.ds(chunk * per, per)
+        store = pltpu.make_async_copy(result.at[part], out_ref.at[part], store_sem.at[chunk])
+        store.start()
+        stores.append(store)
+    for store in stores:
+        store.wait()
     for row in copies:
         for copy in row:
             copy.wait_send()
 
 
-def run_exchange(kernel, operand, matrix, out_shape, src_spec, out_spec, scratch, src_at, dst_at, ident):
+def run_exchange(kernel, operand, matrix, out_shape, src_spec, out_spec, scratch, src_at, dst_at, ident, extra=()):
     count = lax.axis_size("lon")
     return pl.pallas_call(
         functools.partial(kernel, src_at=src_at, dst_at=dst_at),
         out_shape=jax.ShapeDtypeStruct(out_shape, operand.dtype),
         in_specs=[src_spec, pl.BlockSpec(memory_space=pltpu.VMEM)],
         out_specs=out_spec,
-        scratch_shapes=[
-            pltpu.VMEM(scratch, operand.dtype),
+        scratch_shapes=[pltpu.VMEM(scratch, operand.dtype)] * (1 + len(extra)) + [
             pltpu.SemaphoreType.DMA((CHUNKS, count)),
             pltpu.SemaphoreType.DMA((CHUNKS, count)),
             pltpu.SemaphoreType.DMA((CHUNKS,)),
-        ],
+        ] + [pltpu.SemaphoreType.DMA((CHUNKS,)) for _ in extra],
         compiler_params=pltpu.CompilerParams(collective_id=ident, has_side_effects=True),
     )(operand, matrix)
 
@@ -381,8 +387,8 @@
     shape = (levels, rows, cells * NTR)
     return run_exchange(
         exit_kernel, field, permutation(pair_order(cells), True), shape,
-        pl.BlockSpec(memory_space=pltpu.VMEM), pl.BlockSpec(memory_space=pltpu.VMEM), shape,
-        src_at, dst_at, 1,
+        pl.BlockSpec(memory_space=pl.ANY), pl.BlockSpec(memory_space=pl.ANY), shape,
+        src_at, dst_at, 1, extra=("result",),
     )
 
 

time: 104 us -> 103 us (level)
  no operation moved by 1% of the time
where the time goes in v18:
time: 103 us; the launch traced here: 102 us
  Pallas kernels  61.6 us (60%)
  other arithmetic  17.8 us (17%)
  local copies, waits for them, and re-layouts  11.2 us (11%)
  waiting for transfers between devices  6.37 us (6%)
  starting transfers between devices  4.51 us (4%)
    pallas_call x1, Pallas kernels, to_columns(): pl.pallas_call(functools.partial(entry_kernel, src_at=src_at, dst_at=dst_...  33.6 us
    pallas_call x1, Pallas kernels, run_exchange(): pl.pallas_call(functools.partial(kernel, src_at=src_at, dst_at=dst_at), o...  28 us
    select_n x18, other arithmetic, roll_rows(): current = jnp.where(bit_mask(amount, position), moved, current)  7.32 us
    ppermute x1, waiting for transfers between devices, lat_halo(): above = lax.ppermute(field[:, :width], ('lon', 'lat'), down)  6.36 us
    unnamed x30, local copies, waits for them, and re-layouts  6.09 us
    add x2, other arithmetic, lat_step(): summed = addend if summed is None else summed + addend  5.73 us
    ppermute x1, starting transfers between devices, lat_halo(): above = lax.ppermute(field[:, :width], ('lon', 'lat'), down)  2.59 us
    slice x8, local copies, waits for them, and re-layouts, lon_cubic(): taps = [jnp.roll(shifted, PAIR * (1 - p), axis=2) for p in range(4)]  2.29 us
  transfers between devices with their start and end apart: 2, of which 1 were waited for; matrix products, arithmetic and copies ran while one was open for 0% of the time, Pallas kernels for 0%

profile of v18, /device:TPU:25, one launch (start us, length us, event | category | flops | bytes accessed | tf_op | source)
XLA Modules:
  0.0 102.4 jit_solution(6161032852785322589)
XLA Ops:
  0.0 33.6 %shard_map.91 = (f32[12,16,2048]{2,1,0:T(8,128)}, f32[12,2,2048]{2,1,0:T(2,128)}, f32[12,3,2048]{2,1,0:T(4,128)}) custom-call(f32[12,64,512]{2,1,0:T(8,128)} %x_ref.1, bf16[512,512]{1,0:T(8,128)(2,1)} %constant.339.clone.matrix_ref), custom_call_target="tpu_custom_call" | custom-call | tf_op jit(solution)/shard_map/pallas_call | solution.py:351
  33.7 1.6 %constant_dynamic-update-slice_fusion.1 = f32[12,19,2048]{2,1,0:T(8,128)S(1)} fusion(f32[12,16,2048]{2,1,0:T(8,128)} %get-tuple-element.9), kind=kLoop, calls=%fused_computation.146 | loop fusion | bytes 3145728
  35.3 0.1 constant_dynamic-update-slice_fusion
  35.5 0.1 constant_dynamic-slice_fusion
  35.6 0.1 constant_dynamic-slice_fusion.1
  35.8 4.0 %fusion.17 = f32[12,16,2048]{2,1,0:T(8,128)S(1)} fusion(f32[12,2,2048]{2,1,0:T(2,128)S(1)} %copy-done.2, f32[12,16,2048]{2,1,0:T(8,128)} %get-tuple-element.9, f32[12,19,2048]{2,1,0:T(8,128)S(1)} %constant_dynamic-update-slice_fusion, f32[12,16]{1,0:T(8,128)S(1)} %get-tuple-element.84, f32[12,16]{1,0:T(8,128)S(1)} %get-tuple-element.83, ...), kind=kLoop, calls=%fused_computation.31 | loop fusion | flops 5111808 | bytes 8065536 | tf_op jit(solution)/shard_map/add | solution.py:52
  39.9 0.1 slice.540
  40.1 0.1 fusion.1
  40.2 0.5 fusion.3
  40.8 0.5 maximum_select_fusion
  41.3 0.1 slice.547
  41.4 0.5 maximum_select_fusion.1
  42.0 0.5 maximum_select_fusion.2
  42.5 0.1 slice.551
  42.6 0.5 maximum_select_fusion.3
  43.2 0.5 maximum_select_fusion.4
  43.7 0.1 slice.556
  43.8 0.2 maximum_select_fusion.5
  44.1 0.1 slice.558
  44.2 0.2 maximum_select_fusion.6
  44.4 0.1 slice.560
  44.6 0.2 maximum_select_fusion.7
  44.8 0.6 fusion.210
  45.4 0.1 fusion.211
  45.5 0.5 slice.565
  46.0 0.9 fusion.27
  47.0 0.1 slice.567
  47.1 0.6 copy-done.4
  47.6 0.1 constant_dynamic-slice_fusion.3
  48.0 0.3 fusion.28
  48.2 0.4 subtract_dynamic-update-slice_fusion.1
  49.1 0.1 constant_dynamic-update-slice_fusion.3
  49.2 0.1 constant_dynamic-update-slice_fusion.2
  49.2 0.1 slice.592
  49.4 1.9 %collective-permute-start = (f32[12,2,2048]{2,1,0:T(2,128)S(1)}, f32[12,2,2048]{2,1,0:T(2,128)S(1)}, u32[]{:S(2)}, u32[]{:S(2)}) collective-permute-start(f32[12,2,2048]{2,1,0:T(2,128)S(1)} %slice.592), channel_id=1, source_target_pairs={{0,8},{8,16},{16,24},{24,1},{32,40},{40,48},{48,56},{56,33},{64,72... | collective-permute-start | bytes 589832 | tf_op jit(solution)/shard_map/ppermute | solution.py:409
  51.3 2.6 %collective-permute-start.1 = (f32[12,3,2048]{2,1,0:T(4,128)S(1)}, f32[12,3,2048]{2,1,0:T(4,128)S(1)}, u32[]{:S(2)}, u32[]{:S(2)}) collective-permute-start(f32[12,3,2048]{2,1,0:T(4,128)S(1)} %slice.595), channel_id=1, source_target_pairs={{8,0},{16,8},{24,16},{1,24},{40,32},{48,40},{56,48},{33,56},{72,64... | collective-permute-start | bytes 884744 | tf_op jit(solution)/shard_map/ppermute | solution.py:410
  54.1 6.4 %collective-permute-done.1 = f32[12,3,2048]{2,1,0:T(4,128)S(1)} collective-permute-done((f32[12,3,2048]{2,1,0:T(4,128)S(1)}, f32[12,3,2048]{2,1,0:T(4,128)S(1)}, u32[]{:S(2)}, u32[]{:S(2)}) %collective-permute-start.1) | collective-permute-done | bytes 294944 | tf_op jit(solution)/shard_map/ppermute | solution.py:410
  60.4 1.7 %fusion.10 = f32[12,16,2048]{2,1,0:T(8,128)S(1)} fusion(f32[12,2,2048]{2,1,0:T(2,128)S(1)} %collective-permute-done, f32[12,16,2048]{2,1,0:T(8,128)S(1)} %constant_dynamic-update-slice_fusion.2, f32[12,3,2048]{2,1,0:T(4,128)S(1)} %collective-permute-done.1, f32[12,16]{1,0:T(8,128)S(1)} %get-tuple-element.74, f32[12,16]{1,0:T(8,128)S(1)} %get-tuple-element.73, ...), kind=kLoop, calls=%fused_computation.24 | loop fusion | flops 6291456 | bytes 3641856 | tf_op jit(solution)/shard_map/add | solution.py:52
  62.3 0.1 slice.600
  62.4 0.1 fusion
  62.5 0.5 fusion.2
  63.1 0.5 maximum_select_fusion.8
  63.7 0.5 maximum_select_fusion.9
  64.3 0.5 maximum_select_fusion.10
  64.9 0.5 maximum_select_fusion.11
  65.5 0.5 maximum_select_fusion.12
  66.0 0.1 slice.616
  66.2 0.2 maximum_select_fusion.13
  66.4 0.1 slice.618
  66.5 0.2 maximum_select_fusion.14
  66.8 0.1 slice.620
  66.9 0.2 maximum_select_fusion.15
  67.1 0.6 fusion.208
  67.7 0.1 fusion.209
  67.8 0.5 slice.625
  68.3 0.9 fusion.31
  69.3 0.1 slice.627
  69.4 0.3 fusion.32
  69.6 0.4 subtract_dynamic-update-slice_fusion
  70.5 0.1 constant_dynamic-update-slice_fusion.14
  70.6 0.1 constant_dynamic-update-slice_fusion.13.src_ref
  70.7 1.1 %copy-done = f32[12,16,2048]{2,1,0:T(8,128)} copy-done((f32[12,16,2048]{2,1,0:T(8,128)}, f32[12,16,2048]{2,1,0:T(8,128)S(1)}, u32[]{:S(2)}) %copy-start) | copy-done | bytes 1572888
  71.8 28.0 %shard_map.92 = f32[12,64,512]{2,1,0:T(8,128)} custom-call(f32[12,16,2048]{2,1,0:T(8,128)} %copy-done, bf16[512,512]{1,0:T(8,128)(2,1)} %constant.340.clone.matrix_ref), custom_call_target="tpu_custom_call" | custom-call | tf_op jit(solution)/shard_map/pallas_call | solution.py:318
  99.8 2.7 %copy.562 = f32[12,64,512]{2,1,0:T(8,128)} copy(f32[12,64,512]{2,1,0:T(8,128)} %shard_map.92) | data formatting | bytes 3145728
  (69 shorter events, 2.4 us)
Async XLA Ops:
  33.7 1.6 %copy-start.1 = (f32[12,3,2048]{2,1,0:T(4,128)S(1)}, f32[12,3,2048]{2,1,0:T(4,128)}, u32[]{:S(2)}) copy-start(f32[12,3,2048]{2,1,0:T(4,128)} %get-tuple-element.10) | copy-start | bytes 884740
  33.7 1.8 %copy-start.5 = (s32[2,12,64]{2,0,1:T(2,128)S(1)}, s32[2,12,64]{2,0,1:T(2,128)}, u32[]{:S(2)}) copy-start(s32[2,12,64]{2,0,1:T(2,128)} %param.10) | copy-start | bytes 18436
  33.7 1.8 %copy-start.6 = (s32[2,12,64]{2,0,1:T(2,128)S(1)}, s32[2,12,64]{2,0,1:T(2,128)}, u32[]{:S(2)}) copy-start(s32[2,12,64]{2,0,1:T(2,128)} %param.12) | copy-start | bytes 18436
  33.7 1.9 %copy-start.7 = (f32[2,12,64]{2,0,1:T(2,128)S(1)}, f32[2,12,64]{2,0,1:T(2,128)}, u32[]{:S(2)}) copy-start(f32[2,12,64]{2,0,1:T(2,128)} %param.13) | copy-start | bytes 18436
  33.7 1.9 %copy-start.8 = (f32[2,12,64]{2,0,1:T(2,128)S(1)}, f32[2,12,64]{2,0,1:T(2,128)}, u32[]{:S(2)}) copy-start(f32[2,12,64]{2,0,1:T(2,128)} %param.11) | copy-start | bytes 18436
  33.7 2.0 %copy-start.2 = (f32[12,2,2048]{2,1,0:T(2,128)S(1)}, f32[12,2,2048]{2,1,0:T(2,128)}, u32[]{:S(2)}) copy-start(f32[12,2,2048]{2,1,0:T(2,128)} %get-tuple-element.8) | copy-start | bytes 589828
  46.9 0.7 copy-start.4
  46.9 0.8 copy-start.3
  49.4 4.7 %collective-permute-start = (f32[12,2,2048]{2,1,0:T(2,128)S(1)}, f32[12,2,2048]{2,1,0:T(2,128)S(1)}, u32[]{:S(2)}, u32[]{:S(2)}) collective-permute-start(f32[12,2,2048]{2,1,0:T(2,128)S(1)} %slice.592), channel_id=1, source_target_pairs={{0,8},{8,16},{16,24},{24,1},{32,40},{40,48},{48,56},{56,33},{64,72... | collective-permute-start | bytes 589832 | tf_op jit(solution)/shard_map/ppermute | solution.py:409
  51.3 9.1 %collective-permute-start.1 = (f32[12,3,2048]{2,1,0:T(4,128)S(1)}, f32[12,3,2048]{2,1,0:T(4,128)S(1)}, u32[]{:S(2)}, u32[]{:S(2)}) collective-permute-start(f32[12,3,2048]{2,1,0:T(4,128)S(1)} %slice.595), channel_id=1, source_target_pairs={{8,0},{16,8},{24,16},{1,24},{40,32},{48,40},{56,48},{33,56},{72,64... | collective-permute-start | bytes 884744 | tf_op jit(solution)/shard_map/ppermute | solution.py:410
  70.7 1.1 %copy-start = (f32[12,16,2048]{2,1,0:T(8,128)}, f32[12,16,2048]{2,1,0:T(8,128)S(1)}, u32[]{:S(2)}) copy-start(f32[12,16,2048]{2,1,0:T(8,128)S(1)} %constant_dynamic-update-slice_fusion.13.src_ref) | copy-start | bytes 4718596

commit v19 on v13

--- a/solution.py
+++ b/solution.py
@@ -410,9 +410,21 @@
     reach = cells // 4
     amount = shift + reach
     current = jnp.roll(field, -PAIR * reach, axis=2)
-    for position in range((2 * reach - 1).bit_length()):
-        moved = jnp.roll(current, PAIR * 2**position, axis=2)
-        current = jnp.where(bit_mask(amount, position), moved, current)
+    stages = (2 * reach - 1).bit_length()
+    position = 0
+    while position < stages:
+        step = PAIR * 2**position
+        if position + 1 < stages and step < 128:
+            one = jnp.roll(current, step, axis=2)
+            two = jnp.roll(current, 2 * step, axis=2)
+            three = jnp.roll(current, 3 * step, axis=2)
+            low, high = bit_mask(amount, position), bit_mask(amount, position + 1)
+            current = jnp.where(high, jnp.where(low, three, two), jnp.where(low, one, current))
+            position += 2
+        else:
+            moved = jnp.roll(current, step, axis=2)
+            current = jnp.where(bit_mask(amount, position), moved, current)
+            position += 1
     return current
 
 

time: 104 us -> 107 us (1.029)
  other arithmetic: 17.8 us -> 21.3 us
  waiting for transfers between devices: 6.37 us -> 3.1 us
  Pallas kernels: 62 us -> 63.9 us
  starting transfers between devices: 4.51 us -> 5.74 us
    select_n x0 -> x6, other arithmetic: none -> 8.82 us  [roll_rows(): jnp.where(high, jnp.where(low, three, two), jnp.where(low, one, current))]
    select_n x18 -> x6, other arithmetic: 7.32 us -> 1.46 us  [roll_rows(): current = jnp.where(bit_mask(amount, position), moved, current)]
    ppermute x1, waiting for transfers between devices: 6.36 us -> 0.82 us  [lat_halo(): above = lax.ppermute(field[:, :width], ('lon', 'lat'), down)]
    ppermute x1, waiting for transfers between devices: 0.01 us -> 2.28 us  [lat_halo(): below = lax.ppermute(field[:, rows - width + 1:], ('lon', 'lat'), up)]
    pallas_call x1, Pallas kernels: 28.4 us -> 30.3 us  [run_exchange(): pl.pallas_call(functools.partial(kernel, src_at=src_at, dst_at=dst_at), o...]
    ppermute x1, starting transfers between devices: 1.92 us -> 3.44 us  [lat_halo(): below = lax.ppermute(field[:, rows - width + 1:], ('lon', 'lat'), up)]
    slice x24 -> x30, local copies, waits for them, and re-layouts: 1.79 us -> 2.33 us  [the longest x12 0.77 us: roll_rows(): moved = jnp.roll(current, step, axis=2)]
  transfers between devices with their start and end apart: 2 -> 2, of which waited for: 1 -> 2; matrix products, arithmetic and copies ran while one was open for 0% -> 0% of each run, Pallas kernels for 0% -> 0%
where the time goes in v19:
time: 107 us
  Pallas kernels  63.9 us (60%)
  other arithmetic  21.3 us (20%)
  local copies, waits for them, and re-layouts  11.8 us (11%)
  starting transfers between devices  5.74 us (5%)
  waiting for transfers between devices  3.1 us (3%)
    pallas_call x1, Pallas kernels, to_columns(): pl.pallas_call(functools.partial(entry_kernel, src_at=src_at, dst_at=dst_...  33.6 us
    pallas_call x1, Pallas kernels, run_exchange(): pl.pallas_call(functools.partial(kernel, src_at=src_at, dst_at=dst_at), o...  30.3 us
    select_n x6, other arithmetic, roll_rows(): jnp.where(high, jnp.where(low, three, two), jnp.where(low, one, current))  8.82 us
    unnamed x30, local copies, waits for them, and re-layouts  6.1 us
    add x2, other arithmetic, lat_step(): summed = addend if summed is None else summed + addend  5.74 us
    ppermute x1, starting transfers between devices, lat_halo(): below = lax.ppermute(field[:, rows - width + 1:], ('lon', 'lat'), up)  3.44 us
    ppermute x1, starting transfers between devices, lat_halo(): above = lax.ppermute(field[:, :width], ('lon', 'lat'), down)  2.3 us
    slice x8, local copies, waits for them, and re-layouts, lon_cubic(): taps = [jnp.roll(shifted, PAIR * (1 - p), axis=2) for p in range(4)]  2.29 us
  transfers between devices with their start and end apart: 2, of which 2 were waited for; matrix products, arithmetic and copies ran while one was open for 0% of the time, Pallas kernels for 0%

profile of v19, /device:TPU:25, one launch (start us, length us, event | category | flops | bytes accessed | tf_op | source)
XLA Modules:
  0.0 106.7 jit_solution(813669915274921984)
XLA Ops:
  0.0 33.6 %shard_map.91 = (f32[12,16,2048]{2,1,0:T(8,128)}, f32[12,2,2048]{2,1,0:T(2,128)}, f32[12,3,2048]{2,1,0:T(4,128)}) custom-call(f32[12,64,512]{2,1,0:T(8,128)} %x_ref.1, bf16[512,512]{1,0:T(8,128)(2,1)} %constant.339.clone.matrix_ref), custom_call_target="tpu_custom_call" | custom-call | tf_op jit(solution)/shard_map/pallas_call | solution.py:345
  33.7 1.6 %constant_dynamic-update-slice_fusion.1 = f32[12,19,2048]{2,1,0:T(8,128)S(1)} fusion(f32[12,16,2048]{2,1,0:T(8,128)} %get-tuple-element.9), kind=kLoop, calls=%fused_computation.164 | loop fusion | bytes 3145728
  35.3 0.1 constant_dynamic-slice_fusion
  35.5 0.1 constant_dynamic-slice_fusion.1
  35.6 0.1 constant_dynamic-update-slice_fusion
  35.8 4.0 %fusion.19 = f32[12,16,2048]{2,1,0:T(8,128)S(1)} fusion(f32[12,2,2048]{2,1,0:T(2,128)S(1)} %copy-done.2, f32[12,16,2048]{2,1,0:T(8,128)} %get-tuple-element.9, f32[12,19,2048]{2,1,0:T(8,128)S(1)} %constant_dynamic-update-slice_fusion, f32[12,16]{1,0:T(8,128)S(1)} %get-tuple-element.84, f32[12,16]{1,0:T(8,128)S(1)} %get-tuple-element.83, ...), kind=kLoop, calls=%fused_computation.41 | loop fusion | flops 5111808 | bytes 8065536 | tf_op jit(solution)/shard_map/add | solution.py:52
  39.9 0.1 fusion.5
  40.0 0.1 fusion.4
  40.2 0.1 fusion.3
  40.4 0.1 slice.607
  40.5 0.1 slice.610
  40.6 1.5 %fusion.27 = f32[12,16,2048]{2,1,0:T(8,128)S(1)} fusion(f32[12,16,512]{2,1,0:T(8,128)S(1)} %slice.604, f32[12,16,1536]{2,1,0:T(8,128)S(1)} %slice.603, f32[12,16,2042]{2,1,0:T(8,128)S(1)} %fusion.3, f32[12,16,6]{2,1,0:T(8,128)S(1)} %slice.602, f32[12,16,2044]{2,1,0:T(8,128)S(1)} %fusion.4, f32[12,16,4]{2,1,0:T(8,128)S(1)} %slice.607, ...), kind=kLoop, calls=%fused_computation.49 | loop fusion | flops 2752512 | bytes 7864704 | tf_op jit(solution)/shard_map/jit(_where)/select_n | solution.py:422
  42.2 0.1 slice.615
  42.4 1.5 %fusion.31 = f32[12,16,2048]{2,1,0:T(8,128)S(1)} fusion(f32[12,16,2024]{2,1,0:T(8,128)S(1)} %bitcast.619, f32[12,16,24]{2,1,0:T(8,128)S(1)} %slice.613, f32[12,16,2032]{2,1,0:T(8,128)S(1)} %bitcast.620, f32[12,16,16]{2,1,0:T(8,128)S(1)} %slice.615, f32[12,16,2048]{2,1,0:T(8,128)S(1)} %fusion.27, f32[12,16,2040]{2,1,0:T(8,128)S(1)} %bitcast.621, ...), kind=kLoop, calls=%fused_computation.61 | loop fusion | flops 2359296 | bytes 7864704 | tf_op jit(solution)/shard_map/jit(_where)/select_n | solution.py:422
  44.1 0.1 slice.623
  44.2 1.4 %fusion.32 = f32[12,16,2048]{2,1,0:T(8,128)S(1)} fusion(f32[12,16,1952]{2,1,0:T(8,128)S(1)} %bitcast.625, f32[12,16,96]{2,1,0:T(8,128)S(1)} %slice.619, f32[12,16,1984]{2,1,0:T(8,128)S(1)} %bitcast.626, f32[12,16,64]{2,1,0:T(8,128)S(1)} %slice.621, f32[12,16,2048]{2,1,0:T(8,128)S(1)} %fusion.31, f32[12,16,2016]{2,1,0:T(8,128)S(1)} %bitcast.627, ...), kind=kLoop, calls=%fused_computation.64 | loop fusion | flops 2359296 | bytes 7864704 | tf_op jit(solution)/shard_map/jit(_where)/select_n | solution.py:422
  45.6 0.1 slice.626
  45.8 0.3 maximum_select_fusion.5
  46.1 0.1 slice.628
  46.2 0.2 maximum_select_fusion.6
  46.4 0.1 slice.630
  46.6 0.2 maximum_select_fusion.7
  46.8 0.6 fusion.220
  47.4 0.5 slice.635
  48.0 0.9 fusion.35
  49.0 0.1 slice.637
  49.1 0.6 copy-done.4
  49.6 0.1 constant_dynamic-slice_fusion.3
  50.0 0.3 fusion.36
  50.2 0.4 subtract_dynamic-update-slice_fusion.1
  51.1 0.1 constant_dynamic-update-slice_fusion.3
  51.2 0.1 constant_dynamic-update-slice_fusion.2
  51.3 2.3 %collective-permute-start.1 = (f32[12,3,2048]{2,1,0:T(4,128)S(1)}, f32[12,3,2048]{2,1,0:T(4,128)S(1)}, u32[]{:S(2)}, u32[]{:S(2)}) collective-permute-start(f32[12,3,2048]{2,1,0:T(4,128)S(1)} %slice.665), channel_id=1, source_target_pairs={{8,0},{16,8},{24,16},{1,24},{40,32},{48,40},{56,48},{33,56},{72,64... | collective-permute-start | bytes 884744 | tf_op jit(solution)/shard_map/ppermute | solution.py:404
  53.6 0.1 slice.662
  53.7 3.4 %collective-permute-start = (f32[12,2,2048]{2,1,0:T(2,128)S(1)}, f32[12,2,2048]{2,1,0:T(2,128)S(1)}, u32[]{:S(2)}, u32[]{:S(2)}) collective-permute-start(f32[12,2,2048]{2,1,0:T(2,128)S(1)} %slice.662), channel_id=1, source_target_pairs={{0,8},{8,16},{16,24},{24,1},{32,40},{40,48},{48,56},{56,33},{64,72... | collective-permute-start | bytes 589832 | tf_op jit(solution)/shard_map/ppermute | solution.py:403
  57.3 2.3 %collective-permute-done = f32[12,2,2048]{2,1,0:T(2,128)S(1)} collective-permute-done((f32[12,2,2048]{2,1,0:T(2,128)S(1)}, f32[12,2,2048]{2,1,0:T(2,128)S(1)}, u32[]{:S(2)}, u32[]{:S(2)}) %collective-permute-start) | collective-permute-done | bytes 196640 | tf_op jit(solution)/shard_map/ppermute | solution.py:403
  59.6 0.8 collective-permute-done.1
  60.4 1.7 %fusion.12 = f32[12,16,2048]{2,1,0:T(8,128)S(1)} fusion(f32[12,2,2048]{2,1,0:T(2,128)S(1)} %collective-permute-done, f32[12,16,2048]{2,1,0:T(8,128)S(1)} %constant_dynamic-update-slice_fusion.2, f32[12,3,2048]{2,1,0:T(4,128)S(1)} %collective-permute-done.1, f32[12,16]{1,0:T(8,128)S(1)} %get-tuple-element.74, f32[12,16]{1,0:T(8,128)S(1)} %get-tuple-element.73, ...), kind=kLoop, calls=%fused_computation.34 | loop fusion | flops 6291456 | bytes 3641856 | tf_op jit(solution)/shard_map/add | solution.py:52
  62.3 0.1 fusion.2
  62.4 0.1 fusion.1
  62.5 0.1 fusion
  62.7 0.1 slice.675
  62.8 0.1 slice.678
  62.9 1.5 %fusion.25 = f32[12,16,2048]{2,1,0:T(8,128)S(1)} fusion(f32[12,16,512]{2,1,0:T(8,128)S(1)} %slice.672, f32[12,16,1536]{2,1,0:T(8,128)S(1)} %slice.671, f32[12,16,2042]{2,1,0:T(8,128)S(1)} %fusion, f32[12,16,6]{2,1,0:T(8,128)S(1)} %slice.670, f32[12,16,2044]{2,1,0:T(8,128)S(1)} %fusion.1, f32[12,16,4]{2,1,0:T(8,128)S(1)} %slice.675, ...), kind=kLoop, calls=%fused_computation.47 | loop fusion | flops 2752512 | bytes 7864704 | tf_op jit(solution)/shard_map/jit(_where)/select_n | solution.py:422
  64.5 0.1 slice.683
  64.7 1.5 %fusion.37 = f32[12,16,2048]{2,1,0:T(8,128)S(1)} fusion(f32[12,16,2024]{2,1,0:T(8,128)S(1)} %bitcast.622, f32[12,16,24]{2,1,0:T(8,128)S(1)} %slice.681, f32[12,16,2032]{2,1,0:T(8,128)S(1)} %bitcast.623, f32[12,16,16]{2,1,0:T(8,128)S(1)} %slice.683, f32[12,16,2048]{2,1,0:T(8,128)S(1)} %fusion.25, f32[12,16,2040]{2,1,0:T(8,128)S(1)} %bitcast.624, ...), kind=kLoop, calls=%fused_computation.79 | loop fusion | flops 2359296 | bytes 7864704 | tf_op jit(solution)/shard_map/jit(_where)/select_n | solution.py:422
  66.5 1.4 %fusion.38 = f32[12,16,2048]{2,1,0:T(8,128)S(1)} fusion(f32[12,16,1952]{2,1,0:T(8,128)S(1)} %bitcast.628, f32[12,16,96]{2,1,0:T(8,128)S(1)} %slice.687, f32[12,16,1984]{2,1,0:T(8,128)S(1)} %bitcast.629, f32[12,16,64]{2,1,0:T(8,128)S(1)} %slice.689, f32[12,16,2048]{2,1,0:T(8,128)S(1)} %fusion.37, f32[12,16,2016]{2,1,0:T(8,128)S(1)} %bitcast.630, ...), kind=kLoop, calls=%fused_computation.82 | loop fusion | flops 2359296 | bytes 7864704 | tf_op jit(solution)/shard_map/jit(_where)/select_n | solution.py:422
  67.9 0.1 slice.694
  68.1 0.3 maximum_select_fusion.13
  68.4 0.1 slice.696
  68.5 0.2 maximum_select_fusion.14
  68.7 0.1 slice.698
  68.9 0.2 maximum_select_fusion.15
  69.1 0.6 fusion.218
  69.7 0.5 slice.703
  70.3 0.9 fusion.41
  71.2 0.1 slice.705
  71.3 0.3 fusion.42
  71.6 0.4 subtract_dynamic-update-slice_fusion
  72.4 0.1 constant_dynamic-update-slice_fusion.14
  72.5 0.1 constant_dynamic-update-slice_fusion.13.src_ref
  72.6 1.1 %copy-done = f32[12,16,2048]{2,1,0:T(8,128)} copy-done((f32[12,16,2048]{2,1,0:T(8,128)}, f32[12,16,2048]{2,1,0:T(8,128)S(1)}, u32[]{:S(2)}) %copy-start) | copy-done | bytes 1572888
  73.8 30.3 %shard_map.92 = f32[12,64,512]{2,1,0:T(8,128)} custom-call(f32[12,16,2048]{2,1,0:T(8,128)} %copy-done, bf16[512,512]{1,0:T(8,128)(2,1)} %constant.340.clone.matrix_ref), custom_call_target="tpu_custom_call" | custom-call | tf_op jit(solution)/shard_map/pallas_call | solution.py:311
  104.0 2.7 %copy.562 = f32[12,64,512]{2,1,0:T(8,128)} copy(f32[12,64,512]{2,1,0:T(8,128)} %shard_map.92) | data formatting | bytes 3145728
  (73 shorter events, 2.8 us)
Async XLA Ops:
  33.7 1.7 %copy-start.5 = (s32[2,12,64]{2,0,1:T(2,128)S(1)}, s32[2,12,64]{2,0,1:T(2,128)}, u32[]{:S(2)}) copy-start(s32[2,12,64]{2,0,1:T(2,128)} %param.10) | copy-start | bytes 18436
  33.7 1.6 %copy-start.6 = (s32[2,12,64]{2,0,1:T(2,128)S(1)}, s32[2,12,64]{2,0,1:T(2,128)}, u32[]{:S(2)}) copy-start(s32[2,12,64]{2,0,1:T(2,128)} %param.12) | copy-start | bytes 18436
  33.7 1.8 %copy-start.7 = (f32[2,12,64]{2,0,1:T(2,128)S(1)}, f32[2,12,64]{2,0,1:T(2,128)}, u32[]{:S(2)}) copy-start(f32[2,12,64]{2,0,1:T(2,128)} %param.13) | copy-start | bytes 18436
  33.7 1.8 %copy-start.8 = (f32[2,12,64]{2,0,1:T(2,128)S(1)}, f32[2,12,64]{2,0,1:T(2,128)}, u32[]{:S(2)}) copy-start(f32[2,12,64]{2,0,1:T(2,128)} %param.11) | copy-start | bytes 18436
  33.7 1.9 %copy-start.1 = (f32[12,3,2048]{2,1,0:T(4,128)S(1)}, f32[12,3,2048]{2,1,0:T(4,128)}, u32[]{:S(2)}) copy-start(f32[12,3,2048]{2,1,0:T(4,128)} %get-tuple-element.10) | copy-start | bytes 884740
  33.7 2.1 %copy-start.2 = (f32[12,2,2048]{2,1,0:T(2,128)S(1)}, f32[12,2,2048]{2,1,0:T(2,128)}, u32[]{:S(2)}) copy-start(f32[12,2,2048]{2,1,0:T(2,128)} %get-tuple-element.8) | copy-start | bytes 589828
  48.9 0.7 copy-start.4
  48.9 0.8 copy-start.3
  51.3 9.1 %collective-permute-start.1 = (f32[12,3,2048]{2,1,0:T(4,128)S(1)}, f32[12,3,2048]{2,1,0:T(4,128)S(1)}, u32[]{:S(2)}, u32[]{:S(2)}) collective-permute-start(f32[12,3,2048]{2,1,0:T(4,128)S(1)} %slice.665), channel_id=1, source_target_pairs={{8,0},{16,8},{24,16},{1,24},{40,32},{48,40},{56,48},{33,56},{72,64... | collective-permute-start | bytes 884744 | tf_op jit(solution)/shard_map/ppermute | solution.py:404
  53.7 5.9 %collective-permute-start = (f32[12,2,2048]{2,1,0:T(2,128)S(1)}, f32[12,2,2048]{2,1,0:T(2,128)S(1)}, u32[]{:S(2)}, u32[]{:S(2)}) collective-permute-start(f32[12,2,2048]{2,1,0:T(2,128)S(1)} %slice.662), channel_id=1, source_target_pairs={{0,8},{8,16},{16,24},{24,1},{32,40},{40,48},{48,56},{56,33},{64,72... | collective-permute-start | bytes 589832 | tf_op jit(solution)/shard_map/ppermute | solution.py:403
  72.6 1.1 %copy-start = (f32[12,16,2048]{2,1,0:T(8,128)}, f32[12,16,2048]{2,1,0:T(8,128)S(1)}, u32[]{:S(2)}) copy-start(f32[12,16,2048]{2,1,0:T(8,128)S(1)} %constant_dynamic-update-slice_fusion.13.src_ref) | copy-start | bytes 4718596

commit v20 on v19

--- a/solution.py
+++ b/solution.py
@@ -414,7 +414,7 @@
     position = 0
     while position < stages:
         step = PAIR * 2**position
-        if position + 1 < stages and step < 128:
+        if position + 1 < stages and step >= 128:
             one = jnp.roll(current, step, axis=2)
             two = jnp.roll(current, 2 * step, axis=2)
             three = jnp.roll(current, 3 * step, axis=2)

time: 107 us -> 104 us (0.972)
  other arithmetic: 21.3 us -> 17.8 us
  waiting for transfers between devices: 3.1 us -> 6.37 us
  Pallas kernels: 63.9 us -> 62 us
  starting transfers between devices: 5.74 us -> 4.51 us
    select_n x6 -> x2, other arithmetic: 8.82 us -> 0.69 us  [roll_rows(): jnp.where(high, jnp.where(low, three, two), jnp.where(low, one, current))]
    ppermute x1, waiting for transfers between devices: 0.82 us -> 6.36 us  [lat_halo(): above = lax.ppermute(field[:, :width], ('lon', 'lat'), down)]
    select_n x6 -> x14, other arithmetic: 1.46 us -> 6.61 us  [roll_rows(): current = jnp.where(bit_mask(amount, position), moved, current)]
    ppermute x1, waiting for transfers between devices: 2.28 us -> 0.01 us  [lat_halo(): below = lax.ppermute(field[:, rows - width + 1:], ('lon', 'lat'), up)]
    pallas_call x1, Pallas kernels: 30.3 us -> 28.4 us  [run_exchange(): pl.pallas_call(functools.partial(kernel, src_at=src_at, dst_at=dst_at), o...]
    ppermute x1, starting transfers between devices: 3.44 us -> 1.92 us  [lat_halo(): below = lax.ppermute(field[:, rows - width + 1:], ('lon', 'lat'), up)]
  transfers between devices with their start and end apart: 2 -> 2, of which waited for: 2 -> 1; matrix products, arithmetic and copies ran while one was open for 0% -> 0% of each run, Pallas kernels for 0% -> 0%
where the time goes in v20:
time: 104 us; the launch traced here: 103 us
  Pallas kernels  62 us (60%)
  other arithmetic  17.8 us (17%)
  local copies, waits for them, and re-layouts  11.4 us (11%)
  waiting for transfers between devices  6.37 us (6%)
  starting transfers between devices  4.51 us (4%)
    pallas_call x1, Pallas kernels, to_columns(): pl.pallas_call(functools.partial(entry_kernel, src_at=src_at, dst_at=dst_...  33.6 us
    pallas_call x1, Pallas kernels, run_exchange(): pl.pallas_call(functools.partial(kernel, src_at=src_at, dst_at=dst_at), o...  28.4 us
    select_n x14, other arithmetic, roll_rows(): current = jnp.where(bit_mask(amount, position), moved, current)  6.61 us
    ppermute x1, waiting for transfers between devices, lat_halo(): above = lax.ppermute(field[:, :width], ('lon', 'lat'), down)  6.36 us
    unnamed x30, local copies, waits for them, and re-layouts  6.09 us
    add x2, other arithmetic, lat_step(): summed = addend if summed is None else summed + addend  5.73 us
    ppermute x1, starting transfers between devices, lat_halo(): above = lax.ppermute(field[:, :width], ('lon', 'lat'), down)  2.59 us
    slice x8, local copies, waits for them, and re-layouts, lon_cubic(): taps = [jnp.roll(shifted, PAIR * (1 - p), axis=2) for p in range(4)]  2.29 us
  transfers between devices with their start and end apart: 2, of which 1 were waited for; matrix products, arithmetic and copies ran while one was open for 0% of the time, Pallas kernels for 0%

profile of v20, /device:TPU:25, one launch (start us, length us, event | category | flops | bytes accessed | tf_op | source)
XLA Modules:
  0.0 103.0 jit_solution(18100512560726585786)
XLA Ops:
  0.0 33.6 %shard_map.91 = (f32[12,16,2048]{2,1,0:T(8,128)}, f32[12,2,2048]{2,1,0:T(2,128)}, f32[12,3,2048]{2,1,0:T(4,128)}) custom-call(f32[12,64,512]{2,1,0:T(8,128)} %x_ref.1, bf16[512,512]{1,0:T(8,128)(2,1)} %constant.339.clone.matrix_ref), custom_call_target="tpu_custom_call" | custom-call | tf_op jit(solution)/shard_map/pallas_call | solution.py:345
  33.7 1.6 %constant_dynamic-update-slice_fusion.1 = f32[12,19,2048]{2,1,0:T(8,128)S(1)} fusion(f32[12,16,2048]{2,1,0:T(8,128)} %get-tuple-element.9), kind=kLoop, calls=%fused_computation.148 | loop fusion | bytes 3145728
  35.3 0.1 constant_dynamic-update-slice_fusion
  35.5 0.1 constant_dynamic-slice_fusion
  35.6 0.1 constant_dynamic-slice_fusion.1
  35.8 4.0 %fusion.17 = f32[12,16,2048]{2,1,0:T(8,128)S(1)} fusion(f32[12,2,2048]{2,1,0:T(2,128)S(1)} %copy-done.2, f32[12,16,2048]{2,1,0:T(8,128)} %get-tuple-element.9, f32[12,19,2048]{2,1,0:T(8,128)S(1)} %constant_dynamic-update-slice_fusion, f32[12,16]{1,0:T(8,128)S(1)} %get-tuple-element.84, f32[12,16]{1,0:T(8,128)S(1)} %get-tuple-element.83, ...), kind=kLoop, calls=%fused_computation.31 | loop fusion | flops 5111808 | bytes 8065536 | tf_op jit(solution)/shard_map/add | solution.py:52
  39.9 0.1 slice.558
  40.1 0.1 fusion.1
  40.2 0.5 fusion.3
  40.7 0.1 slice.563
  40.8 0.5 maximum_select_fusion
  41.4 0.5 maximum_select_fusion.1
  42.0 0.5 maximum_select_fusion.2
  42.5 0.1 slice.569
  42.6 0.5 maximum_select_fusion.3
  43.2 0.5 maximum_select_fusion.4
  43.7 0.1 slice.574
  43.8 0.1 slice.576
  44.0 0.1 slice.578
  44.1 0.3 fusion.25
  44.6 0.3 maximum_select_fusion.7
  44.9 0.6 fusion.212
  45.5 0.1 fusion.213
  45.6 0.5 slice.585
  46.1 0.9 fusion.28
  47.1 0.1 slice.587
  47.2 0.6 copy-done.4
  47.7 0.1 constant_dynamic-slice_fusion.3
  48.0 0.3 fusion.29
  48.3 0.4 subtract_dynamic-update-slice_fusion.1
  49.1 0.1 constant_dynamic-update-slice_fusion.3
  49.2 0.1 constant_dynamic-update-slice_fusion.2
  49.3 0.1 slice.612
  49.4 1.9 %collective-permute-start = (f32[12,2,2048]{2,1,0:T(2,128)S(1)}, f32[12,2,2048]{2,1,0:T(2,128)S(1)}, u32[]{:S(2)}, u32[]{:S(2)}) collective-permute-start(f32[12,2,2048]{2,1,0:T(2,128)S(1)} %slice.612), channel_id=1, source_target_pairs={{0,8},{8,16},{16,24},{24,1},{32,40},{40,48},{48,56},{56,33},{64,72... | collective-permute-start | bytes 589832 | tf_op jit(solution)/shard_map/ppermute | solution.py:403
  51.4 2.6 %collective-permute-start.1 = (f32[12,3,2048]{2,1,0:T(4,128)S(1)}, f32[12,3,2048]{2,1,0:T(4,128)S(1)}, u32[]{:S(2)}, u32[]{:S(2)}) collective-permute-start(f32[12,3,2048]{2,1,0:T(4,128)S(1)} %slice.615), channel_id=1, source_target_pairs={{8,0},{16,8},{24,16},{1,24},{40,32},{48,40},{56,48},{33,56},{72,64... | collective-permute-start | bytes 884744 | tf_op jit(solution)/shard_map/ppermute | solution.py:404
  54.2 6.4 %collective-permute-done.1 = f32[12,3,2048]{2,1,0:T(4,128)S(1)} collective-permute-done((f32[12,3,2048]{2,1,0:T(4,128)S(1)}, f32[12,3,2048]{2,1,0:T(4,128)S(1)}, u32[]{:S(2)}, u32[]{:S(2)}) %collective-permute-start.1) | collective-permute-done | bytes 294944 | tf_op jit(solution)/shard_map/ppermute | solution.py:404
  60.5 1.7 %fusion.10 = f32[12,16,2048]{2,1,0:T(8,128)S(1)} fusion(f32[12,2,2048]{2,1,0:T(2,128)S(1)} %collective-permute-done, f32[12,16,2048]{2,1,0:T(8,128)S(1)} %constant_dynamic-update-slice_fusion.2, f32[12,3,2048]{2,1,0:T(4,128)S(1)} %collective-permute-done.1, f32[12,16]{1,0:T(8,128)S(1)} %get-tuple-element.74, f32[12,16]{1,0:T(8,128)S(1)} %get-tuple-element.73, ...), kind=kLoop, calls=%fused_computation.24 | loop fusion | flops 6291456 | bytes 3641856 | tf_op jit(solution)/shard_map/add | solution.py:52
  62.5 0.1 fusion
  62.6 0.5 fusion.2
  63.1 0.1 slice.625
  63.2 0.5 maximum_select_fusion.8
  63.8 0.5 maximum_select_fusion.9
  64.3 0.1 slice.629
  64.4 0.5 maximum_select_fusion.10
  64.9 0.1 slice.631
  65.0 0.5 maximum_select_fusion.11
  65.6 0.5 maximum_select_fusion.12
  66.1 0.1 slice.636
  66.3 0.1 slice.638
  66.4 0.1 slice.640
  66.5 0.3 fusion.30
  67.0 0.3 maximum_select_fusion.15
  67.3 0.6 fusion.210
  67.9 0.1 fusion.211
  68.0 0.5 slice.647
  68.5 0.9 fusion.33
  69.4 0.1 slice.649
  69.5 0.3 fusion.34
  69.8 0.4 subtract_dynamic-update-slice_fusion
  70.6 0.1 constant_dynamic-update-slice_fusion.14
  70.7 0.1 constant_dynamic-update-slice_fusion.13.src_ref
  70.9 1.1 %copy-done = f32[12,16,2048]{2,1,0:T(8,128)} copy-done((f32[12,16,2048]{2,1,0:T(8,128)}, f32[12,16,2048]{2,1,0:T(8,128)S(1)}, u32[]{:S(2)}) %copy-start) | copy-done | bytes 1572888
  72.0 28.4 %shard_map.92 = f32[12,64,512]{2,1,0:T(8,128)} custom-call(f32[12,16,2048]{2,1,0:T(8,128)} %copy-done, bf16[512,512]{1,0:T(8,128)(2,1)} %constant.340.clone.matrix_ref), custom_call_target="tpu_custom_call" | custom-call | tf_op jit(solution)/shard_map/pallas_call | solution.py:311
  100.4 2.7 %copy.562 = f32[12,64,512]{2,1,0:T(8,128)} copy(f32[12,64,512]{2,1,0:T(8,128)} %shard_map.92) | data formatting | bytes 3145728
  (71 shorter events, 2.4 us)
Async XLA Ops:
  33.7 1.6 %copy-start.1 = (f32[12,3,2048]{2,1,0:T(4,128)S(1)}, f32[12,3,2048]{2,1,0:T(4,128)}, u32[]{:S(2)}) copy-start(f32[12,3,2048]{2,1,0:T(4,128)} %get-tuple-element.10) | copy-start | bytes 884740
  33.7 1.8 %copy-start.5 = (s32[2,12,64]{2,0,1:T(2,128)S(1)}, s32[2,12,64]{2,0,1:T(2,128)}, u32[]{:S(2)}) copy-start(s32[2,12,64]{2,0,1:T(2,128)} %param.10) | copy-start | bytes 18436
  33.7 1.8 %copy-start.6 = (s32[2,12,64]{2,0,1:T(2,128)S(1)}, s32[2,12,64]{2,0,1:T(2,128)}, u32[]{:S(2)}) copy-start(s32[2,12,64]{2,0,1:T(2,128)} %param.12) | copy-start | bytes 18436
  33.7 1.9 %copy-start.7 = (f32[2,12,64]{2,0,1:T(2,128)S(1)}, f32[2,12,64]{2,0,1:T(2,128)}, u32[]{:S(2)}) copy-start(f32[2,12,64]{2,0,1:T(2,128)} %param.13) | copy-start | bytes 18436
  33.7 1.9 %copy-start.8 = (f32[2,12,64]{2,0,1:T(2,128)S(1)}, f32[2,12,64]{2,0,1:T(2,128)}, u32[]{:S(2)}) copy-start(f32[2,12,64]{2,0,1:T(2,128)} %param.11) | copy-start | bytes 18436
  33.7 2.0 %copy-start.2 = (f32[12,2,2048]{2,1,0:T(2,128)S(1)}, f32[12,2,2048]{2,1,0:T(2,128)}, u32[]{:S(2)}) copy-start(f32[12,2,2048]{2,1,0:T(2,128)} %get-tuple-element.8) | copy-start | bytes 589828
  47.0 0.7 copy-start.4
  47.0 0.8 copy-start.3
  49.4 4.7 %collective-permute-start = (f32[12,2,2048]{2,1,0:T(2,128)S(1)}, f32[12,2,2048]{2,1,0:T(2,128)S(1)}, u32[]{:S(2)}, u32[]{:S(2)}) collective-permute-start(f32[12,2,2048]{2,1,0:T(2,128)S(1)} %slice.612), channel_id=1, source_target_pairs={{0,8},{8,16},{16,24},{24,1},{32,40},{40,48},{48,56},{56,33},{64,72... | collective-permute-start | bytes 589832 | tf_op jit(solution)/shard_map/ppermute | solution.py:403
  51.4 9.1 %collective-permute-start.1 = (f32[12,3,2048]{2,1,0:T(4,128)S(1)}, f32[12,3,2048]{2,1,0:T(4,128)S(1)}, u32[]{:S(2)}, u32[]{:S(2)}) collective-permute-start(f32[12,3,2048]{2,1,0:T(4,128)S(1)} %slice.615), channel_id=1, source_target_pairs={{8,0},{16,8},{24,16},{1,24},{40,32},{48,40},{56,48},{33,56},{72,64... | collective-permute-start | bytes 884744 | tf_op jit(solution)/shard_map/ppermute | solution.py:404
  70.8 1.1 %copy-start = (f32[12,16,2048]{2,1,0:T(8,128)}, f32[12,16,2048]{2,1,0:T(8,128)S(1)}, u32[]{:S(2)}) copy-start(f32[12,16,2048]{2,1,0:T(8,128)S(1)} %constant_dynamic-update-slice_fusion.13.src_ref) | copy-start | bytes 4718596
